TPU v7x, 512 devices: a whole 4x8x8 slice. The times are simulated.
512 devices in a mesh: px: 32 (over y, z_hi, core), py: 16 (over x, z_lo).
Axes of the slice: x: 4, y: 8, z: 8 (z_hi: 2, z_lo: 4; z = z_hi * 4 + z_lo), core: 2. Of those that a mesh axis runs over, the one named last changes fastest.
Arguments:
- density: float32 [512, 512, 256], P('px', 'py'), may hold values from -6 to 6
- external: float32 [512, 512, 256], P('px', 'py'), may hold values from -6 to 6
- orbitals: float32 [1024, 8, 24, 576], P(('px', 'py')), may hold values from -6 to 6
- anchors: int32 [1024, 3], P(('px', 'py')), may hold values from 0 to 511, as said below
- weights: int32 [1024], P(('px', 'py')), may hold values from -1 to 1, as said below
- degrees: int32 [1024], P(('px', 'py')), may hold values from 4 to 24
Outputs:
- hartree_field: float32 [512, 512, 256], P('px', 'py')
- filtered: float32 [1024, 8, 24, 576], P(('px', 'py'))
- new_density: float32 [512, 512, 256], P('px', 'py')
Inputs may be any that keep to these rules, and one draw needn't show every extreme that they name: `anchors`: fragment f lies on device f // 2 of the joined px, py axes; its anchor's first two coordinates lie in that device's block of the grid, its third coordinate is at most 232. `weights`: each weight is -1 or +1.
All inputs are finite; a program needn't handle non-finite values.
Results may differ from a plain program's by a relative error of at most 0.0003.
Values sent between devices are 32-bit elements; how exact they have to be, the bound alone decides.
No kernel may reach another device: no remote copies, remote signals or barrier semaphores. Data moves between devices by JAX's collectives and lax.ppermute only.
A program may use at most 64 MiB of HBM per device.

v0:
```python
import jax
import jax.numpy as jnp
import numpy as np
from jax import lax
from jax.experimental import pallas as pl
from jax.experimental.pallas import tpu as pltpu
from jax.sharding import Mesh
from jax.sharding import PartitionSpec as P

NX, NY, NZ = 512, 512, 256
NPX, NPY = 32, 16
ROWS, COLS = NX // NPX, NY // NPY
KZ = NZ // NPY
FRAG, NORB = 24, 8
PX = ("px_0", "px_1", "px_2")
ALL = PX + ("py",)
SCREENING, WINDOW_GAP, KINETIC_TOP = 0.002, 0.1, 6.0
STEPS = ((0, 0), (0, 1), (1, 0), (1, 1), (2, 0), (2, 1))
PADDED = COLS + 32 + FRAG
F32 = jnp.float32
BF16 = jnp.bfloat16
VMEM = pl.BlockSpec(memory_space=pltpu.VMEM)
SMEM = pl.BlockSpec(memory_space=pltpu.SMEM)


def sine_table(length):
    index = np.arange(1, length + 1, dtype=np.int64)
    product = index[:, None] * index[None, :] % (2 * length + 2)
    return np.sin(product * (np.pi / (length + 1))) * np.sqrt(2.0 / (length + 1))


def halves_of(table):
    high = np.asarray(table, np.float32).astype(BF16)
    low = (table - high.astype(np.float64)).astype(np.float32).astype(BF16)
    return high, low


def eigen_values(length):
    wave = np.arange(1, length + 1, dtype=np.float64) * (np.pi / (length + 1))
    return (4.0 * np.sin(wave / 2.0) ** 2).astype(np.float32)


SINE_Y = halves_of(sine_table(NY))
SINE_Z = halves_of(sine_table(NZ))
EIGEN_Y = eigen_values(NY)[None, :]
EIGEN_Z = eigen_values(NZ)[:, None]


def split2(x):
    high = x.astype(BF16)
    return high, (x - high.astype(F32)).astype(BF16)


def dot3(left, right, dims):
    def one(a, b):
        return lax.dot_general(a, b, (dims, ((), ())), preferred_element_type=F32)

    return one(left[0], right[0]) + (one(left[0], right[1]) + one(left[1], right[0]))


def call(kernel, outs, scratch=(), smem=(), count=1):
    return pl.pallas_call(
        kernel,
        out_shape=outs,
        in_specs=[SMEM if k in smem else VMEM for k in range(count)],
        out_specs=jax.tree.map(lambda _: VMEM, outs),
        scratch_shapes=list(scratch),
        compiler_params=pltpu.CompilerParams(vmem_limit_bytes=48 * 1024 * 1024),
    )


def shape(*dims):
    return jax.ShapeDtypeStruct(dims, F32)


def lanes(rows):
    return lax.broadcasted_iota(jnp.int32, (rows, 128), 1)


def rolled(x, by, axis=1):
    by %= x.shape[axis]
    return pltpu.roll(x, by, axis) if by else x


def decay(ey, ez):
    gap = ey + ez + SCREENING
    root = jnp.sqrt(gap + 0.25 * gap * gap)
    return 1.0 / (1.0 + 0.5 * gap + root), 0.5 / root


def forward_z(density, table_high, table_low, out):
    cells = density[...].reshape(ROWS * COLS, NZ)
    spectrum = dot3((table_high[...], table_low[...]), split2(cells), ((1,), (1,)))
    out[...] = spectrum.reshape(NPY, KZ, ROWS * COLS)


def scan_powers(place, ey, ez, power_out, weight_out, ends_out):
    rate, _ = decay(ey[...], ez[...])
    power = rate
    for _ in range(4):
        power = power * power
    before = jnp.ones((KZ, NY), F32)
    after = before
    for bit in range(5):
        upper = (place[0] >> bit) % 2 == 1
        power_out[bit] = power
        weight_out[bit] = jnp.where(upper, before, after)
        before, after = jnp.where(upper, before * power, before), jnp.where(upper, after, after * power)
        power = power * power
    ends_out[0] = before
    ends_out[1] = after


def forward_y(tiles, table_high, table_low, ey, ez, field_out, moment_out, merged):
    block = lanes(KZ) // COLS
    for row in range(ROWS):
        for tile in range(4):
            total = None
            for k in range(4):
                piece = tiles[4 * tile + k, :, row // 4 * 128 : row // 4 * 128 + 128]
                piece = rolled(piece, (k - row % 4) * COLS)
                total = piece if total is None else jnp.where(block == k, piece, total)
            merged[row * KZ : (row + 1) * KZ, tile * 128 : (tile + 1) * 128] = total
    field = dot3(split2(merged[...]), (table_high[...], table_low[...]), ((1,), (0,)))
    field_out[...] = field
    rate, _ = decay(ey[...], ez[...])
    first = field[:KZ]
    last = field[(ROWS - 1) * KZ :]
    for row in range(1, ROWS):
        first = field[row * KZ : (row + 1) * KZ] + rate * first
        back = ROWS - 1 - row
        last = field[back * KZ : (back + 1) * KZ] + rate * last
    moment_out[:KZ] = first
    moment_out[KZ:] = last


def back_y(field, totals, states, ends, table_high, table_low, ey, ez, tiles_out, solved):
    rate, scale = decay(ey[...], ez[...])
    across = rate
    for _ in range(9):
        across = across * across
    across = across * rate
    norm = rate / (1.0 - across * across)
    right_total, left_total = totals[:KZ], totals[KZ:]
    state = states[:KZ] - norm * (left_total - across * right_total) * ends[0]
    left = states[KZ:] - norm * (right_total - across * left_total) * ends[1]
    for row in range(ROWS):
        state = field[row * KZ : (row + 1) * KZ] + rate * state
        solved[row * KZ : (row + 1) * KZ] = state
    for row in range(ROWS - 1, -1, -1):
        here = pl.ds(row * KZ, KZ)
        solved[here] = scale * (solved[here] + rate * left)
        left = field[here] + rate * left
    columns = dot3(split2(solved[...]), (table_high[...], table_low[...]), ((1,), (0,)))
    solved[...] = columns
    block = lanes(KZ) // COLS
    for peer in range(NPY):
        for tile in range(4):
            total = None
            for k in range(4):
                row = 4 * tile + k
                piece = solved[row * KZ : (row + 1) * KZ, peer // 4 * 128 : peer // 4 * 128 + 128]
                piece = rolled(piece, (k - peer % 4) * COLS)
                total = piece if total is None else jnp.where(block == k, piece, total)
            tiles_out[peer, :, tile * 128 : (tile + 1) * 128] = total


def slots_of(rows):
    return lanes(rows) // 32


def back_z(places, tiles, external, table_high, table_low, field_out, *rest):
    pieces, grid = rest[:6], rest[6]
    spectrum = tiles[...].reshape(NZ, ROWS * COLS)
    turned = spectrum.T
    field = dot3(split2(turned), (table_high[...], table_low[...]), ((1,), (0,)))
    field = field.reshape(ROWS, COLS, NZ)
    field_out[...] = field
    potential = field + external[...]
    for half in range(2):
        grid[half, :, :32] = jnp.zeros((ROWS, 32, 128), F32)
        grid[half, :, 32 + COLS :] = jnp.zeros((ROWS, FRAG, 128), F32)
        grid[half, :, 32 : 32 + COLS] = potential[:, :, half * 128 : half * 128 + 128]
    lane = lanes(FRAG)
    slot_of = slots_of(FRAG)
    for k, (down, along) in enumerate(STEPS):
        groups = 8 if down < 2 else 4

        def cut(group, carry, k=k, along=along, groups=groups):
            total = None
            for slot in range(4):
                frag = slot % 2
                row = group + groups * (slot // 2)
                col, depth = places[6 * k + 3 * frag + 1], places[6 * k + 3 * frag + 2]
                cols = pl.ds(32 + col - 32 * along, FRAG)
                window = jnp.where(lane >= depth, grid[0, row, cols, :], grid[1, row, cols, :])
                window = pltpu.roll(window, (256 + 32 * slot - depth) & 127, 1)
                total = window if total is None else jnp.where(slot_of == slot, window, total)
            pieces[k][group] = total
            return carry

        lax.fori_loop(0, groups, cut, 0)


def orbitals_in(orbitals, out, strips, turned):
    for frag in range(2):
        for tile in range(5):
            width = min(128, FRAG * FRAG - tile * 128)
            strips[frag, tile, :, :width] = orbitals[frag, :, tile * 128 : tile * 128 + width]
    lane = lanes(8)

    def plane(x, carry):
        rows = []
        for yc in range(8):
            tile, off = divmod(72 * yc, 128)
            for frag in range(2):
                piece = rolled(strips[frag, tile, pl.ds(x, 8, stride=FRAG), :], -off)
                if off + 72 > 128:
                    other = rolled(strips[frag, tile + 1, pl.ds(x, 8, stride=FRAG), :], -off)
                    piece = jnp.where(lane < 128 - off, piece, other)
                rows.append(piece)
        turned[...] = jnp.concatenate(rows, 0).T
        for k in range(9):
            out[x, k] = turned[pl.ds(k // 3 * FRAG + k % 3, 8, stride=3), :]
        return carry

    lax.fori_loop(0, FRAG, plane, 0)


def orbitals_out(planes, scale, out, strips, turned):
    lane = lanes(8)
    factor = scale[...]

    def plane(x, carry):
        for k in range(9):
            turned[pl.ds(k // 3 * FRAG + k % 3, 8, stride=3), :] = planes[x, k] * factor
        rows = turned[...].T
        for frag in range(2):
            for tile in range(5):
                total = None
                for yc in range(8):
                    start = 72 * yc - 128 * tile
                    if -72 < start < 128:
                        piece = rows[(2 * yc + frag) * 8 : (2 * yc + frag) * 8 + 8]
                        piece = rolled(piece, start)
                        if total is None:
                            total = piece
                        else:
                            total = jnp.where(lane >= start, piece, total)
                strips[frag, tile, pl.ds(x, 8, stride=FRAG), :] = total
        return carry

    lax.fori_loop(0, FRAG, plane, 0)
    for frag in range(2):
        for tile in range(5):
            width = min(128, FRAG * FRAG - tile * 128)
            out[frag, :, tile * 128 : tile * 128 + width] = strips[frag, tile, :, :width]


def spread(value, lane):
    values = [value]
    for step in (4, 2, 1):
        clear = lane & step == 0
        values = [
            part
            for v in values
            for part in (
                jnp.where(clear, v, rolled(v, step)),
                jnp.where(clear, rolled(v, -step), v),
            )
        ]
    return values


def gather_sums(values, lane):
    for step in (4, 2, 1):
        clear = lane & step == 0
        count = len(values) // 2
        values = [
            jnp.where(
                clear,
                values[k] + rolled(values[k], -step),
                values[k + count] + rolled(values[k + count], step),
            )
            for k in range(count)
        ]
    return values[0]


def total_of(x):
    return jnp.sum(jnp.sum(x, axis=0, keepdims=True), axis=1, keepdims=True)


def filter_fragments(meta, *refs):
    pieces, start = refs[:6], refs[6]
    out, scale_out = refs[7:9]
    shares = refs[9:12]
    boxes, turned, compact, potential, other, spilled = refs[12:]
    lane = lanes(8)
    sub = lax.broadcasted_iota(jnp.int32, (8, 128), 0)
    second = (lane // 8) % 2 == 1
    for down in range(3):
        groups = 8 if down < 2 else 4

        def unpack(group, carry, down=down, groups=groups):
            both = pieces[2 * down][group] + pieces[2 * down + 1][group]
            for slot in range(4):
                row = 16 * down + group + groups * (slot // 2)
                boxes[slot % 2, pl.ds(pl.multiple_of(row * FRAG, 8), FRAG), :] = rolled(both, -32 * slot)
            return carry

        lax.fori_loop(0, groups, unpack, 0)
    lowest = None
    for part in range(3):
        rows = []
        for yc in range(8):
            for frag in range(2):
                base = (meta[frag] + 8 * part) * FRAG + 3 * yc
                took = [boxes[frag, pl.ds(base + yi, 8, stride=FRAG), :] for yi in range(3)]
                rows.append(
                    jnp.where(
                        lane < FRAG,
                        took[0],
                        jnp.where(lane < 2 * FRAG, rolled(took[1], FRAG), rolled(took[2], 2 * FRAG)),
                    )
                )
        turned[...] = jnp.concatenate(rows, 0).T
        for k in range(9):
            value = turned[pl.ds(k // 3 * FRAG + k % 3, 8, stride=3), :]
            compact[9 * part + k] = value
            lowest = value if lowest is None else jnp.minimum(lowest, value)
            highest = value if part + k == 0 else jnp.maximum(highest, value)

    def window(keep):
        low = jnp.where(keep, lowest, jnp.inf)
        high = jnp.where(keep, highest, -jnp.inf)
        low = jnp.min(jnp.min(low, axis=0, keepdims=True), axis=1, keepdims=True) + WINDOW_GAP
        high = jnp.max(jnp.max(high, axis=0, keepdims=True), axis=1, keepdims=True) + KINETIC_TOP
        return 0.5 * (high + low), 0.5 * (high - low)

    centre_0, half_0 = window(~second)
    centre_1, half_1 = window(second)
    centre = jnp.where(second, centre_1, centre_0)
    inverse = 1.0 / jnp.where(second, half_1, half_0)
    for part in range(3):
        for k in range(9):
            value = (3.0 + compact[9 * part + k] - centre) * (2.0 * inverse)
            for x, wide in enumerate(spread(value, lane)):
                potential[8 * part + x, k] = wide
    coupling = -inverse
    degree = jnp.where(second, meta[5], meta[4])

    def apply(source, target, initial=False, step=None):
        live = None if step is None else step <= degree

        def chunk(number, carry):
            behind, here = list(carry[:9]), list(carry[9:])
            for k4 in range(4):
                x = 4 * number + k4
                ahead_x = jnp.minimum(x + 1, FRAG - 1)
                ahead = [source[ahead_x, k] for k in range(9)]
                if k4 == 3:
                    ahead = [jnp.where(x + 1 < FRAG, v, 0.0) for v in ahead]
                for k in range(9):
                    yi, zi = divmod(k, 3)
                    total = behind[k] + ahead[k]
                    if yi > 0:
                        total = total + here[k - 3]
                    else:
                        total = total + jnp.where(lane >= 16, rolled(here[6 + zi], 16), 0.0)
                    if yi < 2:
                        total = total + here[k + 3]
                    else:
                        total = total + jnp.where(lane < 112, rolled(here[zi], -16), 0.0)
                    if zi > 0:
                        total = total + here[k - 1]
                    else:
                        total = total + jnp.where(sub >= 1, rolled(here[k + 2], 1, 0), 0.0)
                    if zi < 2:
                        total = total + here[k + 1]
                    else:
                        total = total + jnp.where(sub < 7, rolled(here[k - 2], -1, 0), 0.0)
                    image = potential[x, k] * here[k] + coupling * total
                    following = 0.5 * image if initial else image - target[x, k]
                    if live is not None:
                        following = jnp.where(live, following, here[k])
                    target[x, k] = following
                behind, here = here, ahead
            return tuple(behind + here)

        zero = [jnp.zeros((8, 128), F32)] * 9
        lax.fori_loop(0, 6, chunk, tuple(zero + [source[0, k] for k in range(9)]))

    def copy(x, carry):
        out[x] = start[x]
        return carry

    lax.fori_loop(0, FRAG, copy, 0)
    apply(out, other, initial=True)
    fewest = jnp.minimum(meta[4], meta[5])
    most = jnp.maximum(meta[4], meta[5])
    plain = (fewest - 1) // 2
    pairs = most // 2

    def free_pair(pair, carry):
        apply(other, out)
        apply(out, other)
        return carry

    def held_pair(pair, carry):
        apply(other, out, step=2 * pair + 2)
        apply(out, other, step=2 * pair + 3)
        return carry

    lax.fori_loop(0, plain, free_pair, 0)
    lax.fori_loop(plain, pairs, held_pair, 0)

    def squares(x, sums):
        for k in range(9):
            value = other[x, k]
            sums = sums + value * value
            out[x, k] = value
        return sums

    sums = lax.fori_loop(0, FRAG, squares, jnp.zeros((8, 128), F32))
    sums = jnp.sum(sums, axis=0, keepdims=True)
    sums = jnp.broadcast_to(sums, (8, 128))
    for step in (16, 32, 64):
        sums = sums + rolled(sums, step)
    scale = jnp.sqrt(float(FRAG**3) / (sums + 1e-06))
    scale_out[...] = scale
    weight = jnp.where(second, meta[3], meta[2]).astype(F32) / NORB

    def clear(row, carry):
        for frag in range(2):
            spilled[frag, pl.ds(pl.multiple_of(row * FRAG, 8), FRAG), :] = jnp.zeros((FRAG, 128), F32)
        return carry

    lax.fori_loop(0, 40, clear, 0)
    for part in range(3):
        for k in range(9):
            values = []
            for x in range(8):
                value = other[8 * part + x, k] * scale
                values.append(value * value)
            turned[pl.ds(k // 3 * FRAG + k % 3, 8, stride=3), :] = gather_sums(values, lane) * weight
        rows = turned[...].T
        for yc in range(8):
            for frag in range(2):
                piece = rows[(2 * yc + frag) * 8 : (2 * yc + frag) * 8 + 8]
                base = (meta[frag] + 8 * part) * FRAG + 3 * yc
                for yi in range(3):
                    spilled[frag, pl.ds(base + yi, 8, stride=FRAG), :] = rolled(piece, -FRAG * yi)
    slot_of = slots_of(FRAG)
    for down in range(3):
        groups = 8 if down < 2 else 4

        def share(group, carry, down=down, groups=groups):
            total = None
            for slot in range(4):
                row = 16 * down + group + groups * (slot // 2)
                piece = spilled[slot % 2, pl.ds(pl.multiple_of(row * FRAG, 8), FRAG), :]
                piece = rolled(piece, 32 * slot)
                total = piece if total is None else jnp.where(slot_of == slot, piece, total)
            shares[down][group] = total
            return carry

        lax.fori_loop(0, groups, share, 0)


def patch(places, *refs):
    shares, out, grid = refs[:6], refs[6], refs[7]

    def clear(row, carry):
        for half in range(2):
            grid[half, row] = jnp.zeros((PADDED, 128), F32)
        return carry

    lax.fori_loop(0, ROWS, clear, 0)
    lane = lanes(FRAG)
    for k, (down, along) in enumerate(STEPS):
        groups = 8 if down < 2 else 4

        def add(group, carry, k=k, along=along, groups=groups):
            both = shares[k][group]
            for slot in range(4):
                frag = slot % 2
                row = group + groups * (slot // 2)
                col, depth = places[6 * k + 3 * frag + 1], places[6 * k + 3 * frag + 2]
                piece = pltpu.roll(both, (256 + depth - 32 * slot) & 127, 1)
                piece = jnp.where(((lane - depth) & 127) < FRAG, piece, 0.0)
                cols = pl.ds(32 + col - 32 * along, FRAG)
                grid[0, row, cols, :] += jnp.where(lane >= depth, piece, 0.0)
                grid[1, row, cols, :] += jnp.where(lane >= depth, 0.0, piece)
            return carry

        lax.fori_loop(0, groups, add, 0)
    for half in range(2):
        out[:, :, half * 128 : half * 128 + 128] = grid[half, :, 32 : 32 + COLS]


def moved(x, down, along):
    pairs = [
        (p * NPY + q, (p + down) * NPY + q + along)
        for p in range(NPX)
        for q in range(NPY)
        if 0 <= p + down < NPX and 0 <= q + along < NPY
    ]
    return lax.ppermute(x, ALL, pairs)


def body(density, external, orbitals, anchors, weights, degrees):
    row_place = lax.axis_index(PX)
    col_place = lax.axis_index("py")
    origin = jnp.stack([row_place * ROWS, col_place * COLS, 0])
    local = (anchors - origin[None, :]).astype(jnp.int32)
    own = jnp.pad(local.reshape(6), (0, 2))
    above = jnp.stack([own, moved(own, 1, 0), moved(own, 2, 0)])
    places = jnp.stack([above, moved(above, 0, 1)], 1)[:, :, :6].reshape(36)
    meta = jnp.concatenate([local[:, 0], weights, degrees, weights]).astype(jnp.int32)

    sine_y = [jnp.asarray(t) for t in SINE_Y]
    sine_z = [jnp.asarray(t) for t in SINE_Z]
    ey = jnp.asarray(EIGEN_Y)
    ez = lax.dynamic_slice(jnp.asarray(EIGEN_Z), (col_place * KZ, 0), (KZ, 1))

    planes = call(
        orbitals_in,
        shape(FRAG, 9, 8, 128),
        [pltpu.VMEM((2, 5, NORB * FRAG, 128), F32), pltpu.VMEM((128, 128), F32)],
    )(orbitals.reshape(2, NORB * FRAG, FRAG * FRAG))
    power, weight, ends = call(
        scan_powers,
        (shape(5, KZ, NY), shape(5, KZ, NY), shape(2, KZ, NY)),
        smem=(0,),
        count=3,
    )(row_place.reshape(1).astype(jnp.int32), ey, ez)

    tiles = call(forward_z, shape(NPY, KZ, ROWS * COLS), count=3)(density, *sine_z)
    tiles = lax.all_to_all(tiles, "py", split_axis=0, concat_axis=0, tiled=True)
    field, totals = call(
        forward_y,
        (shape(ROWS * KZ, NY), shape(2 * KZ, NY)),
        [pltpu.VMEM((ROWS * KZ, NY), F32)],
        count=5,
    )(tiles, *sine_y, ey, ez)

    right, left = jnp.zeros((KZ, NY), F32), jnp.zeros((KZ, NY), F32)
    for bit in range(5):
        pairs = [(p * NPY + q, (p ^ (1 << bit)) * NPY + q) for p in range(NPX) for q in range(NPY)]
        got = lax.ppermute(totals, ALL, pairs)
        upper = (row_place >> bit) % 2 == 1
        high, low = jnp.where(upper, totals, got), jnp.where(upper, got, totals)
        right = right + jnp.where(upper, weight[bit] * got[:KZ], 0.0)
        left = left + jnp.where(upper, 0.0, weight[bit] * got[KZ:])
        totals = jnp.concatenate([high[:KZ] + power[bit] * low[:KZ], low[KZ:] + power[bit] * high[KZ:]])
    states = jnp.concatenate([right, left])

    tiles = call(back_y, shape(NPY, KZ, ROWS * COLS), [pltpu.VMEM((ROWS * KZ, NY), F32)], count=8)(
        field, totals, states, ends, *sine_y, ey, ez
    )
    tiles = lax.all_to_all(tiles, "py", split_axis=0, concat_axis=0, tiled=True)
    hartree_field, *pieces = call(
        back_z,
        [shape(ROWS, COLS, NZ)] + [shape(8 if down < 2 else 4, FRAG, 128) for down, _ in STEPS],
        [pltpu.VMEM((2, ROWS, PADDED, 128), F32)],
        smem=(0,),
        count=5,
    )(places, tiles, external, *sine_z)
    pieces = [pieces[k] if k == 0 else moved(pieces[k], -STEPS[k][0], -STEPS[k][1]) for k in range(6)]
    planes, scale, *shares = call(
        filter_fragments,
        [shape(FRAG, 9, 8, 128), shape(8, 128)] + [shape(n, FRAG, 128) for n in (8, 8, 4)],
        [
            pltpu.VMEM((2, 40 * FRAG, 128), F32),
            pltpu.VMEM((128, 128), F32),
            pltpu.VMEM((27, 8, 128), F32),
            pltpu.VMEM((FRAG, 9, 8, 128), F32),
            pltpu.VMEM((FRAG, 9, 8, 128), F32),
            pltpu.VMEM((2, 40 * FRAG, 128), F32),
        ],
        smem=(0,),
        count=8,
    )(meta, *pieces, planes)
    received = [
        shares[down] if k == 0 else moved(shares[down], down, along)
        for k, (down, along) in enumerate(STEPS)
    ]
    filtered = call(
        orbitals_out,
        shape(2, NORB * FRAG, FRAG * FRAG),
        [pltpu.VMEM((2, 5, NORB * FRAG, 128), F32), pltpu.VMEM((128, 128), F32)],
        count=2,
    )(planes, scale)
    new_density = call(
        patch,
        shape(ROWS, COLS, NZ),
        [pltpu.VMEM((2, ROWS, PADDED, 128), F32)],
        smem=(0,),
        count=7,
    )(places, *received)
    return hartree_field, filtered.reshape(orbitals.shape), new_density


def solution(mesh):
    torus = Mesh(mesh.devices.reshape(8, 2, 2, NPY), ALL)
    grid = P(PX, "py", None)
    return jax.shard_map(
        body,
        mesh=torus,
        in_specs=(grid, grid, P(ALL, None, None, None), P(ALL, None), P(ALL), P(ALL)),
        out_specs=(grid, P(ALL, None, None, None), grid),
        check_vma=False,
    )
```

profile of v0, /device:TPU:39, one launch (start us, length us, event | category | flops | bytes accessed | tf_op | source)
XLA Modules:
  0.0 189.0 jit_solution(4170314812721648164)
XLA Ops:
  0.6 0.0 copy-start.4
  0.6 0.9 copy-done.4
  1.5 0.9 copy-done.6
  2.4 1.0 copy-done.8
  3.5 1.2 shard_map.139
  4.7 9.8 %all-to-all-start = ((f32[16,16,512]{2,1,0:T(8,128)}), f32[16,16,512]{2,1,0:T(8,128)S(1)}, u32[]{:S(2)}, u32[]{:S(2)}) async-start(f32[16,16,512]{2,1,0:T(8,128)} %shard_map.139), calls=%async_computation | async-start | bytes 1048576 | tf_op jit(solution)/shard_map/all_to_all | solution.py:540
  14.5 0.7 constant_dynamic-slice_fusion.ez
  15.2 13.0 %all-to-all-done.tiles = f32[16,16,512]{2,1,0:T(8,128)S(1)} async-done(((f32[16,16,512]{2,1,0:T(8,128)}), f32[16,16,512]{2,1,0:T(8,128)S(1)}, u32[]{:S(2)}, u32[]{:S(2)}) %all-to-all-start) | async-done | bytes 524320 | tf_op jit(solution)/shard_map/all_to_all | solution.py:540
  28.3 0.9 shard_map.140
  29.2 3.6 %collective-permute-start.3 = (f32[32,512]{1,0:T(8,128)S(1)}, f32[32,512]{1,0:T(8,128)S(1)}, u32[]{:S(2)}, u32[]{:S(2)}) collective-permute-start(f32[32,512]{1,0:T(8,128)S(1)} %get-tuple-element.21), channel_id=1, source_target_pairs={{0,16},{1,17},{2,18},{3,19},{4,20},{5,21},{6,22},{7,23},{8,24},{9,... | collective-permute-start | bytes 196616 | tf_op jit(solution)/shard_map/ppermute | solution.py:551
  32.8 0.1 shard_map.141
  32.9 0.7 collective-permute-done.3
  33.7 7.9 %collective-permute-start.4 = (f32[32,512]{1,0:T(8,128)S(1)}, f32[32,512]{1,0:T(8,128)S(1)}, u32[]{:S(2)}, u32[]{:S(2)}) collective-permute-start(f32[32,512]{1,0:T(8,128)S(1)} %pad_maximum_fusion), channel_id=1, source_target_pairs={{0,32},{1,33},{2,34},{3,35},{4,36},{5,37},{6,38},{7,39},{8,40},{9,... | collective-permute-start | bytes 196616 | tf_op jit(solution)/shard_map/ppermute | solution.py:551
  41.7 2.1 %collective-permute-done.4 = f32[32,512]{1,0:T(8,128)S(1)} collective-permute-done((f32[32,512]{1,0:T(8,128)S(1)}, f32[32,512]{1,0:T(8,128)S(1)}, u32[]{:S(2)}, u32[]{:S(2)}) %collective-permute-start.4) | collective-permute-done | bytes 65568 | tf_op jit(solution)/shard_map/ppermute | solution.py:551
  43.8 2.3 %collective-permute-start.5 = (f32[32,512]{1,0:T(8,128)S(1)}, f32[32,512]{1,0:T(8,128)S(1)}, u32[]{:S(2)}, u32[]{:S(2)}) collective-permute-start(f32[32,512]{1,0:T(8,128)S(1)} %pad_maximum_fusion.1), channel_id=1, source_target_pairs={{0,64},{1,65},{2,66},{3,67},{4,68},{5,69},{6,70},{7,71},{8,72},{9,... | collective-permute-start | bytes 196616 | tf_op jit(solution)/shard_map/ppermute | solution.py:551
  46.1 2.7 %collective-permute-done.5 = f32[32,512]{1,0:T(8,128)S(1)} collective-permute-done((f32[32,512]{1,0:T(8,128)S(1)}, f32[32,512]{1,0:T(8,128)S(1)}, u32[]{:S(2)}, u32[]{:S(2)}) %collective-permute-start.5) | collective-permute-done | bytes 65568 | tf_op jit(solution)/shard_map/ppermute | solution.py:551
  48.9 2.4 %collective-permute-start.6 = (f32[32,512]{1,0:T(8,128)S(1)}, f32[32,512]{1,0:T(8,128)S(1)}, u32[]{:S(2)}, u32[]{:S(2)}) collective-permute-start(f32[32,512]{1,0:T(8,128)S(1)} %pad_maximum_fusion.2), channel_id=1, source_target_pairs={{0,128},{1,129},{2,130},{3,131},{4,132},{5,133},{6,134},{7,135},{8... | collective-permute-start | bytes 196616 | tf_op jit(solution)/shard_map/ppermute | solution.py:551
  51.3 4.2 %collective-permute-done.6 = f32[32,512]{1,0:T(8,128)S(1)} collective-permute-done((f32[32,512]{1,0:T(8,128)S(1)}, f32[32,512]{1,0:T(8,128)S(1)}, u32[]{:S(2)}, u32[]{:S(2)}) %collective-permute-start.6) | collective-permute-done | bytes 65568 | tf_op jit(solution)/shard_map/ppermute | solution.py:551
  55.5 1.9 %collective-permute-start.7 = (f32[32,512]{1,0:T(8,128)S(1)}, f32[32,512]{1,0:T(8,128)S(1)}, u32[]{:S(2)}, u32[]{:S(2)}) collective-permute-start(f32[32,512]{1,0:T(8,128)S(1)} %pad_maximum_fusion.3), channel_id=1, source_target_pairs={{0,256},{1,257},{2,258},{3,259},{4,260},{5,261},{6,262},{7,263},{8... | collective-permute-start | bytes 196616 | tf_op jit(solution)/shard_map/ppermute | solution.py:551
  57.5 7.0 %collective-permute-done.7 = f32[32,512]{1,0:T(8,128)S(1)} collective-permute-done((f32[32,512]{1,0:T(8,128)S(1)}, f32[32,512]{1,0:T(8,128)S(1)}, u32[]{:S(2)}, u32[]{:S(2)}) %collective-permute-start.7) | collective-permute-done | bytes 65568 | tf_op jit(solution)/shard_map/ppermute | solution.py:551
  64.6 0.0 copy-start.3
  64.6 0.0 copy-start.5
  64.6 0.0 copy-start.7
  64.6 2.0 %shard_map.142 = f32[16,16,512]{2,1,0:T(8,128)} custom-call(f32[256,512]{1,0:T(8,128)S(1)} %get-tuple-element.20.field, f32[32,512]{1,0:T(8,128)S(1)} %get-tuple-element.61.totals, f32[32,512]{1,0:T(8,128)S(1)} %get-tuple-element.62.states, f32[2,16,512]{2,1,0:T(8,128)S(1)} %get-tuple-element.24.ends, bf16[512,512]{1,0:T(8,128)(2,1)S(1)} %copy-done.1, ...), custom_call_target="tpu_custom_call" | custom-call | tf_op jit(solution)/shard_map/pallas_call | solution.py:559
  66.6 5.7 %all-to-all-start.1 = ((f32[16,16,512]{2,1,0:T(8,128)}), f32[16,16,512]{2,1,0:T(8,128)S(1)}, u32[]{:S(2)}, u32[]{:S(2)}) async-start(f32[16,16,512]{2,1,0:T(8,128)} %shard_map.142), calls=%async_computation.1 | async-start | bytes 1048576 | tf_op jit(solution)/shard_map/all_to_all | solution.py:562
  72.3 0.1 pad_add_fusion.2
  72.4 0.6 copy-done.10
  73.0 0.1 reshape.22
  73.0 12.2 %collective-permute-start = (s32[8]{0:T(128)S(1)}, s32[8]{0:T(128)S(1)}, u32[]{:S(2)}, u32[]{:S(2)}) collective-permute-start(s32[8]{0:T(128)S(1)} %get-tuple-element.60), channel_id=1, source_target_pairs={{0,16},{1,17},{2,18},{3,19},{4,20},{5,21},{6,22},{7,23},{8,24},{9,... | collective-permute-start | bytes 104 | tf_op jit(solution)/shard_map/ppermute | solution.py:509
  85.3 1.9 %collective-permute-start.1 = (s32[8]{0:T(128)S(1)}, s32[8]{0:T(128)S(1)}, u32[]{:S(2)}, u32[]{:S(2)}) collective-permute-start(s32[8]{0:T(128)S(1)} %get-tuple-element.60), channel_id=1, source_target_pairs={{0,32},{1,33},{2,34},{3,35},{4,36},{5,37},{6,38},{7,39},{8,40},{9,... | collective-permute-start | bytes 104 | tf_op jit(solution)/shard_map/ppermute | solution.py:509
  87.2 0.0 collective-permute-done
  87.2 8.4 %collective-permute-done.1 = s32[8]{0:T(128)S(1)} collective-permute-done((s32[8]{0:T(128)S(1)}, s32[8]{0:T(128)S(1)}, u32[]{:S(2)}, u32[]{:S(2)}) %collective-permute-start.1) | collective-permute-done | bytes 64 | tf_op jit(solution)/shard_map/ppermute | solution.py:509
  95.6 3.1 %collective-permute-start.2 = (s32[3,8]{1,0:T(4,128)S(1)}, s32[3,8]{1,0:T(4,128)S(1)}, u32[]{:S(2)}, u32[]{:S(2)}) collective-permute-start(s32[3,8]{1,0:T(4,128)S(1)} %get-tuple-element.58), channel_id=1, source_target_pairs={{0,1},{1,2},{2,3},{3,4},{4,5},{5,6},{6,7},{7,8},{8,9},{9,10},{10,1... | collective-permute-start | bytes 296 | tf_op jit(solution)/shard_map/ppermute | solution.py:509
  98.7 0.1 slice_reduce_fusion
  98.8 3.8 %collective-permute-done.2 = s32[3,8]{1,0:T(4,128)S(1)} collective-permute-done((s32[3,8]{1,0:T(4,128)S(1)}, s32[3,8]{1,0:T(4,128)S(1)}, u32[]{:S(2)}, u32[]{:S(2)}) %collective-permute-start.2) | collective-permute-done | bytes 128 | tf_op jit(solution)/shard_map/ppermute | solution.py:509
  102.7 0.1 reshape.23.places
  102.7 0.0 all-to-all-done.1.tiles
  102.8 5.0 %shard_map.143 = (f32[16,32,256]{2,1,0:T(8,128)}, f32[8,24,128]{2,1,0:T(8,128)S(1)}, f32[8,24,128]{2,1,0:T(8,128)S(1)}, f32[8,24,128]{2,1,0:T(8,128)S(1)}, f32[8...) custom-call(s32[36]{0:T(128)S(1)} %reshape.23.places, ...), custom_call_target="tpu_custom_call" | custom-call | tf_op jit(solution)/shard_map/pallas_call | solution.py:563
  107.8 1.9 %collective-permute-start.11 = (f32[4,24,128]{2,1,0:T(8,128)S(1)}, f32[4,24,128]{2,1,0:T(8,128)S(1)}, u32[]{:S(2)}, u32[]{:S(2)}) collective-permute-start(f32[4,24,128]{2,1,0:T(8,128)S(1)} %get-tuple-element.30), channel_id=1, source_target_pairs={{32,0},{33,1},{34,2},{35,3},{36,4},{37,5},{38,6},{39,7},{40,8},{41... | collective-permute-start | bytes 147464 | tf_op jit(solution)/shard_map/ppermute | solution.py:509
  109.7 3.1 %collective-permute-start.12 = (f32[4,24,128]{2,1,0:T(8,128)S(1)}, f32[4,24,128]{2,1,0:T(8,128)S(1)}, u32[]{:S(2)}, u32[]{:S(2)}) collective-permute-start(f32[4,24,128]{2,1,0:T(8,128)S(1)} %get-tuple-element.31), channel_id=1, source_target_pairs={{33,0},{34,1},{35,2},{36,3},{37,4},{38,5},{39,6},{40,7},{41,8},{42... | collective-permute-start | bytes 147464 | tf_op jit(solution)/shard_map/ppermute | solution.py:509
  112.8 4.0 %collective-permute-start.8 = (f32[8,24,128]{2,1,0:T(8,128)S(1)}, f32[8,24,128]{2,1,0:T(8,128)S(1)}, u32[]{:S(2)}, u32[]{:S(2)}) collective-permute-start(f32[8,24,128]{2,1,0:T(8,128)S(1)} %get-tuple-element.27), channel_id=1, source_target_pairs={{1,0},{2,1},{3,2},{4,3},{5,4},{6,5},{7,6},{8,7},{9,8},{10,9},{11,1... | collective-permute-start | bytes 294920 | tf_op jit(solution)/shard_map/ppermute | solution.py:509
  116.8 0.0 copy-start.11
  116.8 0.0 copy-start.12
  116.9 1.9 %collective-permute-start.9 = (f32[8,24,128]{2,1,0:T(8,128)S(1)}, f32[8,24,128]{2,1,0:T(8,128)S(1)}, u32[]{:S(2)}, u32[]{:S(2)}) collective-permute-start(f32[8,24,128]{2,1,0:T(8,128)S(1)} %get-tuple-element.28), channel_id=1, source_target_pairs={{16,0},{17,1},{18,2},{19,3},{20,4},{21,5},{22,6},{23,7},{24,8},{25... | collective-permute-start | bytes 294920 | tf_op jit(solution)/shard_map/ppermute | solution.py:509
  118.8 3.4 %collective-permute-start.10 = (f32[8,24,128]{2,1,0:T(8,128)S(1)}, f32[8,24,128]{2,1,0:T(8,128)S(1)}, u32[]{:S(2)}, u32[]{:S(2)}) collective-permute-start(f32[8,24,128]{2,1,0:T(8,128)S(1)} %get-tuple-element.29), channel_id=1, source_target_pairs={{17,0},{18,1},{19,2},{20,3},{21,4},{22,5},{23,6},{24,7},{25,8},{26... | collective-permute-start | bytes 294920 | tf_op jit(solution)/shard_map/ppermute | solution.py:509
  122.2 0.1 pad_add_fusion.3.meta
  122.3 4.2 %shard_map.144.refs_6_ = f32[24,9,8,128]{3,2,1,0:T(8,128)S(1)} custom-call(f32[2,192,576]{2,1,0:T(8,128)S(1)} %bitcast.42), custom_call_target="tpu_custom_call" | custom-call | tf_op jit(solution)/shard_map/pallas_call | solution.py:527
  126.5 0.0 collective-permute-done.11.refs_4_
  126.5 0.0 collective-permute-done.12.refs_5_
  126.5 0.0 collective-permute-done.8.refs_1_
  126.5 0.3 collective-permute-done.9.refs_2_
  126.8 4.1 %collective-permute-done.10.refs_3_ = f32[8,24,128]{2,1,0:T(8,128)S(1)} collective-permute-done((f32[8,24,128]{2,1,0:T(8,128)S(1)}, f32[8,24,128]{2,1,0:T(8,128)S(1)}, u32[]{:S(2)}, u32[]{:S(2)}) %collective-permute-start.10) | collective-permute-done | bytes 98336 | tf_op jit(solution)/shard_map/ppermute | solution.py:509
  130.9 22.5 %shard_map.145 = (f32[24,9,8,128]{3,2,1,0:T(8,128)S(1)}, f32[8,128]{1,0:T(8,128)S(1)}, f32[8,24,128]{2,1,0:T(8,128)S(1)}, f32[8,24,128]{2,1,0:T(8,128)S(1)}, f32[4,24,128]{2,1,0:T(8,128)S(1)}) custom-call(s32[8]{0:T(128)S(1)} %pad_add_fusion.3.meta, f32[8,24,128]{2,1,0:T(8,128)S(1)} %get-tuple-element.26.refs_0_, ...), custom_call_target="tpu_custom_call" | custom-call | tf_op jit(solution)/shard_map/pallas_call | solution.py:571
  153.4 1.9 %collective-permute-start.13 = (f32[8,24,128]{2,1,0:T(8,128)S(1)}, f32[8,24,128]{2,1,0:T(8,128)S(1)}, u32[]{:S(2)}, u32[]{:S(2)}) collective-permute-start(f32[8,24,128]{2,1,0:T(8,128)S(1)} %get-tuple-element.34.refs_0_), channel_id=1, source_target_pairs={{0,1},{1,2},{2,3},{3,4},{4,5},{5,6},{6,7},{7,8},{8,9},{9,10},{10,1... | collective-permute-start | bytes 294920 | tf_op jit(solution)/shard_map/ppermute | solution.py:509
  155.3 1.9 %collective-permute-start.15 = (f32[8,24,128]{2,1,0:T(8,128)S(1)}, f32[8,24,128]{2,1,0:T(8,128)S(1)}, u32[]{:S(2)}, u32[]{:S(2)}) collective-permute-start(f32[8,24,128]{2,1,0:T(8,128)S(1)} %get-tuple-element.35), channel_id=1, source_target_pairs={{0,17},{1,18},{2,19},{3,20},{4,21},{5,22},{6,23},{7,24},{8,25},{9,... | collective-permute-start | bytes 294920 | tf_op jit(solution)/shard_map/ppermute | solution.py:509
  157.3 6.8 %collective-permute-start.14 = (f32[8,24,128]{2,1,0:T(8,128)S(1)}, f32[8,24,128]{2,1,0:T(8,128)S(1)}, u32[]{:S(2)}, u32[]{:S(2)}) collective-permute-start(f32[8,24,128]{2,1,0:T(8,128)S(1)} %get-tuple-element.35), channel_id=1, source_target_pairs={{0,16},{1,17},{2,18},{3,19},{4,20},{5,21},{6,22},{7,23},{8,24},{9,... | collective-permute-start | bytes 294920 | tf_op jit(solution)/shard_map/ppermute | solution.py:509
  164.1 8.8 %collective-permute-start.17 = (f32[4,24,128]{2,1,0:T(8,128)S(1)}, f32[4,24,128]{2,1,0:T(8,128)S(1)}, u32[]{:S(2)}, u32[]{:S(2)}) collective-permute-start(f32[4,24,128]{2,1,0:T(8,128)S(1)} %get-tuple-element.36), channel_id=1, source_target_pairs={{0,33},{1,34},{2,35},{3,36},{4,37},{5,38},{6,39},{7,40},{8,41},{9,... | collective-permute-start | bytes 147464 | tf_op jit(solution)/shard_map/ppermute | solution.py:509
  172.9 3.1 %collective-permute-start.16 = (f32[4,24,128]{2,1,0:T(8,128)S(1)}, f32[4,24,128]{2,1,0:T(8,128)S(1)}, u32[]{:S(2)}, u32[]{:S(2)}) collective-permute-start(f32[4,24,128]{2,1,0:T(8,128)S(1)} %get-tuple-element.36), channel_id=1, source_target_pairs={{0,32},{1,33},{2,34},{3,35},{4,36},{5,37},{6,38},{7,39},{8,40},{9,... | collective-permute-start | bytes 147464 | tf_op jit(solution)/shard_map/ppermute | solution.py:509
  176.0 5.3 %shard_map.146 = f32[2,192,576]{2,1,0:T(8,128)} custom-call(f32[24,9,8,128]{3,2,1,0:T(8,128)S(1)} %get-tuple-element.32.planes, f32[8,128]{1,0:T(8,128)S(1)} %get-tuple-element.33.scale), custom_call_target="tpu_custom_call" | custom-call | tf_op jit(solution)/shard_map/pallas_call | solution.py:589
  181.3 0.0 collective-permute-done.17.refs_5_
  181.3 2.5 %collective-permute-done.16.refs_4_ = f32[4,24,128]{2,1,0:T(8,128)S(1)} collective-permute-done((f32[4,24,128]{2,1,0:T(8,128)S(1)}, f32[4,24,128]{2,1,0:T(8,128)S(1)}, u32[]{:S(2)}, u32[]{:S(2)}) %collective-permute-start.16) | collective-permute-done | bytes 49184 | tf_op jit(solution)/shard_map/ppermute | solution.py:509
  183.8 0.0 collective-permute-done.13.refs_1_
  183.8 0.0 collective-permute-done.15.refs_3_
  183.8 5.2 %shard_map.147 = f32[16,32,256]{2,1,0:T(8,128)} custom-call(s32[36]{0:T(128)S(1)} %reshape.23.places, f32[8,24,128]{2,1,0:T(8,128)S(1)} %get-tuple-element.34.refs_0_, f32[8,24,128]{2,1,0:T(8,128)S(1)} %collective-permute-done.13.refs_1_, f32[8,24,128]{2,1,0:T(8,128)S(1)} %collective-permute-done.14.refs_2_, ...), custom_call_target="tpu_custom_call" | custom-call | tf_op jit(solution)/shard_map/pallas_call | solution.py:595
  (39 shorter events, 0.3 us)
Async XLA Ops:
  0.6 0.9 copy-start.4
  1.5 0.9 copy-start.6
  2.4 1.0 copy-start.8
  4.7 23.6 %copy-start = (bf16[512,512]{1,0:T(8,128)(2,1)S(1)}, bf16[512,512]{1,0:T(8,128)(2,1)}, u32[]{:S(2)}) copy-start(bf16[512,512]{1,0:T(8,128)(2,1)} %constant.77.clone.table_low) | copy-start | bytes 1572868
  4.7 23.6 %copy-start.1 = (bf16[512,512]{1,0:T(8,128)(2,1)S(1)}, bf16[512,512]{1,0:T(8,128)(2,1)}, u32[]{:S(2)}) copy-start(bf16[512,512]{1,0:T(8,128)(2,1)} %constant.76.clone.table_high) | copy-start | bytes 1572868
  4.7 23.6 %all-to-all-start = ((f32[16,16,512]{2,1,0:T(8,128)}), f32[16,16,512]{2,1,0:T(8,128)S(1)}, u32[]{:S(2)}, u32[]{:S(2)}) async-start(f32[16,16,512]{2,1,0:T(8,128)} %shard_map.139), calls=%async_computation | async-start | bytes 1048576 | tf_op jit(solution)/shard_map/all_to_all | solution.py:540
  14.5 13.8 %copy-start.9 = (f32[1,512]{1,0:T(1,128)S(1)}, f32[1,512]{1,0:T(1,128)}, u32[]{:S(2)}) copy-start(f32[1,512]{1,0:T(1,128)} %constant.80.clone.ey) | copy-start | bytes 6148
  29.2 4.5 %collective-permute-start.3 = (f32[32,512]{1,0:T(8,128)S(1)}, f32[32,512]{1,0:T(8,128)S(1)}, u32[]{:S(2)}, u32[]{:S(2)}) collective-permute-start(f32[32,512]{1,0:T(8,128)S(1)} %get-tuple-element.21), channel_id=1, source_target_pairs={{0,16},{1,17},{2,18},{3,19},{4,20},{5,21},{6,22},{7,23},{8,24},{9,... | collective-permute-start | bytes 196616 | tf_op jit(solution)/shard_map/ppermute | solution.py:551
  33.7 10.0 %collective-permute-start.4 = (f32[32,512]{1,0:T(8,128)S(1)}, f32[32,512]{1,0:T(8,128)S(1)}, u32[]{:S(2)}, u32[]{:S(2)}) collective-permute-start(f32[32,512]{1,0:T(8,128)S(1)} %pad_maximum_fusion), channel_id=1, source_target_pairs={{0,32},{1,33},{2,34},{3,35},{4,36},{5,37},{6,38},{7,39},{8,40},{9,... | collective-permute-start | bytes 196616 | tf_op jit(solution)/shard_map/ppermute | solution.py:551
  43.8 5.0 %collective-permute-start.5 = (f32[32,512]{1,0:T(8,128)S(1)}, f32[32,512]{1,0:T(8,128)S(1)}, u32[]{:S(2)}, u32[]{:S(2)}) collective-permute-start(f32[32,512]{1,0:T(8,128)S(1)} %pad_maximum_fusion.1), channel_id=1, source_target_pairs={{0,64},{1,65},{2,66},{3,67},{4,68},{5,69},{6,70},{7,71},{8,72},{9,... | collective-permute-start | bytes 196616 | tf_op jit(solution)/shard_map/ppermute | solution.py:551
  48.9 6.6 %collective-permute-start.6 = (f32[32,512]{1,0:T(8,128)S(1)}, f32[32,512]{1,0:T(8,128)S(1)}, u32[]{:S(2)}, u32[]{:S(2)}) collective-permute-start(f32[32,512]{1,0:T(8,128)S(1)} %pad_maximum_fusion.2), channel_id=1, source_target_pairs={{0,128},{1,129},{2,130},{3,131},{4,132},{5,133},{6,134},{7,135},{8... | collective-permute-start | bytes 196616 | tf_op jit(solution)/shard_map/ppermute | solution.py:551
  55.5 8.9 %collective-permute-start.7 = (f32[32,512]{1,0:T(8,128)S(1)}, f32[32,512]{1,0:T(8,128)S(1)}, u32[]{:S(2)}, u32[]{:S(2)}) collective-permute-start(f32[32,512]{1,0:T(8,128)S(1)} %pad_maximum_fusion.3), channel_id=1, source_target_pairs={{0,256},{1,257},{2,258},{3,259},{4,260},{5,261},{6,262},{7,263},{8... | collective-permute-start | bytes 196616 | tf_op jit(solution)/shard_map/ppermute | solution.py:551
  64.6 38.2 %copy-start.3 = (f32[16,32,256]{2,1,0:T(8,128)S(1)}, f32[16,32,256]{2,1,0:T(8,128)}, u32[]{:S(2)}) copy-start(f32[16,32,256]{2,1,0:T(8,128)} %external.1) | copy-start | bytes 1572868
  64.6 38.2 %copy-start.5 = (bf16[256,256]{1,0:T(8,128)(2,1)S(1)}, bf16[256,256]{1,0:T(8,128)(2,1)}, u32[]{:S(2)}) copy-start(bf16[256,256]{1,0:T(8,128)(2,1)} %constant.79.clone.table_low) | copy-start | bytes 393220
  64.6 38.2 %copy-start.7 = (bf16[256,256]{1,0:T(8,128)(2,1)S(1)}, bf16[256,256]{1,0:T(8,128)(2,1)}, u32[]{:S(2)}) copy-start(bf16[256,256]{1,0:T(8,128)(2,1)} %constant.78.clone.table_high) | copy-start | bytes 393220
  66.6 55.7 %copy-start.2 = (f32[2,8,24,576]{3,2,1,0:T(8,128)S(1)}, f32[2,8,24,576]{3,2,1,0:T(8,128)}, u32[]{:S(2)}) copy-start(f32[2,8,24,576]{3,2,1,0:T(8,128)} %param.14) | copy-start | bytes 2654212
  66.6 36.1 %all-to-all-start.1 = ((f32[16,16,512]{2,1,0:T(8,128)}), f32[16,16,512]{2,1,0:T(8,128)S(1)}, u32[]{:S(2)}, u32[]{:S(2)}) async-start(f32[16,16,512]{2,1,0:T(8,128)} %shard_map.142), calls=%async_computation.1 | async-start | bytes 1048576 | tf_op jit(solution)/shard_map/all_to_all | solution.py:562
  72.3 0.7 copy-start.10
  73.0 14.2 %collective-permute-start = (s32[8]{0:T(128)S(1)}, s32[8]{0:T(128)S(1)}, u32[]{:S(2)}, u32[]{:S(2)}) collective-permute-start(s32[8]{0:T(128)S(1)} %get-tuple-element.60), channel_id=1, source_target_pairs={{0,16},{1,17},{2,18},{3,19},{4,20},{5,21},{6,22},{7,23},{8,24},{9,... | collective-permute-start | bytes 104 | tf_op jit(solution)/shard_map/ppermute | solution.py:509
  85.3 10.3 %collective-permute-start.1 = (s32[8]{0:T(128)S(1)}, s32[8]{0:T(128)S(1)}, u32[]{:S(2)}, u32[]{:S(2)}) collective-permute-start(s32[8]{0:T(128)S(1)} %get-tuple-element.60), channel_id=1, source_target_pairs={{0,32},{1,33},{2,34},{3,35},{4,36},{5,37},{6,38},{7,39},{8,40},{9,... | collective-permute-start | bytes 104 | tf_op jit(solution)/shard_map/ppermute | solution.py:509
  95.6 7.0 %collective-permute-start.2 = (s32[3,8]{1,0:T(4,128)S(1)}, s32[3,8]{1,0:T(4,128)S(1)}, u32[]{:S(2)}, u32[]{:S(2)}) collective-permute-start(s32[3,8]{1,0:T(4,128)S(1)} %get-tuple-element.58), channel_id=1, source_target_pairs={{0,1},{1,2},{2,3},{3,4},{4,5},{5,6},{6,7},{7,8},{8,9},{9,10},{10,1... | collective-permute-start | bytes 296 | tf_op jit(solution)/shard_map/ppermute | solution.py:509
  107.8 18.7 %collective-permute-start.11 = (f32[4,24,128]{2,1,0:T(8,128)S(1)}, f32[4,24,128]{2,1,0:T(8,128)S(1)}, u32[]{:S(2)}, u32[]{:S(2)}) collective-permute-start(f32[4,24,128]{2,1,0:T(8,128)S(1)} %get-tuple-element.30), channel_id=1, source_target_pairs={{32,0},{33,1},{34,2},{35,3},{36,4},{37,5},{38,6},{39,7},{40,8},{41... | collective-permute-start | bytes 147464 | tf_op jit(solution)/shard_map/ppermute | solution.py:509
  109.7 16.8 %collective-permute-start.12 = (f32[4,24,128]{2,1,0:T(8,128)S(1)}, f32[4,24,128]{2,1,0:T(8,128)S(1)}, u32[]{:S(2)}, u32[]{:S(2)}) collective-permute-start(f32[4,24,128]{2,1,0:T(8,128)S(1)} %get-tuple-element.31), channel_id=1, source_target_pairs={{33,0},{34,1},{35,2},{36,3},{37,4},{38,5},{39,6},{40,7},{41,8},{42... | collective-permute-start | bytes 147464 | tf_op jit(solution)/shard_map/ppermute | solution.py:509
  112.8 13.7 %collective-permute-start.8 = (f32[8,24,128]{2,1,0:T(8,128)S(1)}, f32[8,24,128]{2,1,0:T(8,128)S(1)}, u32[]{:S(2)}, u32[]{:S(2)}) collective-permute-start(f32[8,24,128]{2,1,0:T(8,128)S(1)} %get-tuple-element.27), channel_id=1, source_target_pairs={{1,0},{2,1},{3,2},{4,3},{5,4},{6,5},{7,6},{8,7},{9,8},{10,9},{11,1... | collective-permute-start | bytes 294920 | tf_op jit(solution)/shard_map/ppermute | solution.py:509
  116.8 5.3 %copy-start.11 = (s32[2]{0:T(128)S(1)}, s32[2]{0:T(128)}, u32[]{:S(2)}) copy-start(s32[2]{0:T(128)} %param.16) | copy-start | bytes 28
  116.8 5.3 %copy-start.12 = (s32[2]{0:T(128)S(1)}, s32[2]{0:T(128)}, u32[]{:S(2)}) copy-start(s32[2]{0:T(128)} %param.17) | copy-start | bytes 28
  116.9 10.0 %collective-permute-start.9 = (f32[8,24,128]{2,1,0:T(8,128)S(1)}, f32[8,24,128]{2,1,0:T(8,128)S(1)}, u32[]{:S(2)}, u32[]{:S(2)}) collective-permute-start(f32[8,24,128]{2,1,0:T(8,128)S(1)} %get-tuple-element.28), channel_id=1, source_target_pairs={{16,0},{17,1},{18,2},{19,3},{20,4},{21,5},{22,6},{23,7},{24,8},{25... | collective-permute-start | bytes 294920 | tf_op jit(solution)/shard_map/ppermute | solution.py:509
  118.8 12.1 %collective-permute-start.10 = (f32[8,24,128]{2,1,0:T(8,128)S(1)}, f32[8,24,128]{2,1,0:T(8,128)S(1)}, u32[]{:S(2)}, u32[]{:S(2)}) collective-permute-start(f32[8,24,128]{2,1,0:T(8,128)S(1)} %get-tuple-element.29), channel_id=1, source_target_pairs={{17,0},{18,1},{19,2},{20,3},{21,4},{22,5},{23,6},{24,7},{25,8},{26... | collective-permute-start | bytes 294920 | tf_op jit(solution)/shard_map/ppermute | solution.py:509
  153.4 30.4 %collective-permute-start.13 = (f32[8,24,128]{2,1,0:T(8,128)S(1)}, f32[8,24,128]{2,1,0:T(8,128)S(1)}, u32[]{:S(2)}, u32[]{:S(2)}) collective-permute-start(f32[8,24,128]{2,1,0:T(8,128)S(1)} %get-tuple-element.34.refs_0_), channel_id=1, source_target_pairs={{0,1},{1,2},{2,3},{3,4},{4,5},{5,6},{6,7},{7,8},{8,9},{9,10},{10,1... | collective-permute-start | bytes 294920 | tf_op jit(solution)/shard_map/ppermute | solution.py:509
  155.3 28.4 %collective-permute-start.15 = (f32[8,24,128]{2,1,0:T(8,128)S(1)}, f32[8,24,128]{2,1,0:T(8,128)S(1)}, u32[]{:S(2)}, u32[]{:S(2)}) collective-permute-start(f32[8,24,128]{2,1,0:T(8,128)S(1)} %get-tuple-element.35), channel_id=1, source_target_pairs={{0,17},{1,18},{2,19},{3,20},{4,21},{5,22},{6,23},{7,24},{8,25},{9,... | collective-permute-start | bytes 294920 | tf_op jit(solution)/shard_map/ppermute | solution.py:509
  157.3 26.5 %collective-permute-start.14 = (f32[8,24,128]{2,1,0:T(8,128)S(1)}, f32[8,24,128]{2,1,0:T(8,128)S(1)}, u32[]{:S(2)}, u32[]{:S(2)}) collective-permute-start(f32[8,24,128]{2,1,0:T(8,128)S(1)} %get-tuple-element.35), channel_id=1, source_target_pairs={{0,16},{1,17},{2,18},{3,19},{4,20},{5,21},{6,22},{7,23},{8,24},{9,... | collective-permute-start | bytes 294920 | tf_op jit(solution)/shard_map/ppermute | solution.py:509
  164.1 17.2 %collective-permute-start.17 = (f32[4,24,128]{2,1,0:T(8,128)S(1)}, f32[4,24,128]{2,1,0:T(8,128)S(1)}, u32[]{:S(2)}, u32[]{:S(2)}) collective-permute-start(f32[4,24,128]{2,1,0:T(8,128)S(1)} %get-tuple-element.36), channel_id=1, source_target_pairs={{0,33},{1,34},{2,35},{3,36},{4,37},{5,38},{6,39},{7,40},{8,41},{9,... | collective-permute-start | bytes 147464 | tf_op jit(solution)/shard_map/ppermute | solution.py:509
  172.9 10.9 %collective-permute-start.16 = (f32[4,24,128]{2,1,0:T(8,128)S(1)}, f32[4,24,128]{2,1,0:T(8,128)S(1)}, u32[]{:S(2)}, u32[]{:S(2)}) collective-permute-start(f32[4,24,128]{2,1,0:T(8,128)S(1)} %get-tuple-element.36), channel_id=1, source_target_pairs={{0,32},{1,33},{2,34},{3,35},{4,36},{5,37},{6,38},{7,39},{8,40},{9,... | collective-permute-start | bytes 147464 | tf_op jit(solution)/shard_map/ppermute | solution.py:509
where the time goes:
time: 190 us; the launch traced here: 189 us
  starting transfers between devices  87.8 us (46%)
  waiting for transfers between devices  48.8 us (26%)
  Pallas kernels  46.4 us (24%)
  local copies, waits for them, and re-layouts  4.49 us (2%)
    ppermute x13, starting transfers between devices, moved(): return lax.ppermute(x, ALL, pairs)  54.1 us
    pallas_call x1, Pallas kernels, body(): call(filter_fragments, [shape(FRAG, 9, 8, 128), shape(8, 128)] + [shape(n...  22.5 us
    ppermute x13, waiting for transfers between devices, moved(): return lax.ppermute(x, ALL, pairs)  19.1 us
    ppermute x5, starting transfers between devices, body(): got = lax.ppermute(totals, ALL, pairs)  18.2 us
    ppermute x5, waiting for transfers between devices, body(): got = lax.ppermute(totals, ALL, pairs)  16.6 us
    all_to_all x2, starting transfers between devices, body(): tiles = lax.all_to_all(tiles, 'py', split_axis=0, concat_axis=0, tiled=True)  15.5 us
    all_to_all x2, waiting for transfers between devices, body(): tiles = lax.all_to_all(tiles, 'py', split_axis=0, concat_axis=0, tiled=True)  13.1 us
    pallas_call x1, Pallas kernels, body(): call(orbitals_out, shape(2, NORB * FRAG, FRAG * FRAG), [pltpu.VMEM((2, 5,...  5.25 us
  transfers between devices with their start and end apart: 20, of which 11 were waited for; matrix products, arithmetic and copies ran while one was open for 1% of the time, Pallas kernels for 5%

commit v1 on v0

--- a/solution.py
+++ b/solution.py
@@ -21,6 +21,7 @@
 BF16 = jnp.bfloat16
 VMEM = pl.BlockSpec(memory_space=pltpu.VMEM)
 SMEM = pl.BlockSpec(memory_space=pltpu.SMEM)
+ANYWHERE = pl.BlockSpec(memory_space=pl.ANY)
 
 
 def sine_table(length):
@@ -58,11 +59,11 @@
     return one(left[0], right[0]) + (one(left[0], right[1]) + one(left[1], right[0]))
 
 
-def call(kernel, outs, scratch=(), smem=(), count=1):
+def call(kernel, outs, scratch=(), smem=(), count=1, space=VMEM):
     return pl.pallas_call(
         kernel,
         out_shape=outs,
-        in_specs=[SMEM if k in smem else VMEM for k in range(count)],
+        in_specs=[SMEM if k in smem else space for k in range(count)],
         out_specs=jax.tree.map(lambda _: VMEM, outs),
         scratch_shapes=list(scratch),
         compiler_params=pltpu.CompilerParams(vmem_limit_bytes=48 * 1024 * 1024),
@@ -88,9 +89,16 @@
     return 1.0 / (1.0 + 0.5 * gap + root), 0.5 / root
 
 
-def forward_z(density, table_high, table_low, out):
-    cells = density[...].reshape(ROWS * COLS, NZ)
-    spectrum = dot3((table_high[...], table_low[...]), split2(cells), ((1,), (1,)))
+def forward_z(density, table_high, table_low, out, cells, high, low, sems):
+    copies = [
+        pltpu.make_async_copy(source, target, sems.at[k])
+        for k, (source, target) in enumerate(((density, cells), (table_high, high), (table_low, low)))
+    ]
+    for one in copies:
+        one.start()
+    for one in copies:
+        one.wait()
+    spectrum = dot3((high[...], low[...]), split2(cells[...].reshape(ROWS * COLS, NZ)), ((1,), (1,)))
     out[...] = spectrum.reshape(NPY, KZ, ROWS * COLS)
 
 
@@ -103,12 +111,17 @@
     after = before
     for bit in range(5):
         upper = (place[0] >> bit) % 2 == 1
-        power_out[bit] = power
-        weight_out[bit] = jnp.where(upper, before, after)
+        if bit < 3:
+            power_out[bit] = power
+        if bit < 2:
+            weight_out[bit] = jnp.where(upper, before, after)
+        if bit == 2:
+            ends_out[0] = before
+            ends_out[1] = after
         before, after = jnp.where(upper, before * power, before), jnp.where(upper, after, after * power)
         power = power * power
-    ends_out[0] = before
-    ends_out[1] = after
+    ends_out[2] = before
+    ends_out[3] = after
 
 
 def forward_y(tiles, table_high, table_low, ey, ez, field_out, moment_out, merged):
@@ -134,16 +147,25 @@
     moment_out[KZ:] = last
 
 
-def back_y(field, totals, states, ends, table_high, table_low, ey, ez, tiles_out, solved):
+def back_y(place, field, totals, right, left, power, ends, *rest):
+    table_high, table_low, ey, ez, tiles_out, solved = rest
     rate, scale = decay(ey[...], ez[...])
     across = rate
     for _ in range(9):
         across = across * across
     across = across * rate
     norm = rate / (1.0 - across * across)
-    right_total, left_total = totals[:KZ], totals[KZ:]
-    state = states[:KZ] - norm * (left_total - across * right_total) * ends[0]
-    left = states[KZ:] - norm * (right_total - across * left_total) * ends[1]
+    four = power[2]
+    right_total = left_total = jnp.zeros((KZ, NY), F32)
+    state, after = right_total, left_total
+    for k in range(NPX // 4):
+        state = jnp.where(k == place[0], right_total, state)
+        right_total = totals[k, :KZ] + four * right_total
+    for k in range(NPX // 4 - 1, -1, -1):
+        after = jnp.where(k == place[0], left_total, after)
+        left_total = totals[k, KZ:] + four * left_total
+    state = right[...] + ends[0] * state - norm * (left_total - across * right_total) * ends[2]
+    left = left[...] + ends[1] * after - norm * (right_total - across * left_total) * ends[3]
     for row in range(ROWS):
         state = field[row * KZ : (row + 1) * KZ] + rate * state
         solved[row * KZ : (row + 1) * KZ] = state
@@ -186,20 +208,24 @@
     for k, (down, along) in enumerate(STEPS):
         groups = 8 if down < 2 else 4
 
-        def cut(group, carry, k=k, along=along, groups=groups):
-            total = None
-            for slot in range(4):
-                frag = slot % 2
-                row = group + groups * (slot // 2)
-                col, depth = places[6 * k + 3 * frag + 1], places[6 * k + 3 * frag + 2]
-                cols = pl.ds(32 + col - 32 * along, FRAG)
-                window = jnp.where(lane >= depth, grid[0, row, cols, :], grid[1, row, cols, :])
-                window = pltpu.roll(window, (256 + 32 * slot - depth) & 127, 1)
-                total = window if total is None else jnp.where(slot_of == slot, window, total)
-            pieces[k][group] = total
+        def cut(number, carry, k=k, along=along, groups=groups):
+            totals = []
+            for part in range(4):
+                total = None
+                for slot in range(4):
+                    frag = slot % 2
+                    row = 4 * number + part + groups * (slot // 2)
+                    col, depth = places[6 * k + 3 * frag + 1], places[6 * k + 3 * frag + 2]
+                    cols = pl.ds(32 + col - 32 * along, FRAG)
+                    window = jnp.where(lane >= depth, grid[0, row, cols, :], grid[1, row, cols, :])
+                    window = pltpu.roll(window, (256 + 32 * slot - depth) & 127, 1)
+                    total = window if total is None else jnp.where(slot_of == slot, window, total)
+                totals.append(total)
+            for part in range(4):
+                pieces[k][4 * number + part] = totals[part]
             return carry
 
-        lax.fori_loop(0, groups, cut, 0)
+        lax.fori_loop(0, groups // 4, cut, 0)
 
 
 def orbitals_in(orbitals, out, strips, turned):
@@ -209,7 +235,7 @@
             strips[frag, tile, :, :width] = orbitals[frag, :, tile * 128 : tile * 128 + width]
     lane = lanes(8)
 
-    def plane(x, carry):
+    def plane(x, place):
         rows = []
         for yc in range(8):
             tile, off = divmod(72 * yc, 128)
@@ -219,22 +245,25 @@
                     other = rolled(strips[frag, tile + 1, pl.ds(x, 8, stride=FRAG), :], -off)
                     piece = jnp.where(lane < 128 - off, piece, other)
                 rows.append(piece)
-        turned[...] = jnp.concatenate(rows, 0).T
-        for k in range(9):
-            out[x, k] = turned[pl.ds(k // 3 * FRAG + k % 3, 8, stride=3), :]
+        place[...] = jnp.concatenate(rows, 0).T
+
+    def planes(number, carry):
+        for part in range(3):
+            plane(3 * number + part, turned.at[part])
+        for part in range(3):
+            for k in range(9):
+                rows = pl.ds(k // 3 * FRAG + k % 3, 8, stride=3)
+                out[3 * number + part, k] = turned.at[part][rows, :]
         return carry
 
-    lax.fori_loop(0, FRAG, plane, 0)
+    lax.fori_loop(0, FRAG // 3, planes, 0)
 
 
 def orbitals_out(planes, scale, out, strips, turned):
     lane = lanes(8)
     factor = scale[...]
 
-    def plane(x, carry):
-        for k in range(9):
-            turned[pl.ds(k // 3 * FRAG + k % 3, 8, stride=3), :] = planes[x, k] * factor
-        rows = turned[...].T
+    def plane(x, rows):
         for frag in range(2):
             for tile in range(5):
                 total = None
@@ -248,9 +277,18 @@
                         else:
                             total = jnp.where(lane >= start, piece, total)
                 strips[frag, tile, pl.ds(x, 8, stride=FRAG), :] = total
+
+    def trip(number, carry):
+        for part in range(3):
+            for k in range(9):
+                rows = pl.ds(k // 3 * FRAG + k % 3, 8, stride=3)
+                turned.at[part][rows, :] = planes[3 * number + part, k] * factor
+        rows = [turned[part].T for part in range(3)]
+        for part in range(3):
+            plane(3 * number + part, rows[part])
         return carry
 
-    lax.fori_loop(0, FRAG, plane, 0)
+    lax.fori_loop(0, FRAG // 3, trip, 0)
     for frag in range(2):
         for tile in range(5):
             width = min(128, FRAG * FRAG - tile * 128)
@@ -302,14 +340,20 @@
     for down in range(3):
         groups = 8 if down < 2 else 4
 
-        def unpack(group, carry, down=down, groups=groups):
-            both = pieces[2 * down][group] + pieces[2 * down + 1][group]
-            for slot in range(4):
-                row = 16 * down + group + groups * (slot // 2)
-                boxes[slot % 2, pl.ds(pl.multiple_of(row * FRAG, 8), FRAG), :] = rolled(both, -32 * slot)
+        def unpack(number, carry, down=down, groups=groups):
+            moved_windows = []
+            for part in range(4):
+                group = 4 * number + part
+                both = pieces[2 * down][group] + pieces[2 * down + 1][group]
+                moved_windows.append([rolled(both, -32 * slot) for slot in range(4)])
+            for part in range(4):
+                for slot in range(4):
+                    row = 16 * down + 4 * number + part + groups * (slot // 2)
+                    rows = pl.ds(pl.multiple_of(row * FRAG, 8), FRAG)
+                    boxes[slot % 2, rows, :] = moved_windows[part][slot]
             return carry
 
-        lax.fori_loop(0, groups, unpack, 0)
+        lax.fori_loop(0, groups // 4, unpack, 0)
     lowest = None
     for part in range(3):
         rows = []
@@ -324,9 +368,10 @@
                         jnp.where(lane < 2 * FRAG, rolled(took[1], FRAG), rolled(took[2], 2 * FRAG)),
                     )
                 )
-        turned[...] = jnp.concatenate(rows, 0).T
+        turned[part] = jnp.concatenate(rows, 0).T
+    for part in range(3):
         for k in range(9):
-            value = turned[pl.ds(k // 3 * FRAG + k % 3, 8, stride=3), :]
+            value = turned.at[part][pl.ds(k // 3 * FRAG + k % 3, 8, stride=3), :]
             compact[9 * part + k] = value
             lowest = value if lowest is None else jnp.minimum(lowest, value)
             highest = value if part + k == 0 else jnp.maximum(highest, value)
@@ -350,16 +395,17 @@
     coupling = -inverse
     degree = jnp.where(second, meta[5], meta[4])
 
-    def apply(source, target, initial=False, step=None):
+    def apply(source, target, earlier=None, initial=False, step=None):
         live = None if step is None else step <= degree
+        earlier = target if earlier is None else earlier
 
         def chunk(number, carry):
             behind, here = list(carry[:9]), list(carry[9:])
-            for k4 in range(4):
-                x = 4 * number + k4
+            for k4 in range(8):
+                x = 8 * number + k4
                 ahead_x = jnp.minimum(x + 1, FRAG - 1)
                 ahead = [source[ahead_x, k] for k in range(9)]
-                if k4 == 3:
+                if k4 == 7:
                     ahead = [jnp.where(x + 1 < FRAG, v, 0.0) for v in ahead]
                 for k in range(9):
                     yi, zi = divmod(k, 3)
@@ -381,7 +427,7 @@
                     else:
                         total = total + jnp.where(sub < 7, rolled(here[k - 2], -1, 0), 0.0)
                     image = potential[x, k] * here[k] + coupling * total
-                    following = 0.5 * image if initial else image - target[x, k]
+                    following = 0.5 * image if initial else image - earlier[x, k]
                     if live is not None:
                         following = jnp.where(live, following, here[k])
                     target[x, k] = following
@@ -389,40 +435,33 @@
             return tuple(behind + here)
 
         zero = [jnp.zeros((8, 128), F32)] * 9
-        lax.fori_loop(0, 6, chunk, tuple(zero + [source[0, k] for k in range(9)]))
-
-    def copy(x, carry):
-        out[x] = start[x]
-        return carry
-
-    lax.fori_loop(0, FRAG, copy, 0)
-    apply(out, other, initial=True)
+        lax.fori_loop(0, 3, chunk, tuple(zero + [source[0, k] for k in range(9)]))
+
+    apply(start, other, initial=True)
+    apply(other, out, earlier=start)
     fewest = jnp.minimum(meta[4], meta[5])
     most = jnp.maximum(meta[4], meta[5])
-    plain = (fewest - 1) // 2
-    pairs = most // 2
+    plain = (fewest - 2) // 2
+    pairs = (most - 1) // 2
 
     def free_pair(pair, carry):
+        apply(out, other)
         apply(other, out)
-        apply(out, other)
         return carry
 
     def held_pair(pair, carry):
-        apply(other, out, step=2 * pair + 2)
         apply(out, other, step=2 * pair + 3)
+        apply(other, out, step=2 * pair + 4)
         return carry
 
     lax.fori_loop(0, plain, free_pair, 0)
     lax.fori_loop(plain, pairs, held_pair, 0)
 
     def squares(x, sums):
-        for k in range(9):
-            value = other[x, k]
-            sums = sums + value * value
-            out[x, k] = value
-        return sums
-
-    sums = lax.fori_loop(0, FRAG, squares, jnp.zeros((8, 128), F32))
+        return tuple(sums[k] + out[x, k] * out[x, k] for k in range(9))
+
+    sums = lax.fori_loop(0, FRAG, squares, (jnp.zeros((8, 128), F32),) * 9)
+    sums = sum(sums[1:], sums[0])
     sums = jnp.sum(sums, axis=0, keepdims=True)
     sums = jnp.broadcast_to(sums, (8, 128))
     for step in (16, 32, 64):
@@ -441,10 +480,11 @@
         for k in range(9):
             values = []
             for x in range(8):
-                value = other[8 * part + x, k] * scale
+                value = out[8 * part + x, k] * scale
                 values.append(value * value)
-            turned[pl.ds(k // 3 * FRAG + k % 3, 8, stride=3), :] = gather_sums(values, lane) * weight
-        rows = turned[...].T
+            turned.at[part][pl.ds(k // 3 * FRAG + k % 3, 8, stride=3), :] = gather_sums(values, lane) * weight
+    for part in range(3):
+        rows = turned[part].T
         for yc in range(8):
             for frag in range(2):
                 piece = rows[(2 * yc + frag) * 8 : (2 * yc + frag) * 8 + 8]
@@ -455,17 +495,21 @@
     for down in range(3):
         groups = 8 if down < 2 else 4
 
-        def share(group, carry, down=down, groups=groups):
-            total = None
-            for slot in range(4):
-                row = 16 * down + group + groups * (slot // 2)
-                piece = spilled[slot % 2, pl.ds(pl.multiple_of(row * FRAG, 8), FRAG), :]
-                piece = rolled(piece, 32 * slot)
-                total = piece if total is None else jnp.where(slot_of == slot, piece, total)
-            shares[down][group] = total
+        def share(number, carry, down=down, groups=groups):
+            totals = []
+            for part in range(4):
+                total = None
+                for slot in range(4):
+                    row = 16 * down + 4 * number + part + groups * (slot // 2)
+                    piece = spilled[slot % 2, pl.ds(pl.multiple_of(row * FRAG, 8), FRAG), :]
+                    piece = rolled(piece, 32 * slot)
+                    total = piece if total is None else jnp.where(slot_of == slot, piece, total)
+                totals.append(total)
+            for part in range(4):
+                shares[down][4 * number + part] = totals[part]
             return carry
 
-        lax.fori_loop(0, groups, share, 0)
+        lax.fori_loop(0, groups // 4, share, 0)
 
 
 def patch(places, *refs):
@@ -481,20 +525,25 @@
     for k, (down, along) in enumerate(STEPS):
         groups = 8 if down < 2 else 4
 
-        def add(group, carry, k=k, along=along, groups=groups):
-            both = shares[k][group]
-            for slot in range(4):
-                frag = slot % 2
-                row = group + groups * (slot // 2)
-                col, depth = places[6 * k + 3 * frag + 1], places[6 * k + 3 * frag + 2]
-                piece = pltpu.roll(both, (256 + depth - 32 * slot) & 127, 1)
-                piece = jnp.where(((lane - depth) & 127) < FRAG, piece, 0.0)
-                cols = pl.ds(32 + col - 32 * along, FRAG)
-                grid[0, row, cols, :] += jnp.where(lane >= depth, piece, 0.0)
-                grid[1, row, cols, :] += jnp.where(lane >= depth, 0.0, piece)
+        def add(number, carry, k=k, along=along, groups=groups):
+            pieces = []
+            for part in range(4):
+                both = shares[k][4 * number + part]
+                for slot in range(4):
+                    depth = places[6 * k + 3 * (slot % 2) + 2]
+                    pieces.append(pltpu.roll(both, (256 + depth - 32 * slot) & 127, 1))
+            for part in range(4):
+                for slot in range(4):
+                    frag = slot % 2
+                    row = 4 * number + part + groups * (slot // 2)
+                    col, depth = places[6 * k + 3 * frag + 1], places[6 * k + 3 * frag + 2]
+                    piece = jnp.where(((lane - depth) & 127) < FRAG, pieces[4 * part + slot], 0.0)
+                    cols = pl.ds(32 + col - 32 * along, FRAG)
+                    grid[0, row, cols, :] += jnp.where(lane >= depth, piece, 0.0)
+                    grid[1, row, cols, :] += jnp.where(lane >= depth, 0.0, piece)
             return carry
 
-        lax.fori_loop(0, groups, add, 0)
+        lax.fori_loop(0, groups // 4, add, 0)
     for half in range(2):
         out[:, :, half * 128 : half * 128 + 128] = grid[half, :, 32 : 32 + COLS]
 
@@ -527,16 +576,27 @@
     planes = call(
         orbitals_in,
         shape(FRAG, 9, 8, 128),
-        [pltpu.VMEM((2, 5, NORB * FRAG, 128), F32), pltpu.VMEM((128, 128), F32)],
+        [pltpu.VMEM((2, 5, NORB * FRAG, 128), F32), pltpu.VMEM((3, 128, 128), F32)],
     )(orbitals.reshape(2, NORB * FRAG, FRAG * FRAG))
     power, weight, ends = call(
         scan_powers,
-        (shape(5, KZ, NY), shape(5, KZ, NY), shape(2, KZ, NY)),
+        (shape(3, KZ, NY), shape(2, KZ, NY), shape(4, KZ, NY)),
         smem=(0,),
         count=3,
     )(row_place.reshape(1).astype(jnp.int32), ey, ez)
 
-    tiles = call(forward_z, shape(NPY, KZ, ROWS * COLS), count=3)(density, *sine_z)
+    tiles = call(
+        forward_z,
+        shape(NPY, KZ, ROWS * COLS),
+        [
+            pltpu.VMEM((ROWS, COLS, NZ), F32),
+            pltpu.VMEM((NZ, NZ), BF16),
+            pltpu.VMEM((NZ, NZ), BF16),
+            pltpu.SemaphoreType.DMA((3,)),
+        ],
+        count=3,
+        space=ANYWHERE,
+    )(density, *sine_z)
     tiles = lax.all_to_all(tiles, "py", split_axis=0, concat_axis=0, tiled=True)
     field, totals = call(
         forward_y,
@@ -546,7 +606,7 @@
     )(tiles, *sine_y, ey, ez)
 
     right, left = jnp.zeros((KZ, NY), F32), jnp.zeros((KZ, NY), F32)
-    for bit in range(5):
+    for bit in range(2):
         pairs = [(p * NPY + q, (p ^ (1 << bit)) * NPY + q) for p in range(NPX) for q in range(NPY)]
         got = lax.ppermute(totals, ALL, pairs)
         upper = (row_place >> bit) % 2 == 1
@@ -554,10 +614,18 @@
         right = right + jnp.where(upper, weight[bit] * got[:KZ], 0.0)
         left = left + jnp.where(upper, 0.0, weight[bit] * got[KZ:])
         totals = jnp.concatenate([high[:KZ] + power[bit] * low[:KZ], low[KZ:] + power[bit] * high[KZ:]])
-    states = jnp.concatenate([right, left])
-
-    tiles = call(back_y, shape(NPY, KZ, ROWS * COLS), [pltpu.VMEM((ROWS * KZ, NY), F32)], count=8)(
-        field, totals, states, ends, *sine_y, ey, ez
+    totals = lax.all_to_all(
+        jnp.broadcast_to(totals, (NPX // 4, 2 * KZ, NY)), "px_0", split_axis=0, concat_axis=0, tiled=True
+    )
+
+    tiles = call(
+        back_y,
+        shape(NPY, KZ, ROWS * COLS),
+        [pltpu.VMEM((ROWS * KZ, NY), F32)],
+        smem=(0,),
+        count=11,
+    )(
+        (row_place // 4).reshape(1).astype(jnp.int32), field, totals, right, left, power, ends, *sine_y, ey, ez
     )
     tiles = lax.all_to_all(tiles, "py", split_axis=0, concat_axis=0, tiled=True)
     hartree_field, *pieces = call(
@@ -573,7 +641,7 @@
         [shape(FRAG, 9, 8, 128), shape(8, 128)] + [shape(n, FRAG, 128) for n in (8, 8, 4)],
         [
             pltpu.VMEM((2, 40 * FRAG, 128), F32),
-            pltpu.VMEM((128, 128), F32),
+            pltpu.VMEM((3, 128, 128), F32),
             pltpu.VMEM((27, 8, 128), F32),
             pltpu.VMEM((FRAG, 9, 8, 128), F32),
             pltpu.VMEM((FRAG, 9, 8, 128), F32),
@@ -589,7 +657,7 @@
     filtered = call(
         orbitals_out,
         shape(2, NORB * FRAG, FRAG * FRAG),
-        [pltpu.VMEM((2, 5, NORB * FRAG, 128), F32), pltpu.VMEM((128, 128), F32)],
+        [pltpu.VMEM((2, 5, NORB * FRAG, 128), F32), pltpu.VMEM((3, 128, 128), F32)],
         count=2,
     )(planes, scale)
     new_density = call(

time: 190 us -> 174 us (0.916)
  the two profiles are of different devices: /device:TPU:39 before, /device:TPU:75 now
where the time goes in v1:
time: 174 us
  starting transfers between devices  92.8 us (53%)
  waiting for transfers between devices  48.2 us (28%)
  Pallas kernels  26.1 us (15%)
  local copies, waits for them, and re-layouts  5.34 us (3%)
    ppermute x13, starting transfers between devices, moved(): return lax.ppermute(x, ALL, pairs)  58.9 us
    ppermute x13, waiting for transfers between devices, moved(): return lax.ppermute(x, ALL, pairs)  19.9 us
    all_to_all x2, starting transfers between devices, body(): tiles = lax.all_to_all(tiles, 'py', split_axis=0, concat_axis=0, tiled=True)  14.4 us
    all_to_all x1, waiting for transfers between devices, body(): lax.all_to_all(jnp.broadcast_to(totals, (NPX // 4, 2 * KZ, NY)), 'px_0',...  12.7 us
    ppermute x2, starting transfers between devices, body(): got = lax.ppermute(totals, ALL, pairs)  12.5 us
    all_to_all x2, waiting for transfers between devices, body(): tiles = lax.all_to_all(tiles, 'py', split_axis=0, concat_axis=0, tiled=True)  11.3 us
    pallas_call x1, Pallas kernels, body(): call(filter_fragments, [shape(FRAG, 9, 8, 128), shape(8, 128)] + [shape(n...  10.6 us
    all_to_all x1, starting transfers between devices, body(): lax.all_to_all(jnp.broadcast_to(totals, (NPX // 4, 2 * KZ, NY)), 'px_0',...  6.98 us
  transfers between devices with their start and end apart: 18, of which 9 were waited for; matrix products, arithmetic and copies ran while one was open for 1% of the time, Pallas kernels for 3%

profile of v1, /device:TPU:75, one launch (start us, length us, event | category | flops | bytes accessed | tf_op | source)
XLA Modules:
  0.0 173.7 jit_solution(3225022060676260694)
XLA Ops:
  0.6 0.0 copy-start.4
  0.6 0.9 copy-done.4
  1.5 0.9 copy-done.6
  2.4 1.0 copy-done.8
  3.5 1.6 shard_map.139
  5.1 0.0 copy-start
  5.1 0.0 copy-start.1
  5.1 8.9 %all-to-all-start = ((f32[16,16,512]{2,1,0:T(8,128)}), f32[16,16,512]{2,1,0:T(8,128)S(1)}, u32[]{:S(2)}, u32[]{:S(2)}) async-start(f32[16,16,512]{2,1,0:T(8,128)} %shard_map.139), calls=%async_computation | async-start | bytes 1048576 | tf_op jit(solution)/shard_map/all_to_all | solution.py:600
  14.1 0.7 constant_dynamic-slice_fusion.ez.rest_3_
  14.8 11.3 %all-to-all-done.tiles = f32[16,16,512]{2,1,0:T(8,128)S(1)} async-done(((f32[16,16,512]{2,1,0:T(8,128)}), f32[16,16,512]{2,1,0:T(8,128)S(1)}, u32[]{:S(2)}, u32[]{:S(2)}) %all-to-all-start) | async-done | bytes 524320 | tf_op jit(solution)/shard_map/all_to_all | solution.py:600
  26.1 0.0 copy-done
  26.1 0.0 copy-done.1
  26.1 0.9 shard_map.140
  27.0 4.6 %collective-permute-start.3 = (f32[32,512]{1,0:T(8,128)S(1)}, f32[32,512]{1,0:T(8,128)S(1)}, u32[]{:S(2)}, u32[]{:S(2)}) collective-permute-start(f32[32,512]{1,0:T(8,128)S(1)} %get-tuple-element.21), channel_id=1, source_target_pairs={{0,16},{1,17},{2,18},{3,19},{4,20},{5,21},{6,22},{7,23},{8,24},{9,... | collective-permute-start | bytes 196616 | tf_op jit(solution)/shard_map/ppermute | solution.py:611
  31.6 0.1 shard_map.141
  31.8 0.7 collective-permute-done.3
  32.5 7.9 %collective-permute-start.4 = (f32[32,512]{1,0:T(8,128)S(1)}, f32[32,512]{1,0:T(8,128)S(1)}, u32[]{:S(2)}, u32[]{:S(2)}) collective-permute-start(f32[32,512]{1,0:T(8,128)S(1)} %pad_maximum_fusion), channel_id=1, source_target_pairs={{0,32},{1,33},{2,34},{3,35},{4,36},{5,37},{6,38},{7,39},{8,40},{9,... | collective-permute-start | bytes 196616 | tf_op jit(solution)/shard_map/ppermute | solution.py:611
  40.5 3.5 %collective-permute-done.4 = f32[32,512]{1,0:T(8,128)S(1)} collective-permute-done((f32[32,512]{1,0:T(8,128)S(1)}, f32[32,512]{1,0:T(8,128)S(1)}, u32[]{:S(2)}, u32[]{:S(2)}) %collective-permute-start.4) | collective-permute-done | bytes 65568 | tf_op jit(solution)/shard_map/ppermute | solution.py:611
  44.1 0.9 broadcast_in_dim.12
  44.9 7.0 %all-to-all-start.1 = ((f32[8,32,512]{2,1,0:T(8,128)}), f32[8,32,512]{2,1,0:T(8,128)S(1)}, u32[]{:S(2)}, u32[]{:S(2)}) async-start(f32[8,32,512]{2,1,0:T(8,128)} %broadcast_in_dim.12), calls=%async_computation.1 | async-start | bytes 1048576 | tf_op jit(solution)/shard_map/all_to_all | solution.py:617
  51.9 12.7 %all-to-all-done.1.totals = f32[8,32,512]{2,1,0:T(8,128)S(1)} async-done(((f32[8,32,512]{2,1,0:T(8,128)}), f32[8,32,512]{2,1,0:T(8,128)S(1)}, u32[]{:S(2)}, u32[]{:S(2)}) %all-to-all-start.1) | async-done | bytes 524320 | tf_op jit(solution)/shard_map/all_to_all | solution.py:617
  64.6 2.0 %shard_map.142 = f32[16,16,512]{2,1,0:T(8,128)} custom-call(s32[1]{0:T(128)} %bitcast.7.place, f32[256,512]{1,0:T(8,128)S(1)} %get-tuple-element.20.field, f32[8,32,512]{2,1,0:T(8,128)S(1)} %all-to-all-done.1.totals, f32[16,512]{1,0:T(8,128)S(1)} %get-tuple-element.42.right, f32[16,512]{1,0:T(8,128)S(1)} %get-tuple-element.41.left, ...), custom_call_target="tpu_custom_call" | custom-call | tf_op jit(solution)/shard_map/pallas_call | solution.py:621
  66.6 5.5 %all-to-all-start.2 = ((f32[16,16,512]{2,1,0:T(8,128)}), f32[16,16,512]{2,1,0:T(8,128)S(1)}, u32[]{:S(2)}, u32[]{:S(2)}) async-start(f32[16,16,512]{2,1,0:T(8,128)} %shard_map.142), calls=%async_computation.2 | async-start | bytes 1048576 | tf_op jit(solution)/shard_map/all_to_all | solution.py:630
  72.1 0.1 pad_add_fusion.2
  72.2 0.6 copy-done.10
  72.8 0.1 reshape.25
  72.8 11.0 %collective-permute-start = (s32[8]{0:T(128)S(1)}, s32[8]{0:T(128)S(1)}, u32[]{:S(2)}, u32[]{:S(2)}) collective-permute-start(s32[8]{0:T(128)S(1)} %get-tuple-element.50), channel_id=1, source_target_pairs={{0,16},{1,17},{2,18},{3,19},{4,20},{5,21},{6,22},{7,23},{8,24},{9,... | collective-permute-start | bytes 104 | tf_op jit(solution)/shard_map/ppermute | solution.py:558
  83.9 1.9 %collective-permute-start.1 = (s32[8]{0:T(128)S(1)}, s32[8]{0:T(128)S(1)}, u32[]{:S(2)}, u32[]{:S(2)}) collective-permute-start(s32[8]{0:T(128)S(1)} %get-tuple-element.50), channel_id=1, source_target_pairs={{0,32},{1,33},{2,34},{3,35},{4,36},{5,37},{6,38},{7,39},{8,40},{9,... | collective-permute-start | bytes 104 | tf_op jit(solution)/shard_map/ppermute | solution.py:558
  85.8 0.0 collective-permute-done
  85.8 7.2 %collective-permute-done.1 = s32[8]{0:T(128)S(1)} collective-permute-done((s32[8]{0:T(128)S(1)}, s32[8]{0:T(128)S(1)}, u32[]{:S(2)}, u32[]{:S(2)}) %collective-permute-start.1) | collective-permute-done | bytes 64 | tf_op jit(solution)/shard_map/ppermute | solution.py:558
  93.0 3.1 %collective-permute-start.2 = (s32[3,8]{1,0:T(4,128)S(1)}, s32[3,8]{1,0:T(4,128)S(1)}, u32[]{:S(2)}, u32[]{:S(2)}) collective-permute-start(s32[3,8]{1,0:T(4,128)S(1)} %get-tuple-element.48), channel_id=1, source_target_pairs={{0,1},{1,2},{2,3},{3,4},{4,5},{5,6},{6,7},{7,8},{8,9},{9,10},{10,1... | collective-permute-start | bytes 296 | tf_op jit(solution)/shard_map/ppermute | solution.py:558
  96.1 0.1 slice_reduce_fusion
  96.2 1.1 collective-permute-done.2
  97.3 0.1 reshape.26.places
  97.4 0.0 all-to-all-done.2.tiles
  97.4 2.8 %shard_map.143 = (f32[16,32,256]{2,1,0:T(8,128)}, f32[8,24,128]{2,1,0:T(8,128)S(1)}, f32[8,24,128]{2,1,0:T(8,128)S(1)}, f32[8,24,128]{2,1,0:T(8,128)S(1)}, f32[8...) custom-call(s32[36]{0:T(128)S(1)} %reshape.26.places, ...), custom_call_target="tpu_custom_call" | custom-call | tf_op jit(solution)/shard_map/pallas_call | solution.py:631
  100.3 2.4 %collective-permute-start.8 = (f32[4,24,128]{2,1,0:T(8,128)S(1)}, f32[4,24,128]{2,1,0:T(8,128)S(1)}, u32[]{:S(2)}, u32[]{:S(2)}) collective-permute-start(f32[4,24,128]{2,1,0:T(8,128)S(1)} %get-tuple-element.30), channel_id=1, source_target_pairs={{32,0},{33,1},{34,2},{35,3},{36,4},{37,5},{38,6},{39,7},{40,8},{41... | collective-permute-start | bytes 147464 | tf_op jit(solution)/shard_map/ppermute | solution.py:558
  102.7 3.7 %collective-permute-start.9 = (f32[4,24,128]{2,1,0:T(8,128)S(1)}, f32[4,24,128]{2,1,0:T(8,128)S(1)}, u32[]{:S(2)}, u32[]{:S(2)}) collective-permute-start(f32[4,24,128]{2,1,0:T(8,128)S(1)} %get-tuple-element.31), channel_id=1, source_target_pairs={{33,0},{34,1},{35,2},{36,3},{37,4},{38,5},{39,6},{40,7},{41,8},{42... | collective-permute-start | bytes 147464 | tf_op jit(solution)/shard_map/ppermute | solution.py:558
  106.4 3.1 %collective-permute-start.5 = (f32[8,24,128]{2,1,0:T(8,128)S(1)}, f32[8,24,128]{2,1,0:T(8,128)S(1)}, u32[]{:S(2)}, u32[]{:S(2)}) collective-permute-start(f32[8,24,128]{2,1,0:T(8,128)S(1)} %get-tuple-element.27), channel_id=1, source_target_pairs={{1,0},{2,1},{3,2},{4,3},{5,4},{6,5},{7,6},{8,7},{9,8},{10,9},{11,1... | collective-permute-start | bytes 294920 | tf_op jit(solution)/shard_map/ppermute | solution.py:558
  109.5 0.0 copy-start.11
  109.5 0.0 copy-start.12
  109.5 4.4 %collective-permute-start.6 = (f32[8,24,128]{2,1,0:T(8,128)S(1)}, f32[8,24,128]{2,1,0:T(8,128)S(1)}, u32[]{:S(2)}, u32[]{:S(2)}) collective-permute-start(f32[8,24,128]{2,1,0:T(8,128)S(1)} %get-tuple-element.28), channel_id=1, source_target_pairs={{16,0},{17,1},{18,2},{19,3},{20,4},{21,5},{22,6},{23,7},{24,8},{25... | collective-permute-start | bytes 294920 | tf_op jit(solution)/shard_map/ppermute | solution.py:558
  113.9 2.1 %collective-permute-start.7 = (f32[8,24,128]{2,1,0:T(8,128)S(1)}, f32[8,24,128]{2,1,0:T(8,128)S(1)}, u32[]{:S(2)}, u32[]{:S(2)}) collective-permute-start(f32[8,24,128]{2,1,0:T(8,128)S(1)} %get-tuple-element.29), channel_id=1, source_target_pairs={{17,0},{18,1},{19,2},{20,3},{21,4},{22,5},{23,6},{24,7},{25,8},{26... | collective-permute-start | bytes 294920 | tf_op jit(solution)/shard_map/ppermute | solution.py:558
  116.0 0.1 pad_add_fusion.3.meta
  116.1 0.0 copy-done.2
  116.1 2.0 %shard_map.144.refs_6_ = f32[24,9,8,128]{3,2,1,0:T(8,128)S(1)} custom-call(f32[2,192,576]{2,1,0:T(8,128)S(1)} %bitcast.25), custom_call_target="tpu_custom_call" | custom-call | tf_op jit(solution)/shard_map/pallas_call | solution.py:576
  118.2 0.0 collective-permute-done.8.refs_4_
  118.2 0.0 collective-permute-done.9.refs_5_
  118.2 0.0 collective-permute-done.5.refs_1_
  118.2 2.9 %collective-permute-done.6.refs_2_ = f32[8,24,128]{2,1,0:T(8,128)S(1)} collective-permute-done((f32[8,24,128]{2,1,0:T(8,128)S(1)}, f32[8,24,128]{2,1,0:T(8,128)S(1)}, u32[]{:S(2)}, u32[]{:S(2)}) %collective-permute-start.6) | collective-permute-done | bytes 98336 | tf_op jit(solution)/shard_map/ppermute | solution.py:558
  121.1 3.9 %collective-permute-done.7.refs_3_ = f32[8,24,128]{2,1,0:T(8,128)S(1)} collective-permute-done((f32[8,24,128]{2,1,0:T(8,128)S(1)}, f32[8,24,128]{2,1,0:T(8,128)S(1)}, u32[]{:S(2)}, u32[]{:S(2)}) %collective-permute-start.7) | collective-permute-done | bytes 98336 | tf_op jit(solution)/shard_map/ppermute | solution.py:558
  125.0 10.6 %shard_map.145 = (f32[24,9,8,128]{3,2,1,0:T(8,128)S(1)}, f32[8,128]{1,0:T(8,128)S(1)}, f32[8,24,128]{2,1,0:T(8,128)S(1)}, f32[8,24,128]{2,1,0:T(8,128)S(1)}, f32[4,24,128]{2,1,0:T(8,128)S(1)}) custom-call(s32[8]{0:T(128)S(1)} %pad_add_fusion.3.meta, f32[8,24,128]{2,1,0:T(8,128)S(1)} %get-tuple-element.26.refs_0_, ...), custom_call_target="tpu_custom_call" | custom-call | tf_op jit(solution)/shard_map/pallas_call | solution.py:639
  135.7 8.4 %collective-permute-start.10 = (f32[8,24,128]{2,1,0:T(8,128)S(1)}, f32[8,24,128]{2,1,0:T(8,128)S(1)}, u32[]{:S(2)}, u32[]{:S(2)}) collective-permute-start(f32[8,24,128]{2,1,0:T(8,128)S(1)} %get-tuple-element.34.refs_0_), channel_id=1, source_target_pairs={{0,1},{1,2},{2,3},{3,4},{4,5},{5,6},{6,7},{7,8},{8,9},{9,10},{10,1... | collective-permute-start | bytes 294920 | tf_op jit(solution)/shard_map/ppermute | solution.py:558
  144.1 3.0 %collective-permute-start.12 = (f32[8,24,128]{2,1,0:T(8,128)S(1)}, f32[8,24,128]{2,1,0:T(8,128)S(1)}, u32[]{:S(2)}, u32[]{:S(2)}) collective-permute-start(f32[8,24,128]{2,1,0:T(8,128)S(1)} %get-tuple-element.35), channel_id=1, source_target_pairs={{0,17},{1,18},{2,19},{3,20},{4,21},{5,22},{6,23},{7,24},{8,25},{9,... | collective-permute-start | bytes 294920 | tf_op jit(solution)/shard_map/ppermute | solution.py:558
  147.1 4.9 %collective-permute-start.11 = (f32[8,24,128]{2,1,0:T(8,128)S(1)}, f32[8,24,128]{2,1,0:T(8,128)S(1)}, u32[]{:S(2)}, u32[]{:S(2)}) collective-permute-start(f32[8,24,128]{2,1,0:T(8,128)S(1)} %get-tuple-element.35), channel_id=1, source_target_pairs={{0,16},{1,17},{2,18},{3,19},{4,20},{5,21},{6,22},{7,23},{8,24},{9,... | collective-permute-start | bytes 294920 | tf_op jit(solution)/shard_map/ppermute | solution.py:558
  152.0 9.0 %collective-permute-start.14 = (f32[4,24,128]{2,1,0:T(8,128)S(1)}, f32[4,24,128]{2,1,0:T(8,128)S(1)}, u32[]{:S(2)}, u32[]{:S(2)}) collective-permute-start(f32[4,24,128]{2,1,0:T(8,128)S(1)} %get-tuple-element.36), channel_id=1, source_target_pairs={{0,33},{1,34},{2,35},{3,36},{4,37},{5,38},{6,39},{7,40},{8,41},{9,... | collective-permute-start | bytes 147464 | tf_op jit(solution)/shard_map/ppermute | solution.py:558
  161.0 1.9 %collective-permute-start.13 = (f32[4,24,128]{2,1,0:T(8,128)S(1)}, f32[4,24,128]{2,1,0:T(8,128)S(1)}, u32[]{:S(2)}, u32[]{:S(2)}) collective-permute-start(f32[4,24,128]{2,1,0:T(8,128)S(1)} %get-tuple-element.36), channel_id=1, source_target_pairs={{0,32},{1,33},{2,34},{3,35},{4,36},{5,37},{6,38},{7,39},{8,40},{9,... | collective-permute-start | bytes 147464 | tf_op jit(solution)/shard_map/ppermute | solution.py:558
  162.9 2.9 %shard_map.146 = f32[2,192,576]{2,1,0:T(8,128)} custom-call(f32[24,9,8,128]{3,2,1,0:T(8,128)S(1)} %get-tuple-element.32.planes, f32[8,128]{1,0:T(8,128)S(1)} %get-tuple-element.33.scale), custom_call_target="tpu_custom_call" | custom-call | tf_op jit(solution)/shard_map/pallas_call | solution.py:657
  165.8 0.0 collective-permute-done.14.refs_5_
  165.8 4.8 %collective-permute-done.13.refs_4_ = f32[4,24,128]{2,1,0:T(8,128)S(1)} collective-permute-done((f32[4,24,128]{2,1,0:T(8,128)S(1)}, f32[4,24,128]{2,1,0:T(8,128)S(1)}, u32[]{:S(2)}, u32[]{:S(2)}) %collective-permute-start.13) | collective-permute-done | bytes 49184 | tf_op jit(solution)/shard_map/ppermute | solution.py:558
  170.6 0.0 collective-permute-done.10.refs_1_
  170.6 0.0 collective-permute-done.12.refs_3_
  170.6 0.0 collective-permute-done.11.refs_2_
  170.6 3.1 %shard_map.147 = f32[16,32,256]{2,1,0:T(8,128)} custom-call(s32[36]{0:T(128)S(1)} %reshape.26.places, f32[8,24,128]{2,1,0:T(8,128)S(1)} %get-tuple-element.34.refs_0_, f32[8,24,128]{2,1,0:T(8,128)S(1)} %collective-permute-done.10.refs_1_, f32[8,24,128]{2,1,0:T(8,128)S(1)} %collective-permute-done.11.refs_2_, ...), custom_call_target="tpu_custom_call" | custom-call | tf_op jit(solution)/shard_map/pallas_call | solution.py:663
  (26 shorter events, 0.1 us)
Async XLA Ops:
  0.6 0.9 copy-start.4
  1.5 0.9 copy-start.6
  2.4 1.0 copy-start.8
  5.1 21.0 %copy-start = (bf16[512,512]{1,0:T(8,128)(2,1)S(1)}, bf16[512,512]{1,0:T(8,128)(2,1)}, u32[]{:S(2)}) copy-start(bf16[512,512]{1,0:T(8,128)(2,1)} %constant.75.clone.table_low.rest_1_) | copy-start | bytes 1572868
  5.1 21.0 %copy-start.1 = (bf16[512,512]{1,0:T(8,128)(2,1)S(1)}, bf16[512,512]{1,0:T(8,128)(2,1)}, u32[]{:S(2)}) copy-start(bf16[512,512]{1,0:T(8,128)(2,1)} %constant.74.clone.table_high.rest_0_) | copy-start | bytes 1572868
  5.1 21.0 %all-to-all-start = ((f32[16,16,512]{2,1,0:T(8,128)}), f32[16,16,512]{2,1,0:T(8,128)S(1)}, u32[]{:S(2)}, u32[]{:S(2)}) async-start(f32[16,16,512]{2,1,0:T(8,128)} %shard_map.139), calls=%async_computation | async-start | bytes 1048576 | tf_op jit(solution)/shard_map/all_to_all | solution.py:600
  14.1 12.1 %copy-start.9 = (f32[1,512]{1,0:T(1,128)S(1)}, f32[1,512]{1,0:T(1,128)}, u32[]{:S(2)}) copy-start(f32[1,512]{1,0:T(1,128)} %constant.78.clone.ey.rest_2_) | copy-start | bytes 6148
  27.0 5.5 %collective-permute-start.3 = (f32[32,512]{1,0:T(8,128)S(1)}, f32[32,512]{1,0:T(8,128)S(1)}, u32[]{:S(2)}, u32[]{:S(2)}) collective-permute-start(f32[32,512]{1,0:T(8,128)S(1)} %get-tuple-element.21), channel_id=1, source_target_pairs={{0,16},{1,17},{2,18},{3,19},{4,20},{5,21},{6,22},{7,23},{8,24},{9,... | collective-permute-start | bytes 196616 | tf_op jit(solution)/shard_map/ppermute | solution.py:611
  32.5 11.5 %collective-permute-start.4 = (f32[32,512]{1,0:T(8,128)S(1)}, f32[32,512]{1,0:T(8,128)S(1)}, u32[]{:S(2)}, u32[]{:S(2)}) collective-permute-start(f32[32,512]{1,0:T(8,128)S(1)} %pad_maximum_fusion), channel_id=1, source_target_pairs={{0,32},{1,33},{2,34},{3,35},{4,36},{5,37},{6,38},{7,39},{8,40},{9,... | collective-permute-start | bytes 196616 | tf_op jit(solution)/shard_map/ppermute | solution.py:611
  44.9 19.7 %all-to-all-start.1 = ((f32[8,32,512]{2,1,0:T(8,128)}), f32[8,32,512]{2,1,0:T(8,128)S(1)}, u32[]{:S(2)}, u32[]{:S(2)}) async-start(f32[8,32,512]{2,1,0:T(8,128)} %broadcast_in_dim.12), calls=%async_computation.1 | async-start | bytes 1048576 | tf_op jit(solution)/shard_map/all_to_all | solution.py:617
  64.6 32.8 %copy-start.3 = (f32[16,32,256]{2,1,0:T(8,128)S(1)}, f32[16,32,256]{2,1,0:T(8,128)}, u32[]{:S(2)}) copy-start(f32[16,32,256]{2,1,0:T(8,128)} %external.1) | copy-start | bytes 1572868
  64.6 32.8 %copy-start.5 = (bf16[256,256]{1,0:T(8,128)(2,1)S(1)}, bf16[256,256]{1,0:T(8,128)(2,1)}, u32[]{:S(2)}) copy-start(bf16[256,256]{1,0:T(8,128)(2,1)} %constant.77.clone.table_low) | copy-start | bytes 393220
  64.6 32.8 %copy-start.7 = (bf16[256,256]{1,0:T(8,128)(2,1)S(1)}, bf16[256,256]{1,0:T(8,128)(2,1)}, u32[]{:S(2)}) copy-start(bf16[256,256]{1,0:T(8,128)(2,1)} %constant.76.clone.table_high) | copy-start | bytes 393220
  66.6 49.5 %copy-start.2 = (f32[2,8,24,576]{3,2,1,0:T(8,128)S(1)}, f32[2,8,24,576]{3,2,1,0:T(8,128)}, u32[]{:S(2)}) copy-start(f32[2,8,24,576]{3,2,1,0:T(8,128)} %param.14) | copy-start | bytes 2654212
  66.6 30.8 %all-to-all-start.2 = ((f32[16,16,512]{2,1,0:T(8,128)}), f32[16,16,512]{2,1,0:T(8,128)S(1)}, u32[]{:S(2)}, u32[]{:S(2)}) async-start(f32[16,16,512]{2,1,0:T(8,128)} %shard_map.142), calls=%async_computation.2 | async-start | bytes 1048576 | tf_op jit(solution)/shard_map/all_to_all | solution.py:630
  72.1 0.7 copy-start.10
  72.8 12.9 %collective-permute-start = (s32[8]{0:T(128)S(1)}, s32[8]{0:T(128)S(1)}, u32[]{:S(2)}, u32[]{:S(2)}) collective-permute-start(s32[8]{0:T(128)S(1)} %get-tuple-element.50), channel_id=1, source_target_pairs={{0,16},{1,17},{2,18},{3,19},{4,20},{5,21},{6,22},{7,23},{8,24},{9,... | collective-permute-start | bytes 104 | tf_op jit(solution)/shard_map/ppermute | solution.py:558
  83.9 9.1 %collective-permute-start.1 = (s32[8]{0:T(128)S(1)}, s32[8]{0:T(128)S(1)}, u32[]{:S(2)}, u32[]{:S(2)}) collective-permute-start(s32[8]{0:T(128)S(1)} %get-tuple-element.50), channel_id=1, source_target_pairs={{0,32},{1,33},{2,34},{3,35},{4,36},{5,37},{6,38},{7,39},{8,40},{9,... | collective-permute-start | bytes 104 | tf_op jit(solution)/shard_map/ppermute | solution.py:558
  93.0 4.3 %collective-permute-start.2 = (s32[3,8]{1,0:T(4,128)S(1)}, s32[3,8]{1,0:T(4,128)S(1)}, u32[]{:S(2)}, u32[]{:S(2)}) collective-permute-start(s32[3,8]{1,0:T(4,128)S(1)} %get-tuple-element.48), channel_id=1, source_target_pairs={{0,1},{1,2},{2,3},{3,4},{4,5},{5,6},{6,7},{7,8},{8,9},{9,10},{10,1... | collective-permute-start | bytes 296 | tf_op jit(solution)/shard_map/ppermute | solution.py:558
  100.3 17.9 %collective-permute-start.8 = (f32[4,24,128]{2,1,0:T(8,128)S(1)}, f32[4,24,128]{2,1,0:T(8,128)S(1)}, u32[]{:S(2)}, u32[]{:S(2)}) collective-permute-start(f32[4,24,128]{2,1,0:T(8,128)S(1)} %get-tuple-element.30), channel_id=1, source_target_pairs={{32,0},{33,1},{34,2},{35,3},{36,4},{37,5},{38,6},{39,7},{40,8},{41... | collective-permute-start | bytes 147464 | tf_op jit(solution)/shard_map/ppermute | solution.py:558
  102.7 15.5 %collective-permute-start.9 = (f32[4,24,128]{2,1,0:T(8,128)S(1)}, f32[4,24,128]{2,1,0:T(8,128)S(1)}, u32[]{:S(2)}, u32[]{:S(2)}) collective-permute-start(f32[4,24,128]{2,1,0:T(8,128)S(1)} %get-tuple-element.31), channel_id=1, source_target_pairs={{33,0},{34,1},{35,2},{36,3},{37,4},{38,5},{39,6},{40,7},{41,8},{42... | collective-permute-start | bytes 147464 | tf_op jit(solution)/shard_map/ppermute | solution.py:558
  106.4 11.8 %collective-permute-start.5 = (f32[8,24,128]{2,1,0:T(8,128)S(1)}, f32[8,24,128]{2,1,0:T(8,128)S(1)}, u32[]{:S(2)}, u32[]{:S(2)}) collective-permute-start(f32[8,24,128]{2,1,0:T(8,128)S(1)} %get-tuple-element.27), channel_id=1, source_target_pairs={{1,0},{2,1},{3,2},{4,3},{5,4},{6,5},{7,6},{8,7},{9,8},{10,9},{11,1... | collective-permute-start | bytes 294920 | tf_op jit(solution)/shard_map/ppermute | solution.py:558
  109.5 6.6 %copy-start.11 = (s32[2]{0:T(128)S(1)}, s32[2]{0:T(128)}, u32[]{:S(2)}) copy-start(s32[2]{0:T(128)} %param.16) | copy-start | bytes 28
  109.5 6.5 %copy-start.12 = (s32[2]{0:T(128)S(1)}, s32[2]{0:T(128)}, u32[]{:S(2)}) copy-start(s32[2]{0:T(128)} %param.17) | copy-start | bytes 28
  109.5 11.6 %collective-permute-start.6 = (f32[8,24,128]{2,1,0:T(8,128)S(1)}, f32[8,24,128]{2,1,0:T(8,128)S(1)}, u32[]{:S(2)}, u32[]{:S(2)}) collective-permute-start(f32[8,24,128]{2,1,0:T(8,128)S(1)} %get-tuple-element.28), channel_id=1, source_target_pairs={{16,0},{17,1},{18,2},{19,3},{20,4},{21,5},{22,6},{23,7},{24,8},{25... | collective-permute-start | bytes 294920 | tf_op jit(solution)/shard_map/ppermute | solution.py:558
  113.9 11.1 %collective-permute-start.7 = (f32[8,24,128]{2,1,0:T(8,128)S(1)}, f32[8,24,128]{2,1,0:T(8,128)S(1)}, u32[]{:S(2)}, u32[]{:S(2)}) collective-permute-start(f32[8,24,128]{2,1,0:T(8,128)S(1)} %get-tuple-element.29), channel_id=1, source_target_pairs={{17,0},{18,1},{19,2},{20,3},{21,4},{22,5},{23,6},{24,7},{25,8},{26... | collective-permute-start | bytes 294920 | tf_op jit(solution)/shard_map/ppermute | solution.py:558
  135.7 34.9 %collective-permute-start.10 = (f32[8,24,128]{2,1,0:T(8,128)S(1)}, f32[8,24,128]{2,1,0:T(8,128)S(1)}, u32[]{:S(2)}, u32[]{:S(2)}) collective-permute-start(f32[8,24,128]{2,1,0:T(8,128)S(1)} %get-tuple-element.34.refs_0_), channel_id=1, source_target_pairs={{0,1},{1,2},{2,3},{3,4},{4,5},{5,6},{6,7},{7,8},{8,9},{9,10},{10,1... | collective-permute-start | bytes 294920 | tf_op jit(solution)/shard_map/ppermute | solution.py:558
  144.1 26.5 %collective-permute-start.12 = (f32[8,24,128]{2,1,0:T(8,128)S(1)}, f32[8,24,128]{2,1,0:T(8,128)S(1)}, u32[]{:S(2)}, u32[]{:S(2)}) collective-permute-start(f32[8,24,128]{2,1,0:T(8,128)S(1)} %get-tuple-element.35), channel_id=1, source_target_pairs={{0,17},{1,18},{2,19},{3,20},{4,21},{5,22},{6,23},{7,24},{8,25},{9,... | collective-permute-start | bytes 294920 | tf_op jit(solution)/shard_map/ppermute | solution.py:558
  147.1 23.6 %collective-permute-start.11 = (f32[8,24,128]{2,1,0:T(8,128)S(1)}, f32[8,24,128]{2,1,0:T(8,128)S(1)}, u32[]{:S(2)}, u32[]{:S(2)}) collective-permute-start(f32[8,24,128]{2,1,0:T(8,128)S(1)} %get-tuple-element.35), channel_id=1, source_target_pairs={{0,16},{1,17},{2,18},{3,19},{4,20},{5,21},{6,22},{7,23},{8,24},{9,... | collective-permute-start | bytes 294920 | tf_op jit(solution)/shard_map/ppermute | solution.py:558
  152.0 13.8 %collective-permute-start.14 = (f32[4,24,128]{2,1,0:T(8,128)S(1)}, f32[4,24,128]{2,1,0:T(8,128)S(1)}, u32[]{:S(2)}, u32[]{:S(2)}) collective-permute-start(f32[4,24,128]{2,1,0:T(8,128)S(1)} %get-tuple-element.36), channel_id=1, source_target_pairs={{0,33},{1,34},{2,35},{3,36},{4,37},{5,38},{6,39},{7,40},{8,41},{9,... | collective-permute-start | bytes 147464 | tf_op jit(solution)/shard_map/ppermute | solution.py:558
  161.0 9.6 %collective-permute-start.13 = (f32[4,24,128]{2,1,0:T(8,128)S(1)}, f32[4,24,128]{2,1,0:T(8,128)S(1)}, u32[]{:S(2)}, u32[]{:S(2)}) collective-permute-start(f32[4,24,128]{2,1,0:T(8,128)S(1)} %get-tuple-element.36), channel_id=1, source_target_pairs={{0,32},{1,33},{2,34},{3,35},{4,36},{5,37},{6,38},{7,39},{8,40},{9,... | collective-permute-start | bytes 147464 | tf_op jit(solution)/shard_map/ppermute | solution.py:558

commit v2 on v1

--- a/solution.py
+++ b/solution.py
@@ -21,7 +21,6 @@
 BF16 = jnp.bfloat16
 VMEM = pl.BlockSpec(memory_space=pltpu.VMEM)
 SMEM = pl.BlockSpec(memory_space=pltpu.SMEM)
-ANYWHERE = pl.BlockSpec(memory_space=pl.ANY)
 
 
 def sine_table(length):
@@ -42,7 +41,7 @@
 
 
 SINE_Y = halves_of(sine_table(NY))
-SINE_Z = halves_of(sine_table(NZ))
+SINE_Z = np.stack(halves_of(sine_table(NZ)))
 EIGEN_Y = eigen_values(NY)[None, :]
 EIGEN_Z = eigen_values(NZ)[:, None]
 
@@ -59,11 +58,11 @@
     return one(left[0], right[0]) + (one(left[0], right[1]) + one(left[1], right[0]))
 
 
-def call(kernel, outs, scratch=(), smem=(), count=1, space=VMEM):
+def call(kernel, outs, scratch=(), smem=(), count=1):
     return pl.pallas_call(
         kernel,
         out_shape=outs,
-        in_specs=[SMEM if k in smem else space for k in range(count)],
+        in_specs=[SMEM if k in smem else VMEM for k in range(count)],
         out_specs=jax.tree.map(lambda _: VMEM, outs),
         scratch_shapes=list(scratch),
         compiler_params=pltpu.CompilerParams(vmem_limit_bytes=48 * 1024 * 1024),
@@ -89,16 +88,9 @@
     return 1.0 / (1.0 + 0.5 * gap + root), 0.5 / root
 
 
-def forward_z(density, table_high, table_low, out, cells, high, low, sems):
-    copies = [
-        pltpu.make_async_copy(source, target, sems.at[k])
-        for k, (source, target) in enumerate(((density, cells), (table_high, high), (table_low, low)))
-    ]
-    for one in copies:
-        one.start()
-    for one in copies:
-        one.wait()
-    spectrum = dot3((high[...], low[...]), split2(cells[...].reshape(ROWS * COLS, NZ)), ((1,), (1,)))
+def forward_z(density, table, out):
+    cells = density[...].reshape(ROWS * COLS, NZ)
+    spectrum = dot3((table[0], table[1]), split2(cells), ((1,), (1,)))
     out[...] = spectrum.reshape(NPY, KZ, ROWS * COLS)
 
 
@@ -191,11 +183,11 @@
     return lanes(rows) // 32
 
 
-def back_z(places, tiles, external, table_high, table_low, field_out, *rest):
-    pieces, grid = rest[:6], rest[6]
+def back_z(places, tiles, external, table, field_out, *rest):
+    owned, beside, grid = rest[:3], rest[3], rest[4]
     spectrum = tiles[...].reshape(NZ, ROWS * COLS)
     turned = spectrum.T
-    field = dot3(split2(turned), (table_high[...], table_low[...]), ((1,), (0,)))
+    field = dot3(split2(turned), (table[0], table[1]), ((1,), (0,)))
     field = field.reshape(ROWS, COLS, NZ)
     field_out[...] = field
     potential = field + external[...]
@@ -208,7 +200,7 @@
     for k, (down, along) in enumerate(STEPS):
         groups = 8 if down < 2 else 4
 
-        def cut(number, carry, k=k, along=along, groups=groups):
+        def cut(number, carry, k=k, down=down, along=along, groups=groups):
             totals = []
             for part in range(4):
                 total = None
@@ -222,7 +214,10 @@
                     total = window if total is None else jnp.where(slot_of == slot, window, total)
                 totals.append(total)
             for part in range(4):
-                pieces[k][4 * number + part] = totals[part]
+                if along:
+                    beside[8 * down + 4 * number + part] = totals[part]
+                else:
+                    owned[down][4 * number + part] = totals[part]
             return carry
 
         lax.fori_loop(0, groups // 4, cut, 0)
@@ -330,10 +325,10 @@
 
 
 def filter_fragments(meta, *refs):
-    pieces, start = refs[:6], refs[6]
-    out, scale_out = refs[7:9]
-    shares = refs[9:12]
-    boxes, turned, compact, potential, other, spilled = refs[12:]
+    owned, beside, next_rows, last_rows, start = refs[:5]
+    out, scale_out = refs[5:7]
+    shares = refs[7:10]
+    boxes, turned, compact, potential, other, spilled = refs[10:]
     lane = lanes(8)
     sub = lax.broadcasted_iota(jnp.int32, (8, 128), 0)
     second = (lane // 8) % 2 == 1
@@ -344,7 +339,10 @@
             moved_windows = []
             for part in range(4):
                 group = 4 * number + part
-                both = pieces[2 * down][group] + pieces[2 * down + 1][group]
+                if down == 0:
+                    both = owned[group] + beside[group]
+                else:
+                    both = (next_rows if down == 1 else last_rows)[group]
                 moved_windows.append([rolled(both, -32 * slot) for slot in range(4)])
             for part in range(4):
                 for slot in range(4):
@@ -389,14 +387,16 @@
     inverse = 1.0 / jnp.where(second, half_1, half_0)
     for part in range(3):
         for k in range(9):
-            value = (3.0 + compact[9 * part + k] - centre) * (2.0 * inverse)
+            value = -2.0 * (3.0 + compact[9 * part + k] - centre)
             for x, wide in enumerate(spread(value, lane)):
                 potential[8 * part + x, k] = wide
-    coupling = -inverse
+    odd_scale = -inverse
+    even_scale = inverse * inverse
     degree = jnp.where(second, meta[5], meta[4])
 
-    def apply(source, target, earlier=None, initial=False, step=None):
-        live = None if step is None else step <= degree
+    def apply(source, target, earlier=None, initial=False, even=False, step=None):
+        if step is not None:
+            live, just_done = step <= degree, step == degree + 1
         earlier = target if earlier is None else earlier
 
         def chunk(number, carry):
@@ -426,10 +426,15 @@
                         total = total + here[k + 1]
                     else:
                         total = total + jnp.where(sub < 7, rolled(here[k - 2], -1, 0), 0.0)
-                    image = potential[x, k] * here[k] + coupling * total
-                    following = 0.5 * image if initial else image - earlier[x, k]
-                    if live is not None:
-                        following = jnp.where(live, following, here[k])
+                    following = potential[x, k] * here[k] + total
+                    if initial:
+                        following = 0.5 * following
+                    else:
+                        past = earlier[x, k]
+                        following = even_scale * following - past if even else following - past
+                    if step is not None:
+                        kept = jnp.where(just_done, odd_scale * here[k], past)
+                        following = jnp.where(live, following, kept)
                     target[x, k] = following
                 behind, here = here, ahead
             return tuple(behind + here)
@@ -438,7 +443,7 @@
         lax.fori_loop(0, 3, chunk, tuple(zero + [source[0, k] for k in range(9)]))
 
     apply(start, other, initial=True)
-    apply(other, out, earlier=start)
+    apply(other, out, earlier=start, even=True)
     fewest = jnp.minimum(meta[4], meta[5])
     most = jnp.maximum(meta[4], meta[5])
     plain = (fewest - 2) // 2
@@ -446,12 +451,12 @@
 
     def free_pair(pair, carry):
         apply(out, other)
-        apply(other, out)
+        apply(other, out, even=True)
         return carry
 
     def held_pair(pair, carry):
-        apply(out, other, step=2 * pair + 3)
-        apply(other, out, step=2 * pair + 4)
+        apply(out, other)
+        apply(other, out, even=True, step=2 * pair + 4)
         return carry
 
     lax.fori_loop(0, plain, free_pair, 0)
@@ -513,7 +518,7 @@
 
 
 def patch(places, *refs):
-    shares, out, grid = refs[:6], refs[6], refs[7]
+    shares, beside, out, grid = refs[:3], refs[3], refs[4], refs[5]
 
     def clear(row, carry):
         for half in range(2):
@@ -525,10 +530,11 @@
     for k, (down, along) in enumerate(STEPS):
         groups = 8 if down < 2 else 4
 
-        def add(number, carry, k=k, along=along, groups=groups):
+        def add(number, carry, k=k, down=down, along=along, groups=groups):
             pieces = []
             for part in range(4):
-                both = shares[k][4 * number + part]
+                group = 4 * number + part
+                both = beside[8 * down + group] if along else shares[down][group]
                 for slot in range(4):
                     depth = places[6 * k + 3 * (slot % 2) + 2]
                     pieces.append(pltpu.roll(both, (256 + depth - 32 * slot) & 127, 1))
@@ -565,13 +571,14 @@
     local = (anchors - origin[None, :]).astype(jnp.int32)
     own = jnp.pad(local.reshape(6), (0, 2))
     above = jnp.stack([own, moved(own, 1, 0), moved(own, 2, 0)])
-    places = jnp.stack([above, moved(above, 0, 1)], 1)[:, :, :6].reshape(36)
     meta = jnp.concatenate([local[:, 0], weights, degrees, weights]).astype(jnp.int32)
 
     sine_y = [jnp.asarray(t) for t in SINE_Y]
-    sine_z = [jnp.asarray(t) for t in SINE_Z]
+    sine_z = jnp.asarray(SINE_Z)
     ey = jnp.asarray(EIGEN_Y)
     ez = lax.dynamic_slice(jnp.asarray(EIGEN_Z), (col_place * KZ, 0), (KZ, 1))
+    ez, above = lax.optimization_barrier((ez, above))
+    places = jnp.stack([above, moved(above, 0, 1)], 1)[:, :, :6].reshape(36)
 
     planes = call(
         orbitals_in,
@@ -585,18 +592,7 @@
         count=3,
     )(row_place.reshape(1).astype(jnp.int32), ey, ez)
 
-    tiles = call(
-        forward_z,
-        shape(NPY, KZ, ROWS * COLS),
-        [
-            pltpu.VMEM((ROWS, COLS, NZ), F32),
-            pltpu.VMEM((NZ, NZ), BF16),
-            pltpu.VMEM((NZ, NZ), BF16),
-            pltpu.SemaphoreType.DMA((3,)),
-        ],
-        count=3,
-        space=ANYWHERE,
-    )(density, *sine_z)
+    tiles = call(forward_z, shape(NPY, KZ, ROWS * COLS), count=2)(density, sine_z)
     tiles = lax.all_to_all(tiles, "py", split_axis=0, concat_axis=0, tiled=True)
     field, totals = call(
         forward_y,
@@ -628,17 +624,20 @@
         (row_place // 4).reshape(1).astype(jnp.int32), field, totals, right, left, power, ends, *sine_y, ey, ez
     )
     tiles = lax.all_to_all(tiles, "py", split_axis=0, concat_axis=0, tiled=True)
-    hartree_field, *pieces = call(
+    groups = (8, 8, 4)
+    hartree_field, *owned, beside = call(
         back_z,
-        [shape(ROWS, COLS, NZ)] + [shape(8 if down < 2 else 4, FRAG, 128) for down, _ in STEPS],
+        [shape(ROWS, COLS, NZ)] + [shape(n, FRAG, 128) for n in groups + (20,)],
         [pltpu.VMEM((2, ROWS, PADDED, 128), F32)],
         smem=(0,),
-        count=5,
-    )(places, tiles, external, *sine_z)
-    pieces = [pieces[k] if k == 0 else moved(pieces[k], -STEPS[k][0], -STEPS[k][1]) for k in range(6)]
+        count=4,
+    )(places, tiles, external, sine_z)
+    beside = moved(beside, 0, -1)
+    next_rows = moved(owned[1] + beside[8:16], -1, 0)
+    last_rows = moved(owned[2] + beside[16:], -2, 0)
     planes, scale, *shares = call(
         filter_fragments,
-        [shape(FRAG, 9, 8, 128), shape(8, 128)] + [shape(n, FRAG, 128) for n in (8, 8, 4)],
+        [shape(FRAG, 9, 8, 128), shape(8, 128)] + [shape(n, FRAG, 128) for n in groups],
         [
             pltpu.VMEM((2, 40 * FRAG, 128), F32),
             pltpu.VMEM((3, 128, 128), F32),
@@ -648,12 +647,10 @@
             pltpu.VMEM((2, 40 * FRAG, 128), F32),
         ],
         smem=(0,),
-        count=8,
-    )(meta, *pieces, planes)
-    received = [
-        shares[down] if k == 0 else moved(shares[down], down, along)
-        for k, (down, along) in enumerate(STEPS)
-    ]
+        count=6,
+    )(meta, owned[0], beside, next_rows, last_rows, planes)
+    received = [shares[0], moved(shares[1], 1, 0), moved(shares[2], 2, 0)]
+    beside = moved(jnp.concatenate(received), 0, 1)
     filtered = call(
         orbitals_out,
         shape(2, NORB * FRAG, FRAG * FRAG),
@@ -665,8 +662,8 @@
         shape(ROWS, COLS, NZ),
         [pltpu.VMEM((2, ROWS, PADDED, 128), F32)],
         smem=(0,),
-        count=7,
-    )(places, *received)
+        count=5,
+    )(places, *received, beside)
     return hartree_field, filtered.reshape(orbitals.shape), new_density
 
 

time: 174 us -> 167 us (0.960)
  the two profiles are of different devices: /device:TPU:75 before, /device:TPU:14 now
where the time goes in v2:
time: 167 us; the launch traced here: 166 us
  starting transfers between devices  74.7 us (45%)
  waiting for transfers between devices  55.6 us (33%)
  Pallas kernels  30.5 us (18%)
  local copies, waits for them, and re-layouts  4.47 us (3%)
    ppermute x9, starting transfers between devices, moved(): return lax.ppermute(x, ALL, pairs)  37.8 us
    ppermute x9, waiting for transfers between devices, moved(): return lax.ppermute(x, ALL, pairs)  28.7 us
    all_to_all x2, starting transfers between devices, body(): tiles = lax.all_to_all(tiles, 'py', split_axis=0, concat_axis=0, tiled=True)  18.7 us
    all_to_all x1, waiting for transfers between devices, body(): lax.all_to_all(jnp.broadcast_to(totals, (NPX // 4, 2 * KZ, NY)), 'px_0',...  15.8 us
    pallas_call x1, Pallas kernels, body(): call(filter_fragments, [shape(FRAG, 9, 8, 128), shape(8, 128)] + [shape(n...  15.4 us
    ppermute x2, starting transfers between devices, body(): got = lax.ppermute(totals, ALL, pairs)  10.5 us
    ppermute x2, waiting for transfers between devices, body(): got = lax.ppermute(totals, ALL, pairs)  8.2 us
    all_to_all x1, starting transfers between devices, body(): lax.all_to_all(jnp.broadcast_to(totals, (NPX // 4, 2 * KZ, NY)), 'px_0',...  7.66 us
  transfers between devices with their start and end apart: 14, of which 10 were waited for; matrix products, arithmetic and copies ran while one was open for 1% of the time, Pallas kernels for 3%

profile of v2, /device:TPU:14, one launch (start us, length us, event | category | flops | bytes accessed | tf_op | source)
XLA Modules:
  0.0 166.5 jit_solution(7358375197663053493)
XLA Ops:
  0.6 0.0 copy-start.2
  0.6 0.9 copy-done.2
  1.6 0.0 copy-start.6
  1.6 1.0 copy-done.6
  2.6 1.2 shard_map.130
  3.8 0.0 copy-start
  3.8 0.0 copy-start.1
  3.8 10.4 %all-to-all-start = ((f32[16,16,512]{2,1,0:T(8,128)}), f32[16,16,512]{2,1,0:T(8,128)S(1)}, u32[]{:S(2)}, u32[]{:S(2)}) async-start(f32[16,16,512]{2,1,0:T(8,128)} %shard_map.130), calls=%async_computation | async-start | bytes 1048576 | tf_op jit(solution)/shard_map/all_to_all | solution.py:596
  14.2 0.0 copy-start.8
  14.2 0.1 pad_add_fusion.2
  14.3 0.6 copy-done.8
  14.9 0.1 reshape.25
  15.0 1.9 %collective-permute-start = (s32[8]{0:T(128)S(1)}, s32[8]{0:T(128)S(1)}, u32[]{:S(2)}, u32[]{:S(2)}) collective-permute-start(s32[8]{0:T(128)S(1)} %get-tuple-element.48), channel_id=1, source_target_pairs={{0,16},{1,17},{2,18},{3,19},{4,20},{5,21},{6,22},{7,23},{8,24},{9,... | collective-permute-start | bytes 104 | tf_op jit(solution)/shard_map/ppermute | solution.py:564
  16.9 8.2 %collective-permute-start.1 = (s32[8]{0:T(128)S(1)}, s32[8]{0:T(128)S(1)}, u32[]{:S(2)}, u32[]{:S(2)}) collective-permute-start(s32[8]{0:T(128)S(1)} %get-tuple-element.48), channel_id=1, source_target_pairs={{0,32},{1,33},{2,34},{3,35},{4,36},{5,37},{6,38},{7,39},{8,40},{9,... | collective-permute-start | bytes 104 | tf_op jit(solution)/shard_map/ppermute | solution.py:564
  25.1 0.7 constant_dynamic-slice_fusion.ez.rest_3_
  25.8 0.0 collective-permute-done
  25.8 1.4 collective-permute-done.1
  27.2 0.0 copy-start.7
  27.3 1.2 all-to-all-done.tiles
  28.4 0.0 copy-done
  28.4 0.0 copy-done.1
  28.4 0.0 copy-done.7
  28.4 0.9 shard_map.131
  29.3 6.6 %collective-permute-start.3 = (f32[32,512]{1,0:T(8,128)S(1)}, f32[32,512]{1,0:T(8,128)S(1)}, u32[]{:S(2)}, u32[]{:S(2)}) collective-permute-start(f32[32,512]{1,0:T(8,128)S(1)} %get-tuple-element.23), channel_id=1, source_target_pairs={{0,16},{1,17},{2,18},{3,19},{4,20},{5,21},{6,22},{7,23},{8,24},{9,... | collective-permute-start | bytes 196616 | tf_op jit(solution)/shard_map/ppermute | solution.py:607
  35.9 0.1 shard_map.132
  36.1 0.7 collective-permute-done.3
  36.9 3.9 %collective-permute-start.4 = (f32[32,512]{1,0:T(8,128)S(1)}, f32[32,512]{1,0:T(8,128)S(1)}, u32[]{:S(2)}, u32[]{:S(2)}) collective-permute-start(f32[32,512]{1,0:T(8,128)S(1)} %pad_maximum_fusion.1), channel_id=1, source_target_pairs={{0,32},{1,33},{2,34},{3,35},{4,36},{5,37},{6,38},{7,39},{8,40},{9,... | collective-permute-start | bytes 196616 | tf_op jit(solution)/shard_map/ppermute | solution.py:607
  40.8 7.5 %collective-permute-done.4 = f32[32,512]{1,0:T(8,128)S(1)} collective-permute-done((f32[32,512]{1,0:T(8,128)S(1)}, f32[32,512]{1,0:T(8,128)S(1)}, u32[]{:S(2)}, u32[]{:S(2)}) %collective-permute-start.4) | collective-permute-done | bytes 65568 | tf_op jit(solution)/shard_map/ppermute | solution.py:607
  48.3 0.9 broadcast_in_dim.12
  49.2 7.7 %all-to-all-start.1 = ((f32[8,32,512]{2,1,0:T(8,128)}), f32[8,32,512]{2,1,0:T(8,128)S(1)}, u32[]{:S(2)}, u32[]{:S(2)}) async-start(f32[8,32,512]{2,1,0:T(8,128)} %broadcast_in_dim.12), calls=%async_computation.1 | async-start | bytes 1048576 | tf_op jit(solution)/shard_map/all_to_all | solution.py:613
  56.8 15.8 %all-to-all-done.1.totals = f32[8,32,512]{2,1,0:T(8,128)S(1)} async-done(((f32[8,32,512]{2,1,0:T(8,128)}), f32[8,32,512]{2,1,0:T(8,128)S(1)}, u32[]{:S(2)}, u32[]{:S(2)}) %all-to-all-start.1) | async-done | bytes 524320 | tf_op jit(solution)/shard_map/all_to_all | solution.py:613
  72.7 2.0 %shard_map.133 = f32[16,16,512]{2,1,0:T(8,128)} custom-call(s32[1]{0:T(128)} %bitcast.7.place, f32[256,512]{1,0:T(8,128)S(1)} %get-tuple-element.22.field, f32[8,32,512]{2,1,0:T(8,128)S(1)} %all-to-all-done.1.totals, f32[16,512]{1,0:T(8,128)S(1)} %get-tuple-element.42.right, f32[16,512]{1,0:T(8,128)S(1)} %get-tuple-element.41.left, ...), custom_call_target="tpu_custom_call" | custom-call | tf_op jit(solution)/shard_map/pallas_call | solution.py:617
  74.6 0.0 copy-start.3
  74.6 8.4 %all-to-all-start.2 = ((f32[16,16,512]{2,1,0:T(8,128)}), f32[16,16,512]{2,1,0:T(8,128)S(1)}, u32[]{:S(2)}, u32[]{:S(2)}) async-start(f32[16,16,512]{2,1,0:T(8,128)} %shard_map.133), calls=%async_computation.2 | async-start | bytes 1048576 | tf_op jit(solution)/shard_map/all_to_all | solution.py:626
  83.0 3.5 %collective-permute-start.2 = (s32[3,8]{1,0:T(4,128)S(1)}, s32[3,8]{1,0:T(4,128)S(1)}, u32[]{:S(2)}, u32[]{:S(2)}) collective-permute-start(s32[3,8]{1,0:T(4,128)S(1)} %pad_add_fusion.1), channel_id=1, source_target_pairs={{0,1},{1,2},{2,3},{3,4},{4,5},{5,6},{6,7},{7,8},{8,9},{9,10},{10,1... | collective-permute-start | bytes 296 | tf_op jit(solution)/shard_map/ppermute | solution.py:564
  86.5 7.1 %collective-permute-done.2 = s32[3,8]{1,0:T(4,128)S(1)} collective-permute-done((s32[3,8]{1,0:T(4,128)S(1)}, s32[3,8]{1,0:T(4,128)S(1)}, u32[]{:S(2)}, u32[]{:S(2)}) %collective-permute-start.2) | collective-permute-done | bytes 128 | tf_op jit(solution)/shard_map/ppermute | solution.py:564
  93.7 0.1 reshape.26.places
  93.8 1.8 %all-to-all-done.2.tiles = f32[16,16,512]{2,1,0:T(8,128)S(1)} async-done(((f32[16,16,512]{2,1,0:T(8,128)}), f32[16,16,512]{2,1,0:T(8,128)S(1)}, u32[]{:S(2)}, u32[]{:S(2)}) %all-to-all-start.2) | async-done | bytes 524320 | tf_op jit(solution)/shard_map/all_to_all | solution.py:626
  95.5 0.0 copy-done.3
  95.5 0.0 copy-done.5
  95.5 2.8 %shard_map.134 = (f32[16,32,256]{2,1,0:T(8,128)}, f32[8,24,128]{2,1,0:T(8,128)S(1)}, f32[8,24,128]{2,1,0:T(8,128)S(1)}, f32[4,24,128]{2,1,0:T(8,128)S(1)}, f32[20,24,128]{2,1,0:T(8,128)S(1)}) custom-call(s32[36]{0:T(128)S(1)} %reshape.26.places, f32[16,16,512]{2,1,0:T(8,128)S(1)} %all-to-all-done.2.tiles, f32[16,32,256]{2,1,0:T(8,128)S(1)} %copy-done.5, ...), custom_call_target="tpu_custom_call" | custom-call | tf_op jit(solution)/shard_map/pallas_call | solution.py:628
  98.4 3.4 %collective-permute-start.5 = (f32[20,24,128]{2,1,0:T(8,128)S(1)}, f32[20,24,128]{2,1,0:T(8,128)S(1)}, u32[]{:S(2)}, u32[]{:S(2)}) collective-permute-start(f32[20,24,128]{2,1,0:T(8,128)S(1)} %get-tuple-element.29), channel_id=1, source_target_pairs={{1,0},{2,1},{3,2},{4,3},{5,4},{6,5},{7,6},{8,7},{9,8},{10,9},{11,1... | collective-permute-start | bytes 737288 | tf_op jit(solution)/shard_map/ppermute | solution.py:564
  101.8 0.1 slice_reduce_fusion
  101.9 4.6 %collective-permute-done.5.refs_1_ = f32[20,24,128]{2,1,0:T(8,128)S(1)} collective-permute-done((f32[20,24,128]{2,1,0:T(8,128)S(1)}, f32[20,24,128]{2,1,0:T(8,128)S(1)}, u32[]{:S(2)}, u32[]{:S(2)}) %collective-permute-start.5) | collective-permute-done | bytes 245792 | tf_op jit(solution)/shard_map/ppermute | solution.py:564
  106.5 5.5 %collective-permute-start.7 = (f32[4,24,128]{2,1,0:T(8,128)S(1)}, f32[4,24,128]{2,1,0:T(8,128)S(1)}, u32[]{:S(2)}, u32[]{:S(2)}) collective-permute-start(f32[4,24,128]{2,1,0:T(8,128)S(1)} %slice_add_fusion.1), channel_id=1, source_target_pairs={{32,0},{33,1},{34,2},{35,3},{36,4},{37,5},{38,6},{39,7},{40,8},{41... | collective-permute-start | bytes 147464 | tf_op jit(solution)/shard_map/ppermute | solution.py:564
  112.0 0.0 copy-start.9
  112.0 0.0 copy-start.10
  112.1 6.0 %collective-permute-start.6 = (f32[8,24,128]{2,1,0:T(8,128)S(1)}, f32[8,24,128]{2,1,0:T(8,128)S(1)}, u32[]{:S(2)}, u32[]{:S(2)}) collective-permute-start(f32[8,24,128]{2,1,0:T(8,128)S(1)} %slice_add_fusion), channel_id=1, source_target_pairs={{16,0},{17,1},{18,2},{19,3},{20,4},{21,5},{22,6},{23,7},{24,8},{25... | collective-permute-start | bytes 294920 | tf_op jit(solution)/shard_map/ppermute | solution.py:564
  118.0 0.0 copy-done.9
  118.0 0.0 copy-done.10
  118.1 0.1 pad_add_fusion.3.meta
  118.1 0.0 copy-done.4
  118.1 2.0 %shard_map.135.refs_4_ = f32[24,9,8,128]{3,2,1,0:T(8,128)S(1)} custom-call(f32[2,192,576]{2,1,0:T(8,128)S(1)} %bitcast.24), custom_call_target="tpu_custom_call" | custom-call | tf_op jit(solution)/shard_map/pallas_call | solution.py:583
  120.2 0.0 collective-permute-done.7.refs_3_
  120.2 0.0 collective-permute-done.6.refs_2_
  120.2 15.4 %shard_map.136 = (f32[24,9,8,128]{3,2,1,0:T(8,128)S(1)}, f32[8,128]{1,0:T(8,128)S(1)}, f32[8,24,128]{2,1,0:T(8,128)S(1)}, f32[8,24,128]{2,1,0:T(8,128)S(1)}, f32[4,24,128]{2,1,0:T(8,128)S(1)}) custom-call(s32[8]{0:T(128)S(1)} %pad_add_fusion.3.meta, f32[8,24,128]{2,1,0:T(8,128)S(1)} %get-tuple-element.28.refs_0_, ...), custom_call_target="tpu_custom_call" | custom-call | tf_op jit(solution)/shard_map/pallas_call | solution.py:638
  135.7 1.9 %collective-permute-start.8 = (f32[8,24,128]{2,1,0:T(8,128)S(1)}, f32[8,24,128]{2,1,0:T(8,128)S(1)}, u32[]{:S(2)}, u32[]{:S(2)}) collective-permute-start(f32[8,24,128]{2,1,0:T(8,128)S(1)} %get-tuple-element.35), channel_id=1, source_target_pairs={{0,16},{1,17},{2,18},{3,19},{4,20},{5,21},{6,22},{7,23},{8,24},{9,... | collective-permute-start | bytes 294920 | tf_op jit(solution)/shard_map/ppermute | solution.py:564
  137.6 5.5 %collective-permute-start.9 = (f32[4,24,128]{2,1,0:T(8,128)S(1)}, f32[4,24,128]{2,1,0:T(8,128)S(1)}, u32[]{:S(2)}, u32[]{:S(2)}) collective-permute-start(f32[4,24,128]{2,1,0:T(8,128)S(1)} %get-tuple-element.36), channel_id=1, source_target_pairs={{0,32},{1,33},{2,34},{3,35},{4,36},{5,37},{6,38},{7,39},{8,40},{9,... | collective-permute-start | bytes 147464 | tf_op jit(solution)/shard_map/ppermute | solution.py:564
  143.0 6.0 %collective-permute-done.9.refs_2_ = f32[4,24,128]{2,1,0:T(8,128)S(1)} collective-permute-done((f32[4,24,128]{2,1,0:T(8,128)S(1)}, f32[4,24,128]{2,1,0:T(8,128)S(1)}, u32[]{:S(2)}, u32[]{:S(2)}) %collective-permute-start.9) | collective-permute-done | bytes 49184 | tf_op jit(solution)/shard_map/ppermute | solution.py:564
  149.1 0.0 collective-permute-done.8.refs_1_
  149.1 1.9 %collective-permute-start.10 = (f32[20,24,128]{2,1,0:T(8,128)S(1)}, f32[20,24,128]{2,1,0:T(8,128)S(1)}, u32[]{:S(2)}, u32[]{:S(2)}) collective-permute-start(f32[20,24,128]{2,1,0:T(8,128)S(1)} %pad_maximum_fusion), channel_id=1, source_target_pairs={{0,1},{1,2},{2,3},{3,4},{4,5},{5,6},{6,7},{7,8},{8,9},{9,10},{10,1... | collective-permute-start | bytes 737288 | tf_op jit(solution)/shard_map/ppermute | solution.py:564
  151.0 2.9 %shard_map.137 = f32[2,192,576]{2,1,0:T(8,128)} custom-call(f32[24,9,8,128]{3,2,1,0:T(8,128)S(1)} %get-tuple-element.32.planes, f32[8,128]{1,0:T(8,128)S(1)} %get-tuple-element.33.scale), custom_call_target="tpu_custom_call" | custom-call | tf_op jit(solution)/shard_map/pallas_call | solution.py:654
  153.9 9.4 %collective-permute-done.10.refs_3_ = f32[20,24,128]{2,1,0:T(8,128)S(1)} collective-permute-done((f32[20,24,128]{2,1,0:T(8,128)S(1)}, f32[20,24,128]{2,1,0:T(8,128)S(1)}, u32[]{:S(2)}, u32[]{:S(2)}) %collective-permute-start.10) | collective-permute-done | bytes 245792 | tf_op jit(solution)/shard_map/ppermute | solution.py:564
  163.4 3.1 %shard_map.138 = f32[16,32,256]{2,1,0:T(8,128)} custom-call(s32[36]{0:T(128)S(1)} %reshape.26.places, f32[8,24,128]{2,1,0:T(8,128)S(1)} %get-tuple-element.34.refs_0_, f32[8,24,128]{2,1,0:T(8,128)S(1)} %collective-permute-done.8.refs_1_, f32[4,24,128]{2,1,0:T(8,128)S(1)} %collective-permute-done.9.refs_2_, f32[20,24,128]{2,1,0:T(8,128)S(1)} %collective-permute-done.10.refs_3_), custom_call_target="tpu_custom_call" | custom-call | tf_op jit(solution)/shard_map/pallas_call | solution.py:660
  (17 shorter events, 0.2 us)
Async XLA Ops:
  0.6 1.0 copy-start.2
  1.6 1.0 copy-start.6
  3.8 24.6 %copy-start = (bf16[512,512]{1,0:T(8,128)(2,1)S(1)}, bf16[512,512]{1,0:T(8,128)(2,1)}, u32[]{:S(2)}) copy-start(bf16[512,512]{1,0:T(8,128)(2,1)} %constant.73.clone.table_low.rest_1_) | copy-start | bytes 1572868
  3.8 24.6 %copy-start.1 = (bf16[512,512]{1,0:T(8,128)(2,1)S(1)}, bf16[512,512]{1,0:T(8,128)(2,1)}, u32[]{:S(2)}) copy-start(bf16[512,512]{1,0:T(8,128)(2,1)} %constant.72.clone.table_high.rest_0_) | copy-start | bytes 1572868
  3.8 24.6 %all-to-all-start = ((f32[16,16,512]{2,1,0:T(8,128)}), f32[16,16,512]{2,1,0:T(8,128)S(1)}, u32[]{:S(2)}, u32[]{:S(2)}) async-start(f32[16,16,512]{2,1,0:T(8,128)} %shard_map.130), calls=%async_computation | async-start | bytes 1048576 | tf_op jit(solution)/shard_map/all_to_all | solution.py:596
  14.2 0.7 copy-start.8
  15.0 10.9 %collective-permute-start = (s32[8]{0:T(128)S(1)}, s32[8]{0:T(128)S(1)}, u32[]{:S(2)}, u32[]{:S(2)}) collective-permute-start(s32[8]{0:T(128)S(1)} %get-tuple-element.48), channel_id=1, source_target_pairs={{0,16},{1,17},{2,18},{3,19},{4,20},{5,21},{6,22},{7,23},{8,24},{9,... | collective-permute-start | bytes 104 | tf_op jit(solution)/shard_map/ppermute | solution.py:564
  16.9 10.4 %collective-permute-start.1 = (s32[8]{0:T(128)S(1)}, s32[8]{0:T(128)S(1)}, u32[]{:S(2)}, u32[]{:S(2)}) collective-permute-start(s32[8]{0:T(128)S(1)} %get-tuple-element.48), channel_id=1, source_target_pairs={{0,32},{1,33},{2,34},{3,35},{4,36},{5,37},{6,38},{7,39},{8,40},{9,... | collective-permute-start | bytes 104 | tf_op jit(solution)/shard_map/ppermute | solution.py:564
  27.2 1.2 copy-start.7
  29.3 7.5 %collective-permute-start.3 = (f32[32,512]{1,0:T(8,128)S(1)}, f32[32,512]{1,0:T(8,128)S(1)}, u32[]{:S(2)}, u32[]{:S(2)}) collective-permute-start(f32[32,512]{1,0:T(8,128)S(1)} %get-tuple-element.23), channel_id=1, source_target_pairs={{0,16},{1,17},{2,18},{3,19},{4,20},{5,21},{6,22},{7,23},{8,24},{9,... | collective-permute-start | bytes 196616 | tf_op jit(solution)/shard_map/ppermute | solution.py:607
  36.9 11.4 %collective-permute-start.4 = (f32[32,512]{1,0:T(8,128)S(1)}, f32[32,512]{1,0:T(8,128)S(1)}, u32[]{:S(2)}, u32[]{:S(2)}) collective-permute-start(f32[32,512]{1,0:T(8,128)S(1)} %pad_maximum_fusion.1), channel_id=1, source_target_pairs={{0,32},{1,33},{2,34},{3,35},{4,36},{5,37},{6,38},{7,39},{8,40},{9,... | collective-permute-start | bytes 196616 | tf_op jit(solution)/shard_map/ppermute | solution.py:607
  49.2 23.5 %all-to-all-start.1 = ((f32[8,32,512]{2,1,0:T(8,128)}), f32[8,32,512]{2,1,0:T(8,128)S(1)}, u32[]{:S(2)}, u32[]{:S(2)}) async-start(f32[8,32,512]{2,1,0:T(8,128)} %broadcast_in_dim.12), calls=%async_computation.1 | async-start | bytes 1048576 | tf_op jit(solution)/shard_map/all_to_all | solution.py:613
  74.6 20.9 %copy-start.3 = (bf16[2,256,256]{2,1,0:T(8,128)(2,1)S(1)}, bf16[2,256,256]{2,1,0:T(8,128)(2,1)}, u32[]{:S(2)}) copy-start(bf16[2,256,256]{2,1,0:T(8,128)(2,1)} %constant.74.clone.table) | copy-start | bytes 786436
  74.6 20.9 %copy-start.5 = (f32[16,32,256]{2,1,0:T(8,128)S(1)}, f32[16,32,256]{2,1,0:T(8,128)}, u32[]{:S(2)}) copy-start(f32[16,32,256]{2,1,0:T(8,128)} %external.1) | copy-start | bytes 1572868
  74.6 20.9 %all-to-all-start.2 = ((f32[16,16,512]{2,1,0:T(8,128)}), f32[16,16,512]{2,1,0:T(8,128)S(1)}, u32[]{:S(2)}, u32[]{:S(2)}) async-start(f32[16,16,512]{2,1,0:T(8,128)} %shard_map.133), calls=%async_computation.2 | async-start | bytes 1048576 | tf_op jit(solution)/shard_map/all_to_all | solution.py:626
  83.0 35.1 %copy-start.4 = (f32[2,8,24,576]{3,2,1,0:T(8,128)S(1)}, f32[2,8,24,576]{3,2,1,0:T(8,128)}, u32[]{:S(2)}) copy-start(f32[2,8,24,576]{3,2,1,0:T(8,128)} %param.13) | copy-start | bytes 2654212
  83.0 10.6 %collective-permute-start.2 = (s32[3,8]{1,0:T(4,128)S(1)}, s32[3,8]{1,0:T(4,128)S(1)}, u32[]{:S(2)}, u32[]{:S(2)}) collective-permute-start(s32[3,8]{1,0:T(4,128)S(1)} %pad_add_fusion.1), channel_id=1, source_target_pairs={{0,1},{1,2},{2,3},{3,4},{4,5},{5,6},{6,7},{7,8},{8,9},{9,10},{10,1... | collective-permute-start | bytes 296 | tf_op jit(solution)/shard_map/ppermute | solution.py:564
  98.4 8.1 %collective-permute-start.5 = (f32[20,24,128]{2,1,0:T(8,128)S(1)}, f32[20,24,128]{2,1,0:T(8,128)S(1)}, u32[]{:S(2)}, u32[]{:S(2)}) collective-permute-start(f32[20,24,128]{2,1,0:T(8,128)S(1)} %get-tuple-element.29), channel_id=1, source_target_pairs={{1,0},{2,1},{3,2},{4,3},{5,4},{6,5},{7,6},{8,7},{9,8},{10,9},{11,1... | collective-permute-start | bytes 737288 | tf_op jit(solution)/shard_map/ppermute | solution.py:564
  106.5 13.7 %collective-permute-start.7 = (f32[4,24,128]{2,1,0:T(8,128)S(1)}, f32[4,24,128]{2,1,0:T(8,128)S(1)}, u32[]{:S(2)}, u32[]{:S(2)}) collective-permute-start(f32[4,24,128]{2,1,0:T(8,128)S(1)} %slice_add_fusion.1), channel_id=1, source_target_pairs={{32,0},{33,1},{34,2},{35,3},{36,4},{37,5},{38,6},{39,7},{40,8},{41... | collective-permute-start | bytes 147464 | tf_op jit(solution)/shard_map/ppermute | solution.py:564
  112.0 6.0 %copy-start.9 = (s32[2]{0:T(128)S(1)}, s32[2]{0:T(128)}, u32[]{:S(2)}) copy-start(s32[2]{0:T(128)} %param.15) | copy-start | bytes 28
  112.0 6.0 %copy-start.10 = (s32[2]{0:T(128)S(1)}, s32[2]{0:T(128)}, u32[]{:S(2)}) copy-start(s32[2]{0:T(128)} %param.16) | copy-start | bytes 28
  112.1 8.2 %collective-permute-start.6 = (f32[8,24,128]{2,1,0:T(8,128)S(1)}, f32[8,24,128]{2,1,0:T(8,128)S(1)}, u32[]{:S(2)}, u32[]{:S(2)}) collective-permute-start(f32[8,24,128]{2,1,0:T(8,128)S(1)} %slice_add_fusion), channel_id=1, source_target_pairs={{16,0},{17,1},{18,2},{19,3},{20,4},{21,5},{22,6},{23,7},{24,8},{25... | collective-permute-start | bytes 294920 | tf_op jit(solution)/shard_map/ppermute | solution.py:564
  135.7 13.4 %collective-permute-start.8 = (f32[8,24,128]{2,1,0:T(8,128)S(1)}, f32[8,24,128]{2,1,0:T(8,128)S(1)}, u32[]{:S(2)}, u32[]{:S(2)}) collective-permute-start(f32[8,24,128]{2,1,0:T(8,128)S(1)} %get-tuple-element.35), channel_id=1, source_target_pairs={{0,16},{1,17},{2,18},{3,19},{4,20},{5,21},{6,22},{7,23},{8,24},{9,... | collective-permute-start | bytes 294920 | tf_op jit(solution)/shard_map/ppermute | solution.py:564
  137.6 11.5 %collective-permute-start.9 = (f32[4,24,128]{2,1,0:T(8,128)S(1)}, f32[4,24,128]{2,1,0:T(8,128)S(1)}, u32[]{:S(2)}, u32[]{:S(2)}) collective-permute-start(f32[4,24,128]{2,1,0:T(8,128)S(1)} %get-tuple-element.36), channel_id=1, source_target_pairs={{0,32},{1,33},{2,34},{3,35},{4,36},{5,37},{6,38},{7,39},{8,40},{9,... | collective-permute-start | bytes 147464 | tf_op jit(solution)/shard_map/ppermute | solution.py:564
  149.1 14.2 %collective-permute-start.10 = (f32[20,24,128]{2,1,0:T(8,128)S(1)}, f32[20,24,128]{2,1,0:T(8,128)S(1)}, u32[]{:S(2)}, u32[]{:S(2)}) collective-permute-start(f32[20,24,128]{2,1,0:T(8,128)S(1)} %pad_maximum_fusion), channel_id=1, source_target_pairs={{0,1},{1,2},{2,3},{3,4},{4,5},{5,6},{6,7},{7,8},{8,9},{9,10},{10,1... | collective-permute-start | bytes 737288 | tf_op jit(solution)/shard_map/ppermute | solution.py:564

commit v3 on v2

--- a/solution.py
+++ b/solution.py
@@ -103,17 +103,12 @@
     after = before
     for bit in range(5):
         upper = (place[0] >> bit) % 2 == 1
-        if bit < 3:
-            power_out[bit] = power
-        if bit < 2:
-            weight_out[bit] = jnp.where(upper, before, after)
-        if bit == 2:
-            ends_out[0] = before
-            ends_out[1] = after
+        power_out[bit] = power
+        weight_out[bit] = jnp.where(upper, before, after)
         before, after = jnp.where(upper, before * power, before), jnp.where(upper, after, after * power)
         power = power * power
-    ends_out[2] = before
-    ends_out[3] = after
+    ends_out[0] = before
+    ends_out[1] = after
 
 
 def forward_y(tiles, table_high, table_low, ey, ez, field_out, moment_out, merged):
@@ -139,25 +134,16 @@
     moment_out[KZ:] = last
 
 
-def back_y(place, field, totals, right, left, power, ends, *rest):
-    table_high, table_low, ey, ez, tiles_out, solved = rest
+def back_y(field, totals, right, left, ends, table_high, table_low, ey, ez, tiles_out, solved):
     rate, scale = decay(ey[...], ez[...])
     across = rate
     for _ in range(9):
         across = across * across
     across = across * rate
     norm = rate / (1.0 - across * across)
-    four = power[2]
-    right_total = left_total = jnp.zeros((KZ, NY), F32)
-    state, after = right_total, left_total
-    for k in range(NPX // 4):
-        state = jnp.where(k == place[0], right_total, state)
-        right_total = totals[k, :KZ] + four * right_total
-    for k in range(NPX // 4 - 1, -1, -1):
-        after = jnp.where(k == place[0], left_total, after)
-        left_total = totals[k, KZ:] + four * left_total
-    state = right[...] + ends[0] * state - norm * (left_total - across * right_total) * ends[2]
-    left = left[...] + ends[1] * after - norm * (right_total - across * left_total) * ends[3]
+    right_total, left_total = totals[:KZ], totals[KZ:]
+    state = right[...] - norm * (left_total - across * right_total) * ends[0]
+    left = left[...] - norm * (right_total - across * left_total) * ends[1]
     for row in range(ROWS):
         state = field[row * KZ : (row + 1) * KZ] + rate * state
         solved[row * KZ : (row + 1) * KZ] = state
@@ -183,24 +169,21 @@
     return lanes(rows) // 32
 
 
-def back_z(places, tiles, external, table, field_out, *rest):
-    owned, beside, grid = rest[:3], rest[3], rest[4]
-    spectrum = tiles[...].reshape(NZ, ROWS * COLS)
-    turned = spectrum.T
-    field = dot3(split2(turned), (table[0], table[1]), ((1,), (0,)))
-    field = field.reshape(ROWS, COLS, NZ)
-    field_out[...] = field
-    potential = field + external[...]
+def fill_grid(grid, potential):
     for half in range(2):
         grid[half, :, :32] = jnp.zeros((ROWS, 32, 128), F32)
         grid[half, :, 32 + COLS :] = jnp.zeros((ROWS, FRAG, 128), F32)
         grid[half, :, 32 : 32 + COLS] = potential[:, :, half * 128 : half * 128 + 128]
+
+
+def cut_windows(places, grid, along, outs):
     lane = lanes(FRAG)
     slot_of = slots_of(FRAG)
-    for k, (down, along) in enumerate(STEPS):
+    for down in range(3):
         groups = 8 if down < 2 else 4
-
-        def cut(number, carry, k=k, down=down, along=along, groups=groups):
+        k = 2 * down + along
+
+        def cut(number, carry, k=k, down=down, groups=groups):
             totals = []
             for part in range(4):
                 total = None
@@ -215,12 +198,27 @@
                 totals.append(total)
             for part in range(4):
                 if along:
-                    beside[8 * down + 4 * number + part] = totals[part]
+                    outs[0][8 * down + 4 * number + part] = totals[part]
                 else:
-                    owned[down][4 * number + part] = totals[part]
+                    outs[down][4 * number + part] = totals[part]
             return carry
 
         lax.fori_loop(0, groups // 4, cut, 0)
+
+
+def back_z(places, tiles, external, table, field_out, beside, grid):
+    spectrum = tiles[...].reshape(NZ, ROWS * COLS)
+    turned = spectrum.T
+    field = dot3(split2(turned), (table[0], table[1]), ((1,), (0,)))
+    field = field.reshape(ROWS, COLS, NZ)
+    field_out[...] = field
+    fill_grid(grid, field + external[...])
+    cut_windows(places, grid, 1, (beside,))
+
+
+def cut_owned(places, field, external, *rest):
+    fill_grid(rest[3], field[...] + external[...])
+    cut_windows(places, rest[3], 0, rest[:3])
 
 
 def orbitals_in(orbitals, out, strips, turned):
@@ -517,24 +515,17 @@
         lax.fori_loop(0, groups // 4, share, 0)
 
 
-def patch(places, *refs):
-    shares, beside, out, grid = refs[:3], refs[3], refs[4], refs[5]
-
-    def clear(row, carry):
-        for half in range(2):
-            grid[half, row] = jnp.zeros((PADDED, 128), F32)
-        return carry
-
-    lax.fori_loop(0, ROWS, clear, 0)
+def add_windows(places, grid, along, shares):
     lane = lanes(FRAG)
-    for k, (down, along) in enumerate(STEPS):
+    for down in range(3):
         groups = 8 if down < 2 else 4
-
-        def add(number, carry, k=k, down=down, along=along, groups=groups):
+        k = 2 * down + along
+
+        def add(number, carry, k=k, down=down, groups=groups):
             pieces = []
             for part in range(4):
                 group = 4 * number + part
-                both = beside[8 * down + group] if along else shares[down][group]
+                both = shares[0][8 * down + group] if along else shares[down][group]
                 for slot in range(4):
                     depth = places[6 * k + 3 * (slot % 2) + 2]
                     pieces.append(pltpu.roll(both, (256 + depth - 32 * slot) & 127, 1))
@@ -550,6 +541,23 @@
             return carry
 
         lax.fori_loop(0, groups // 4, add, 0)
+
+
+def patch_owned(places, first, second, third, out, grid):
+    def clear(row, carry):
+        for half in range(2):
+            grid[half, row] = jnp.zeros((PADDED, 128), F32)
+        return carry
+
+    lax.fori_loop(0, ROWS, clear, 0)
+    add_windows(places, grid, 0, (first, second, third))
+    for half in range(2):
+        out[:, :, half * 128 : half * 128 + 128] = grid[half, :, 32 : 32 + COLS]
+
+
+def patch_beside(places, owned, beside, out, grid):
+    fill_grid(grid, owned[...])
+    add_windows(places, grid, 1, (beside,))
     for half in range(2):
         out[:, :, half * 128 : half * 128 + 128] = grid[half, :, 32 : 32 + COLS]
 
@@ -587,7 +595,7 @@
     )(orbitals.reshape(2, NORB * FRAG, FRAG * FRAG))
     power, weight, ends = call(
         scan_powers,
-        (shape(3, KZ, NY), shape(2, KZ, NY), shape(4, KZ, NY)),
+        (shape(5, KZ, NY), shape(5, KZ, NY), shape(2, KZ, NY)),
         smem=(0,),
         count=3,
     )(row_place.reshape(1).astype(jnp.int32), ey, ez)
@@ -602,36 +610,27 @@
     )(tiles, *sine_y, ey, ez)
 
     right, left = jnp.zeros((KZ, NY), F32), jnp.zeros((KZ, NY), F32)
-    for bit in range(2):
-        pairs = [(p * NPY + q, (p ^ (1 << bit)) * NPY + q) for p in range(NPX) for q in range(NPY)]
+    for bit, partner in enumerate((1, 2, 4, 8, 24)):
+        pairs = [(p * NPY + q, (p ^ partner) * NPY + q) for p in range(NPX) for q in range(NPY)]
         got = lax.ppermute(totals, ALL, pairs)
         upper = (row_place >> bit) % 2 == 1
         high, low = jnp.where(upper, totals, got), jnp.where(upper, got, totals)
         right = right + jnp.where(upper, weight[bit] * got[:KZ], 0.0)
         left = left + jnp.where(upper, 0.0, weight[bit] * got[KZ:])
         totals = jnp.concatenate([high[:KZ] + power[bit] * low[:KZ], low[KZ:] + power[bit] * high[KZ:]])
-    totals = lax.all_to_all(
-        jnp.broadcast_to(totals, (NPX // 4, 2 * KZ, NY)), "px_0", split_axis=0, concat_axis=0, tiled=True
-    )
-
-    tiles = call(
-        back_y,
-        shape(NPY, KZ, ROWS * COLS),
-        [pltpu.VMEM((ROWS * KZ, NY), F32)],
-        smem=(0,),
-        count=11,
-    )(
-        (row_place // 4).reshape(1).astype(jnp.int32), field, totals, right, left, power, ends, *sine_y, ey, ez
+
+    tiles = call(back_y, shape(NPY, KZ, ROWS * COLS), [pltpu.VMEM((ROWS * KZ, NY), F32)], count=9)(
+        field, totals, right, left, ends, *sine_y, ey, ez
     )
     tiles = lax.all_to_all(tiles, "py", split_axis=0, concat_axis=0, tiled=True)
     groups = (8, 8, 4)
-    hartree_field, *owned, beside = call(
-        back_z,
-        [shape(ROWS, COLS, NZ)] + [shape(n, FRAG, 128) for n in groups + (20,)],
-        [pltpu.VMEM((2, ROWS, PADDED, 128), F32)],
-        smem=(0,),
-        count=4,
+    grid = [pltpu.VMEM((2, ROWS, PADDED, 128), F32)]
+    hartree_field, beside = call(
+        back_z, [shape(ROWS, COLS, NZ), shape(20, FRAG, 128)], grid, smem=(0,), count=4
     )(places, tiles, external, sine_z)
+    owned = call(cut_owned, [shape(n, FRAG, 128) for n in groups], grid, smem=(0,), count=3)(
+        places, hartree_field, external
+    )
     beside = moved(beside, 0, -1)
     next_rows = moved(owned[1] + beside[8:16], -1, 0)
     last_rows = moved(owned[2] + beside[16:], -2, 0)
@@ -657,13 +656,10 @@
         [pltpu.VMEM((2, 5, NORB * FRAG, 128), F32), pltpu.VMEM((3, 128, 128), F32)],
         count=2,
     )(planes, scale)
-    new_density = call(
-        patch,
-        shape(ROWS, COLS, NZ),
-        [pltpu.VMEM((2, ROWS, PADDED, 128), F32)],
-        smem=(0,),
-        count=5,
-    )(places, *received, beside)
+    density_owned = call(patch_owned, shape(ROWS, COLS, NZ), grid, smem=(0,), count=4)(places, *received)
+    new_density = call(patch_beside, shape(ROWS, COLS, NZ), grid, smem=(0,), count=3)(
+        places, density_owned, beside
+    )
     return hartree_field, filtered.reshape(orbitals.shape), new_density
 
 

time: 167 us -> 161 us (0.964)
  the two profiles are of different devices: /device:TPU:14 before, /device:TPU:38 now
where the time goes in v3:
time: 161 us; the launch traced here: 160 us
  starting transfers between devices  69.1 us (43%)
  waiting for transfers between devices  54.9 us (34%)
  Pallas kernels  28.9 us (18%)
  local copies, waits for them, and re-layouts  5.29 us (3%)
    ppermute x9, starting transfers between devices, moved(): return lax.ppermute(x, ALL, pairs)  34.4 us
    ppermute x9, waiting for transfers between devices, moved(): return lax.ppermute(x, ALL, pairs)  29.6 us
    ppermute x5, waiting for transfers between devices, body(): got = lax.ppermute(totals, ALL, pairs)  23.5 us
    all_to_all x2, starting transfers between devices, body(): tiles = lax.all_to_all(tiles, 'py', split_axis=0, concat_axis=0, tiled=True)  17.8 us
    ppermute x5, starting transfers between devices, body(): got = lax.ppermute(totals, ALL, pairs)  16.8 us
    pallas_call x1, Pallas kernels, body(): call(filter_fragments, [shape(FRAG, 9, 8, 128), shape(8, 128)] + [shape(n...  12.4 us
    unnamed x24, local copies, waits for them, and re-layouts  4.29 us
  transfers between devices with their start and end apart: 16, of which 13 were waited for; matrix products, arithmetic and copies ran while one was open for 1% of the time, Pallas kernels for 5%

profile of v3, /device:TPU:38, one launch (start us, length us, event | category | flops | bytes accessed | tf_op | source)
XLA Modules:
  0.0 159.6 jit_solution(17104183111398847911)
XLA Ops:
  0.6 0.0 copy-start.3
  0.6 0.9 copy-done.3
  1.6 1.0 copy-done.6
  2.6 1.2 shard_map.130
  3.8 10.4 %all-to-all-start = ((f32[16,16,512]{2,1,0:T(8,128)}), f32[16,16,512]{2,1,0:T(8,128)S(1)}, u32[]{:S(2)}, u32[]{:S(2)}) async-start(f32[16,16,512]{2,1,0:T(8,128)} %shard_map.130), calls=%async_computation | async-start | bytes 1048576 | tf_op jit(solution)/shard_map/all_to_all | solution.py:604
  14.2 0.1 pad_add_fusion.2
  14.3 0.6 copy-done.9
  14.9 0.1 reshape.22
  15.0 1.9 %collective-permute-start = (s32[8]{0:T(128)S(1)}, s32[8]{0:T(128)S(1)}, u32[]{:S(2)}, u32[]{:S(2)}) collective-permute-start(s32[8]{0:T(128)S(1)} %get-tuple-element.58), channel_id=1, source_target_pairs={{0,16},{1,17},{2,18},{3,19},{4,20},{5,21},{6,22},{7,23},{8,24},{9,... | collective-permute-start | bytes 104 | tf_op jit(solution)/shard_map/ppermute | solution.py:572
  16.9 8.2 %collective-permute-start.1 = (s32[8]{0:T(128)S(1)}, s32[8]{0:T(128)S(1)}, u32[]{:S(2)}, u32[]{:S(2)}) collective-permute-start(s32[8]{0:T(128)S(1)} %get-tuple-element.58), channel_id=1, source_target_pairs={{0,32},{1,33},{2,34},{3,35},{4,36},{5,37},{6,38},{7,39},{8,40},{9,... | collective-permute-start | bytes 104 | tf_op jit(solution)/shard_map/ppermute | solution.py:572
  25.1 0.7 constant_dynamic-slice_fusion.ez
  25.8 0.1 collective-permute-done
  25.9 2.5 %collective-permute-done.1 = s32[8]{0:T(128)S(1)} collective-permute-done((s32[8]{0:T(128)S(1)}, s32[8]{0:T(128)S(1)}, u32[]{:S(2)}, u32[]{:S(2)}) %collective-permute-start.1) | collective-permute-done | bytes 64 | tf_op jit(solution)/shard_map/ppermute | solution.py:572
  28.4 0.0 all-to-all-done.tiles
  28.4 0.0 copy-done.1
  28.4 0.0 copy-done.2
  28.4 0.6 copy-done.8
  29.0 0.9 shard_map.131
  30.0 7.2 %collective-permute-start.3 = (f32[32,512]{1,0:T(8,128)S(1)}, f32[32,512]{1,0:T(8,128)S(1)}, u32[]{:S(2)}, u32[]{:S(2)}) collective-permute-start(f32[32,512]{1,0:T(8,128)S(1)} %get-tuple-element.23), channel_id=1, source_target_pairs={{0,16},{1,17},{2,18},{3,19},{4,20},{5,21},{6,22},{7,23},{8,24},{9,... | collective-permute-start | bytes 196616 | tf_op jit(solution)/shard_map/ppermute | solution.py:615
  37.1 0.1 shard_map.132
  37.3 0.7 collective-permute-done.3
  38.1 2.7 %collective-permute-start.4 = (f32[32,512]{1,0:T(8,128)S(1)}, f32[32,512]{1,0:T(8,128)S(1)}, u32[]{:S(2)}, u32[]{:S(2)}) collective-permute-start(f32[32,512]{1,0:T(8,128)S(1)} %pad_maximum_fusion.1), channel_id=1, source_target_pairs={{0,32},{1,33},{2,34},{3,35},{4,36},{5,37},{6,38},{7,39},{8,40},{9,... | collective-permute-start | bytes 196616 | tf_op jit(solution)/shard_map/ppermute | solution.py:615
  40.8 7.6 %collective-permute-done.4 = f32[32,512]{1,0:T(8,128)S(1)} collective-permute-done((f32[32,512]{1,0:T(8,128)S(1)}, f32[32,512]{1,0:T(8,128)S(1)}, u32[]{:S(2)}, u32[]{:S(2)}) %collective-permute-start.4) | collective-permute-done | bytes 65568 | tf_op jit(solution)/shard_map/ppermute | solution.py:615
  48.4 2.5 %collective-permute-start.5 = (f32[32,512]{1,0:T(8,128)S(1)}, f32[32,512]{1,0:T(8,128)S(1)}, u32[]{:S(2)}, u32[]{:S(2)}) collective-permute-start(f32[32,512]{1,0:T(8,128)S(1)} %pad_maximum_fusion.2), channel_id=1, source_target_pairs={{0,64},{1,65},{2,66},{3,67},{4,68},{5,69},{6,70},{7,71},{8,72},{9,... | collective-permute-start | bytes 196616 | tf_op jit(solution)/shard_map/ppermute | solution.py:615
  50.9 3.7 %collective-permute-done.5 = f32[32,512]{1,0:T(8,128)S(1)} collective-permute-done((f32[32,512]{1,0:T(8,128)S(1)}, f32[32,512]{1,0:T(8,128)S(1)}, u32[]{:S(2)}, u32[]{:S(2)}) %collective-permute-start.5) | collective-permute-done | bytes 65568 | tf_op jit(solution)/shard_map/ppermute | solution.py:615
  54.6 2.6 %collective-permute-start.6 = (f32[32,512]{1,0:T(8,128)S(1)}, f32[32,512]{1,0:T(8,128)S(1)}, u32[]{:S(2)}, u32[]{:S(2)}) collective-permute-start(f32[32,512]{1,0:T(8,128)S(1)} %pad_maximum_fusion.3), channel_id=1, source_target_pairs={{0,128},{1,129},{2,130},{3,131},{4,132},{5,133},{6,134},{7,135},{8... | collective-permute-start | bytes 196616 | tf_op jit(solution)/shard_map/ppermute | solution.py:615
  57.2 5.2 %collective-permute-done.6 = f32[32,512]{1,0:T(8,128)S(1)} collective-permute-done((f32[32,512]{1,0:T(8,128)S(1)}, f32[32,512]{1,0:T(8,128)S(1)}, u32[]{:S(2)}, u32[]{:S(2)}) %collective-permute-start.6) | collective-permute-done | bytes 65568 | tf_op jit(solution)/shard_map/ppermute | solution.py:615
  62.4 1.9 %collective-permute-start.7 = (f32[32,512]{1,0:T(8,128)S(1)}, f32[32,512]{1,0:T(8,128)S(1)}, u32[]{:S(2)}, u32[]{:S(2)}) collective-permute-start(f32[32,512]{1,0:T(8,128)S(1)} %pad_maximum_fusion.4), channel_id=1, source_target_pairs={{0,384},{1,385},{2,386},{3,387},{4,388},{5,389},{6,390},{7,391},{8... | collective-permute-start | bytes 196616 | tf_op jit(solution)/shard_map/ppermute | solution.py:615
  64.4 6.3 %collective-permute-done.7 = f32[32,512]{1,0:T(8,128)S(1)} collective-permute-done((f32[32,512]{1,0:T(8,128)S(1)}, f32[32,512]{1,0:T(8,128)S(1)}, u32[]{:S(2)}, u32[]{:S(2)}) %collective-permute-start.7) | collective-permute-done | bytes 65568 | tf_op jit(solution)/shard_map/ppermute | solution.py:615
  70.8 2.0 %shard_map.133 = f32[16,16,512]{2,1,0:T(8,128)} custom-call(f32[256,512]{1,0:T(8,128)S(1)} %get-tuple-element.22.field, f32[32,512]{1,0:T(8,128)S(1)} %pad_maximum_fusion.5.totals, f32[16,512]{1,0:T(8,128)S(1)} %fusion.10.right, f32[16,512]{1,0:T(8,128)S(1)} %fusion.1.left, f32[2,16,512]{2,1,0:T(8,128)S(1)} %get-tuple-element.26.ends, ...), custom_call_target="tpu_custom_call" | custom-call | tf_op jit(solution)/shard_map/pallas_call | solution.py:622
  72.8 7.5 %all-to-all-start.1 = ((f32[16,16,512]{2,1,0:T(8,128)}), f32[16,16,512]{2,1,0:T(8,128)S(1)}, u32[]{:S(2)}, u32[]{:S(2)}) async-start(f32[16,16,512]{2,1,0:T(8,128)} %shard_map.133), calls=%async_computation.1 | async-start | bytes 1048576 | tf_op jit(solution)/shard_map/all_to_all | solution.py:625
  80.3 3.4 %collective-permute-start.2 = (s32[3,8]{1,0:T(4,128)S(1)}, s32[3,8]{1,0:T(4,128)S(1)}, u32[]{:S(2)}, u32[]{:S(2)}) collective-permute-start(s32[3,8]{1,0:T(4,128)S(1)} %pad_add_fusion.1), channel_id=1, source_target_pairs={{0,1},{1,2},{2,3},{3,4},{4,5},{5,6},{6,7},{7,8},{8,9},{9,10},{10,1... | collective-permute-start | bytes 296 | tf_op jit(solution)/shard_map/ppermute | solution.py:572
  83.7 6.3 %collective-permute-done.2 = s32[3,8]{1,0:T(4,128)S(1)} collective-permute-done((s32[3,8]{1,0:T(4,128)S(1)}, s32[3,8]{1,0:T(4,128)S(1)}, u32[]{:S(2)}, u32[]{:S(2)}) %collective-permute-start.2) | collective-permute-done | bytes 128 | tf_op jit(solution)/shard_map/ppermute | solution.py:572
  90.0 0.1 reshape.23.places
  90.1 1.8 %all-to-all-done.1.tiles = f32[16,16,512]{2,1,0:T(8,128)S(1)} async-done(((f32[16,16,512]{2,1,0:T(8,128)}), f32[16,16,512]{2,1,0:T(8,128)S(1)}, u32[]{:S(2)}, u32[]{:S(2)}) %all-to-all-start.1) | async-done | bytes 524320 | tf_op jit(solution)/shard_map/all_to_all | solution.py:625
  91.8 0.0 copy-done
  91.8 0.0 copy-done.4
  91.8 2.2 %shard_map.134 = (f32[16,32,256]{2,1,0:T(8,128)}, f32[20,24,128]{2,1,0:T(8,128)S(1)}) custom-call(s32[36]{0:T(128)S(1)} %reshape.23.places, f32[16,16,512]{2,1,0:T(8,128)S(1)} %all-to-all-done.1.tiles, f32[16,32,256]{2,1,0:T(8,128)S(1)} %copy-done, bf16[2,256,256]{2,1,0:T(8,128)(2,1)S(1)} %copy-done.4), custom_call_target="tpu_custom_call" | custom-call | tf_op jit(solution)/shard_map/pallas_call | solution.py:628
  94.0 3.5 %collective-permute-start.8 = (f32[20,24,128]{2,1,0:T(8,128)S(1)}, f32[20,24,128]{2,1,0:T(8,128)S(1)}, u32[]{:S(2)}, u32[]{:S(2)}) collective-permute-start(f32[20,24,128]{2,1,0:T(8,128)S(1)} %get-tuple-element.29), channel_id=1, source_target_pairs={{1,0},{2,1},{3,2},{4,3},{5,4},{6,5},{7,6},{8,7},{9,8},{10,9},{11,1... | collective-permute-start | bytes 737288 | tf_op jit(solution)/shard_map/ppermute | solution.py:572
  97.5 0.1 slice_reduce_fusion
  97.7 1.0 copy-done.7
  98.7 1.3 shard_map.135
  100.0 2.3 %collective-permute-done.8.refs_1_ = f32[20,24,128]{2,1,0:T(8,128)S(1)} collective-permute-done((f32[20,24,128]{2,1,0:T(8,128)S(1)}, f32[20,24,128]{2,1,0:T(8,128)S(1)}, u32[]{:S(2)}, u32[]{:S(2)}) %collective-permute-start.8) | collective-permute-done | bytes 245792 | tf_op jit(solution)/shard_map/ppermute | solution.py:572
  102.3 1.9 %collective-permute-start.10 = (f32[4,24,128]{2,1,0:T(8,128)S(1)}, f32[4,24,128]{2,1,0:T(8,128)S(1)}, u32[]{:S(2)}, u32[]{:S(2)}) collective-permute-start(f32[4,24,128]{2,1,0:T(8,128)S(1)} %slice_add_fusion.1), channel_id=1, source_target_pairs={{32,0},{33,1},{34,2},{35,3},{36,4},{37,5},{38,6},{39,7},{40,8},{41... | collective-permute-start | bytes 147464 | tf_op jit(solution)/shard_map/ppermute | solution.py:572
  104.2 0.0 copy-start.10
  104.2 0.0 copy-start.11
  104.2 1.9 %collective-permute-start.9 = (f32[8,24,128]{2,1,0:T(8,128)S(1)}, f32[8,24,128]{2,1,0:T(8,128)S(1)}, u32[]{:S(2)}, u32[]{:S(2)}) collective-permute-start(f32[8,24,128]{2,1,0:T(8,128)S(1)} %slice_add_fusion), channel_id=1, source_target_pairs={{16,0},{17,1},{18,2},{19,3},{20,4},{21,5},{22,6},{23,7},{24,8},{25... | collective-permute-start | bytes 294920 | tf_op jit(solution)/shard_map/ppermute | solution.py:572
  106.2 0.0 copy-done.10
  106.2 0.0 copy-done.11
  106.2 0.1 pad_add_fusion.3.meta
  106.3 0.0 copy-done.5
  106.3 2.0 %shard_map.136.refs_4_ = f32[24,9,8,128]{3,2,1,0:T(8,128)S(1)} custom-call(f32[2,192,576]{2,1,0:T(8,128)S(1)} %bitcast.41), custom_call_target="tpu_custom_call" | custom-call | tf_op jit(solution)/shard_map/pallas_call | solution.py:591
  108.3 3.8 %collective-permute-done.10.refs_3_ = f32[4,24,128]{2,1,0:T(8,128)S(1)} collective-permute-done((f32[4,24,128]{2,1,0:T(8,128)S(1)}, f32[4,24,128]{2,1,0:T(8,128)S(1)}, u32[]{:S(2)}, u32[]{:S(2)}) %collective-permute-start.10) | collective-permute-done | bytes 49184 | tf_op jit(solution)/shard_map/ppermute | solution.py:572
  112.2 0.0 collective-permute-done.9.refs_2_
  112.2 12.4 %shard_map.137 = (f32[24,9,8,128]{3,2,1,0:T(8,128)S(1)}, f32[8,128]{1,0:T(8,128)S(1)}, f32[8,24,128]{2,1,0:T(8,128)S(1)}, f32[8,24,128]{2,1,0:T(8,128)S(1)}, f32[4,24,128]{2,1,0:T(8,128)S(1)}) custom-call(s32[8]{0:T(128)S(1)} %pad_add_fusion.3.meta, f32[8,24,128]{2,1,0:T(8,128)S(1)} %get-tuple-element.28.refs_0_, ...), custom_call_target="tpu_custom_call" | custom-call | tf_op jit(solution)/shard_map/pallas_call | solution.py:637
  124.6 8.9 %collective-permute-start.11 = (f32[8,24,128]{2,1,0:T(8,128)S(1)}, f32[8,24,128]{2,1,0:T(8,128)S(1)}, u32[]{:S(2)}, u32[]{:S(2)}) collective-permute-start(f32[8,24,128]{2,1,0:T(8,128)S(1)} %get-tuple-element.35), channel_id=1, source_target_pairs={{0,16},{1,17},{2,18},{3,19},{4,20},{5,21},{6,22},{7,23},{8,24},{9,... | collective-permute-start | bytes 294920 | tf_op jit(solution)/shard_map/ppermute | solution.py:572
  133.5 2.8 %collective-permute-start.12 = (f32[4,24,128]{2,1,0:T(8,128)S(1)}, f32[4,24,128]{2,1,0:T(8,128)S(1)}, u32[]{:S(2)}, u32[]{:S(2)}) collective-permute-start(f32[4,24,128]{2,1,0:T(8,128)S(1)} %get-tuple-element.36), channel_id=1, source_target_pairs={{0,32},{1,33},{2,34},{3,35},{4,36},{5,37},{6,38},{7,39},{8,40},{9,... | collective-permute-start | bytes 147464 | tf_op jit(solution)/shard_map/ppermute | solution.py:572
  136.3 9.2 %collective-permute-done.12.third = f32[4,24,128]{2,1,0:T(8,128)S(1)} collective-permute-done((f32[4,24,128]{2,1,0:T(8,128)S(1)}, f32[4,24,128]{2,1,0:T(8,128)S(1)}, u32[]{:S(2)}, u32[]{:S(2)}) %collective-permute-start.12) | collective-permute-done | bytes 49184 | tf_op jit(solution)/shard_map/ppermute | solution.py:572
  145.5 0.0 collective-permute-done.11.second
  145.5 1.9 %collective-permute-start.13 = (f32[20,24,128]{2,1,0:T(8,128)S(1)}, f32[20,24,128]{2,1,0:T(8,128)S(1)}, u32[]{:S(2)}, u32[]{:S(2)}) collective-permute-start(f32[20,24,128]{2,1,0:T(8,128)S(1)} %pad_maximum_fusion), channel_id=1, source_target_pairs={{0,1},{1,2},{2,3},{3,4},{4,5},{5,6},{6,7},{7,8},{8,9},{9,10},{10,1... | collective-permute-start | bytes 737288 | tf_op jit(solution)/shard_map/ppermute | solution.py:572
  147.5 2.9 %shard_map.138 = f32[2,192,576]{2,1,0:T(8,128)} custom-call(f32[24,9,8,128]{3,2,1,0:T(8,128)S(1)} %get-tuple-element.32.planes, f32[8,128]{1,0:T(8,128)S(1)} %get-tuple-element.33.scale), custom_call_target="tpu_custom_call" | custom-call | tf_op jit(solution)/shard_map/pallas_call | solution.py:653
  150.4 1.5 shard_map.139.owned
  151.9 5.4 %collective-permute-done.13.beside = f32[20,24,128]{2,1,0:T(8,128)S(1)} collective-permute-done((f32[20,24,128]{2,1,0:T(8,128)S(1)}, f32[20,24,128]{2,1,0:T(8,128)S(1)}, u32[]{:S(2)}, u32[]{:S(2)}) %collective-permute-start.13) | collective-permute-done | bytes 245792 | tf_op jit(solution)/shard_map/ppermute | solution.py:572
  157.3 2.3 %shard_map.140 = f32[16,32,256]{2,1,0:T(8,128)} custom-call(s32[36]{0:T(128)S(1)} %reshape.23.places, f32[16,32,256]{2,1,0:T(8,128)S(1)} %shard_map.139.owned, f32[20,24,128]{2,1,0:T(8,128)S(1)} %collective-permute-done.13.beside), custom_call_target="tpu_custom_call" | custom-call | tf_op jit(solution)/shard_map/pallas_call | solution.py:660
  (34 shorter events, 0.3 us)
Async XLA Ops:
  0.6 1.0 copy-start.3
  1.6 1.0 copy-start.6
  3.8 24.6 %copy-start.1 = (bf16[512,512]{1,0:T(8,128)(2,1)S(1)}, bf16[512,512]{1,0:T(8,128)(2,1)}, u32[]{:S(2)}) copy-start(bf16[512,512]{1,0:T(8,128)(2,1)} %constant.75.clone.table_low) | copy-start | bytes 1572868
  3.8 24.6 %copy-start.2 = (bf16[512,512]{1,0:T(8,128)(2,1)S(1)}, bf16[512,512]{1,0:T(8,128)(2,1)}, u32[]{:S(2)}) copy-start(bf16[512,512]{1,0:T(8,128)(2,1)} %constant.74.clone.table_high) | copy-start | bytes 1572868
  3.8 24.6 %all-to-all-start = ((f32[16,16,512]{2,1,0:T(8,128)}), f32[16,16,512]{2,1,0:T(8,128)S(1)}, u32[]{:S(2)}, u32[]{:S(2)}) async-start(f32[16,16,512]{2,1,0:T(8,128)} %shard_map.130), calls=%async_computation | async-start | bytes 1048576 | tf_op jit(solution)/shard_map/all_to_all | solution.py:604
  14.2 0.7 copy-start.9
  15.0 10.9 %collective-permute-start = (s32[8]{0:T(128)S(1)}, s32[8]{0:T(128)S(1)}, u32[]{:S(2)}, u32[]{:S(2)}) collective-permute-start(s32[8]{0:T(128)S(1)} %get-tuple-element.58), channel_id=1, source_target_pairs={{0,16},{1,17},{2,18},{3,19},{4,20},{5,21},{6,22},{7,23},{8,24},{9,... | collective-permute-start | bytes 104 | tf_op jit(solution)/shard_map/ppermute | solution.py:572
  16.9 11.5 %collective-permute-start.1 = (s32[8]{0:T(128)S(1)}, s32[8]{0:T(128)S(1)}, u32[]{:S(2)}, u32[]{:S(2)}) collective-permute-start(s32[8]{0:T(128)S(1)} %get-tuple-element.58), channel_id=1, source_target_pairs={{0,32},{1,33},{2,34},{3,35},{4,36},{5,37},{6,38},{7,39},{8,40},{9,... | collective-permute-start | bytes 104 | tf_op jit(solution)/shard_map/ppermute | solution.py:572
  28.4 0.7 copy-start.8
  30.0 8.1 %collective-permute-start.3 = (f32[32,512]{1,0:T(8,128)S(1)}, f32[32,512]{1,0:T(8,128)S(1)}, u32[]{:S(2)}, u32[]{:S(2)}) collective-permute-start(f32[32,512]{1,0:T(8,128)S(1)} %get-tuple-element.23), channel_id=1, source_target_pairs={{0,16},{1,17},{2,18},{3,19},{4,20},{5,21},{6,22},{7,23},{8,24},{9,... | collective-permute-start | bytes 196616 | tf_op jit(solution)/shard_map/ppermute | solution.py:615
  38.1 10.3 %collective-permute-start.4 = (f32[32,512]{1,0:T(8,128)S(1)}, f32[32,512]{1,0:T(8,128)S(1)}, u32[]{:S(2)}, u32[]{:S(2)}) collective-permute-start(f32[32,512]{1,0:T(8,128)S(1)} %pad_maximum_fusion.1), channel_id=1, source_target_pairs={{0,32},{1,33},{2,34},{3,35},{4,36},{5,37},{6,38},{7,39},{8,40},{9,... | collective-permute-start | bytes 196616 | tf_op jit(solution)/shard_map/ppermute | solution.py:615
  48.4 6.2 %collective-permute-start.5 = (f32[32,512]{1,0:T(8,128)S(1)}, f32[32,512]{1,0:T(8,128)S(1)}, u32[]{:S(2)}, u32[]{:S(2)}) collective-permute-start(f32[32,512]{1,0:T(8,128)S(1)} %pad_maximum_fusion.2), channel_id=1, source_target_pairs={{0,64},{1,65},{2,66},{3,67},{4,68},{5,69},{6,70},{7,71},{8,72},{9,... | collective-permute-start | bytes 196616 | tf_op jit(solution)/shard_map/ppermute | solution.py:615
  54.6 7.8 %collective-permute-start.6 = (f32[32,512]{1,0:T(8,128)S(1)}, f32[32,512]{1,0:T(8,128)S(1)}, u32[]{:S(2)}, u32[]{:S(2)}) collective-permute-start(f32[32,512]{1,0:T(8,128)S(1)} %pad_maximum_fusion.3), channel_id=1, source_target_pairs={{0,128},{1,129},{2,130},{3,131},{4,132},{5,133},{6,134},{7,135},{8... | collective-permute-start | bytes 196616 | tf_op jit(solution)/shard_map/ppermute | solution.py:615
  62.4 8.3 %collective-permute-start.7 = (f32[32,512]{1,0:T(8,128)S(1)}, f32[32,512]{1,0:T(8,128)S(1)}, u32[]{:S(2)}, u32[]{:S(2)}) collective-permute-start(f32[32,512]{1,0:T(8,128)S(1)} %pad_maximum_fusion.4), channel_id=1, source_target_pairs={{0,384},{1,385},{2,386},{3,387},{4,388},{5,389},{6,390},{7,391},{8... | collective-permute-start | bytes 196616 | tf_op jit(solution)/shard_map/ppermute | solution.py:615
  72.8 19.0 %copy-start = (f32[16,32,256]{2,1,0:T(8,128)S(1)}, f32[16,32,256]{2,1,0:T(8,128)}, u32[]{:S(2)}) copy-start(f32[16,32,256]{2,1,0:T(8,128)} %external.3) | copy-start | bytes 1572868
  72.8 19.0 %copy-start.4 = (bf16[2,256,256]{2,1,0:T(8,128)(2,1)S(1)}, bf16[2,256,256]{2,1,0:T(8,128)(2,1)}, u32[]{:S(2)}) copy-start(bf16[2,256,256]{2,1,0:T(8,128)(2,1)} %constant.76.clone.table) | copy-start | bytes 786436
  72.8 19.0 %all-to-all-start.1 = ((f32[16,16,512]{2,1,0:T(8,128)}), f32[16,16,512]{2,1,0:T(8,128)S(1)}, u32[]{:S(2)}, u32[]{:S(2)}) async-start(f32[16,16,512]{2,1,0:T(8,128)} %shard_map.133), calls=%async_computation.1 | async-start | bytes 1048576 | tf_op jit(solution)/shard_map/all_to_all | solution.py:625
  80.3 9.7 %collective-permute-start.2 = (s32[3,8]{1,0:T(4,128)S(1)}, s32[3,8]{1,0:T(4,128)S(1)}, u32[]{:S(2)}, u32[]{:S(2)}) collective-permute-start(s32[3,8]{1,0:T(4,128)S(1)} %pad_add_fusion.1), channel_id=1, source_target_pairs={{0,1},{1,2},{2,3},{3,4},{4,5},{5,6},{6,7},{7,8},{8,9},{9,10},{10,1... | collective-permute-start | bytes 296 | tf_op jit(solution)/shard_map/ppermute | solution.py:572
  94.0 12.2 %copy-start.5 = (f32[2,8,24,576]{3,2,1,0:T(8,128)S(1)}, f32[2,8,24,576]{3,2,1,0:T(8,128)}, u32[]{:S(2)}) copy-start(f32[2,8,24,576]{3,2,1,0:T(8,128)} %param.13) | copy-start | bytes 2654212
  94.0 8.2 %collective-permute-start.8 = (f32[20,24,128]{2,1,0:T(8,128)S(1)}, f32[20,24,128]{2,1,0:T(8,128)S(1)}, u32[]{:S(2)}, u32[]{:S(2)}) collective-permute-start(f32[20,24,128]{2,1,0:T(8,128)S(1)} %get-tuple-element.29), channel_id=1, source_target_pairs={{1,0},{2,1},{3,2},{4,3},{5,4},{6,5},{7,6},{8,7},{9,8},{10,9},{11,1... | collective-permute-start | bytes 737288 | tf_op jit(solution)/shard_map/ppermute | solution.py:572
  97.7 1.0 copy-start.7
  102.3 9.9 %collective-permute-start.10 = (f32[4,24,128]{2,1,0:T(8,128)S(1)}, f32[4,24,128]{2,1,0:T(8,128)S(1)}, u32[]{:S(2)}, u32[]{:S(2)}) collective-permute-start(f32[4,24,128]{2,1,0:T(8,128)S(1)} %slice_add_fusion.1), channel_id=1, source_target_pairs={{32,0},{33,1},{34,2},{35,3},{36,4},{37,5},{38,6},{39,7},{40,8},{41... | collective-permute-start | bytes 147464 | tf_op jit(solution)/shard_map/ppermute | solution.py:572
  104.2 2.0 %copy-start.10 = (s32[2]{0:T(128)S(1)}, s32[2]{0:T(128)}, u32[]{:S(2)}) copy-start(s32[2]{0:T(128)} %param.15) | copy-start | bytes 28
  104.2 2.0 %copy-start.11 = (s32[2]{0:T(128)S(1)}, s32[2]{0:T(128)}, u32[]{:S(2)}) copy-start(s32[2]{0:T(128)} %param.16) | copy-start | bytes 28
  104.2 7.9 %collective-permute-start.9 = (f32[8,24,128]{2,1,0:T(8,128)S(1)}, f32[8,24,128]{2,1,0:T(8,128)S(1)}, u32[]{:S(2)}, u32[]{:S(2)}) collective-permute-start(f32[8,24,128]{2,1,0:T(8,128)S(1)} %slice_add_fusion), channel_id=1, source_target_pairs={{16,0},{17,1},{18,2},{19,3},{20,4},{21,5},{22,6},{23,7},{24,8},{25... | collective-permute-start | bytes 294920 | tf_op jit(solution)/shard_map/ppermute | solution.py:572
  124.6 20.9 %collective-permute-start.11 = (f32[8,24,128]{2,1,0:T(8,128)S(1)}, f32[8,24,128]{2,1,0:T(8,128)S(1)}, u32[]{:S(2)}, u32[]{:S(2)}) collective-permute-start(f32[8,24,128]{2,1,0:T(8,128)S(1)} %get-tuple-element.35), channel_id=1, source_target_pairs={{0,16},{1,17},{2,18},{3,19},{4,20},{5,21},{6,22},{7,23},{8,24},{9,... | collective-permute-start | bytes 294920 | tf_op jit(solution)/shard_map/ppermute | solution.py:572
  133.5 12.0 %collective-permute-start.12 = (f32[4,24,128]{2,1,0:T(8,128)S(1)}, f32[4,24,128]{2,1,0:T(8,128)S(1)}, u32[]{:S(2)}, u32[]{:S(2)}) collective-permute-start(f32[4,24,128]{2,1,0:T(8,128)S(1)} %get-tuple-element.36), channel_id=1, source_target_pairs={{0,32},{1,33},{2,34},{3,35},{4,36},{5,37},{6,38},{7,39},{8,40},{9,... | collective-permute-start | bytes 147464 | tf_op jit(solution)/shard_map/ppermute | solution.py:572
  145.5 11.8 %collective-permute-start.13 = (f32[20,24,128]{2,1,0:T(8,128)S(1)}, f32[20,24,128]{2,1,0:T(8,128)S(1)}, u32[]{:S(2)}, u32[]{:S(2)}) collective-permute-start(f32[20,24,128]{2,1,0:T(8,128)S(1)} %pad_maximum_fusion), channel_id=1, source_target_pairs={{0,1},{1,2},{2,3},{3,4},{4,5},{5,6},{6,7},{7,8},{8,9},{9,10},{10,1... | collective-permute-start | bytes 737288 | tf_op jit(solution)/shard_map/ppermute | solution.py:572

commit v4 on v3

--- a/solution.py
+++ b/solution.py
@@ -94,21 +94,64 @@
     out[...] = spectrum.reshape(NPY, KZ, ROWS * COLS)
 
 
-def scan_powers(place, ey, ez, power_out, weight_out, ends_out):
+def block_power(rate):
+    for _ in range(4):
+        rate = rate * rate
+    return rate
+
+
+def put_rows(ref, first, value):
+    for half in range(2):
+        for k in range(4):
+            rows = pl.ds(64 * half + first + k, 8, stride=8)
+            ref[rows, :] = value[8 * half : 8 * half + 8, 128 * k : 128 * k + 128]
+
+
+def take_rows(ref, first):
+    return jnp.concatenate(
+        [
+            jnp.concatenate(
+                [ref[pl.ds(64 * half + first + k, 8, stride=8), :] for half in range(2)], 0
+            )
+            for k in range(4)
+        ],
+        1,
+    )
+
+
+def pair_moments(core, own, other, ey, ez, out):
+    power = block_power(decay(ey[...], ez[...])[0])
+    upper = core[0] == 1
+    high = jnp.where(upper, own[...], other[...])
+    low = jnp.where(upper, other[...], own[...])
+    put_rows(out, 0, high[:KZ] + power * low[:KZ])
+    put_rows(out, 4, low[KZ:] + power * high[KZ:])
+
+
+def scan_chips(moments, ey, ez, out):
     rate, _ = decay(ey[...], ez[...])
-    power = rate
-    for _ in range(4):
+    power = block_power(rate)
+    power = power * power
+    right, left = take_rows(moments, 0), take_rows(moments, 4)
+    count = NPX // 2
+    row = lax.broadcasted_iota(jnp.int32, (count, NY), 0)
+    before, after = jnp.ones((count, NY), F32), jnp.ones((count, NY), F32)
+    step = 1
+    while step < count:
+        right = right + power * jnp.where(row >= step, rolled(right, step, 0), 0.0)
+        left = left + power * jnp.where(row < count - step, rolled(left, -step, 0), 0.0)
+        upper = row & step != 0
+        before = jnp.where(upper, before * power, before)
+        after = jnp.where(upper, after, after * power)
         power = power * power
-    before = jnp.ones((KZ, NY), F32)
-    after = before
-    for bit in range(5):
-        upper = (place[0] >> bit) % 2 == 1
-        power_out[bit] = power
-        weight_out[bit] = jnp.where(upper, before, after)
-        before, after = jnp.where(upper, before * power, before), jnp.where(upper, after, after * power)
-        power = power * power
-    ends_out[0] = before
-    ends_out[1] = after
+        step *= 2
+    across = power * rate
+    norm = rate / (1.0 - across * across)
+    right_total, left_total = right[count - 1 :], left[:1]
+    state = jnp.where(row >= 1, rolled(right, 1, 0), 0.0)
+    put_rows(out, 0, state - norm * (left_total - across * right_total) * before)
+    state = jnp.where(row < count - 1, rolled(left, -1, 0), 0.0)
+    put_rows(out, 4, state - norm * (right_total - across * left_total) * after)
 
 
 def forward_y(tiles, table_high, table_low, ey, ez, field_out, moment_out, merged):
@@ -134,16 +177,13 @@
     moment_out[KZ:] = last
 
 
-def back_y(field, totals, right, left, ends, table_high, table_low, ey, ez, tiles_out, solved):
+def back_y(core, field, other, states, table_high, table_low, ey, ez, tiles_out, solved):
     rate, scale = decay(ey[...], ez[...])
-    across = rate
-    for _ in range(9):
-        across = across * across
-    across = across * rate
-    norm = rate / (1.0 - across * across)
-    right_total, left_total = totals[:KZ], totals[KZ:]
-    state = right[...] - norm * (left_total - across * right_total) * ends[0]
-    left = left[...] - norm * (right_total - across * left_total) * ends[1]
+    power = block_power(rate)
+    upper = core[0] == 1
+    state, left = take_rows(states, 0), take_rows(states, 4)
+    state = jnp.where(upper, other[:KZ] + power * state, state)
+    left = jnp.where(upper, left, other[KZ:] + power * left)
     for row in range(ROWS):
         state = field[row * KZ : (row + 1) * KZ] + rate * state
         solved[row * KZ : (row + 1) * KZ] = state
@@ -572,6 +612,15 @@
     return lax.ppermute(x, ALL, pairs)
 
 
+def swapped(tiles):
+    return lax.all_to_all(tiles, "py", split_axis=0, concat_axis=0, tiled=True)
+
+
+def over_chips(rows):
+    tiles = rows.reshape(NPX // 2, 8, 128)
+    return lax.all_to_all(tiles, PX[:2], split_axis=0, concat_axis=0, tiled=True).reshape(rows.shape)
+
+
 def body(density, external, orbitals, anchors, weights, degrees):
     row_place = lax.axis_index(PX)
     col_place = lax.axis_index("py")
@@ -593,36 +642,28 @@
         shape(FRAG, 9, 8, 128),
         [pltpu.VMEM((2, 5, NORB * FRAG, 128), F32), pltpu.VMEM((3, 128, 128), F32)],
     )(orbitals.reshape(2, NORB * FRAG, FRAG * FRAG))
-    power, weight, ends = call(
-        scan_powers,
-        (shape(5, KZ, NY), shape(5, KZ, NY), shape(2, KZ, NY)),
-        smem=(0,),
-        count=3,
-    )(row_place.reshape(1).astype(jnp.int32), ey, ez)
-
     tiles = call(forward_z, shape(NPY, KZ, ROWS * COLS), count=2)(density, sine_z)
-    tiles = lax.all_to_all(tiles, "py", split_axis=0, concat_axis=0, tiled=True)
-    field, totals = call(
+    tiles = swapped(tiles)
+    field, moments = call(
         forward_y,
         (shape(ROWS * KZ, NY), shape(2 * KZ, NY)),
         [pltpu.VMEM((ROWS * KZ, NY), F32)],
         count=5,
     )(tiles, *sine_y, ey, ez)
 
-    right, left = jnp.zeros((KZ, NY), F32), jnp.zeros((KZ, NY), F32)
-    for bit, partner in enumerate((1, 2, 4, 8, 24)):
-        pairs = [(p * NPY + q, (p ^ partner) * NPY + q) for p in range(NPX) for q in range(NPY)]
-        got = lax.ppermute(totals, ALL, pairs)
-        upper = (row_place >> bit) % 2 == 1
-        high, low = jnp.where(upper, totals, got), jnp.where(upper, got, totals)
-        right = right + jnp.where(upper, weight[bit] * got[:KZ], 0.0)
-        left = left + jnp.where(upper, 0.0, weight[bit] * got[KZ:])
-        totals = jnp.concatenate([high[:KZ] + power[bit] * low[:KZ], low[KZ:] + power[bit] * high[KZ:]])
-
-    tiles = call(back_y, shape(NPY, KZ, ROWS * COLS), [pltpu.VMEM((ROWS * KZ, NY), F32)], count=9)(
-        field, totals, right, left, ends, *sine_y, ey, ez
-    )
-    tiles = lax.all_to_all(tiles, "py", split_axis=0, concat_axis=0, tiled=True)
+    core = lax.axis_index("px_2").reshape(1).astype(jnp.int32)
+    chip = row_place // 2
+    other = lax.ppermute(moments, "px_2", [(0, 1), (1, 0)])
+    chips = call(pair_moments, shape(128, 128), smem=(0,), count=5)(core, moments, other, ey, ez)
+    chips = over_chips(chips)
+    chip_ez = lax.dynamic_slice(jnp.asarray(EIGEN_Z), (col_place * KZ + chip, 0), (1, 1))
+    chips = call(scan_chips, shape(128, 128), count=3)(chips, ey, chip_ez)
+    states = over_chips(chips)
+
+    tiles = call(
+        back_y, shape(NPY, KZ, ROWS * COLS), [pltpu.VMEM((ROWS * KZ, NY), F32)], smem=(0,), count=8
+    )(core, field, other, states, *sine_y, ey, ez)
+    tiles = swapped(tiles)
     groups = (8, 8, 4)
     grid = [pltpu.VMEM((2, ROWS, PADDED, 128), F32)]
     hartree_field, beside = call(

time: 161 us -> 165 us (1.025)
  the two profiles are of different devices: /device:TPU:38 before, /device:TPU:10 now
where the time goes in v4:
time: 165 us; the launch traced here: 164 us
  starting transfers between devices  71.8 us (44%)
  waiting for transfers between devices  39.6 us (24%)
  Pallas kernels  30.3 us (18%)
  blocking collectives  15.6 us (9%)
  local copies, waits for them, and re-layouts  5.86 us (4%)
    ppermute x9, starting transfers between devices, moved(): return lax.ppermute(x, ALL, pairs)  38.1 us
    ppermute x9, waiting for transfers between devices, moved(): return lax.ppermute(x, ALL, pairs)  25.7 us
    all_to_all x2, starting transfers between devices, swapped(): return lax.all_to_all(tiles, 'py', split_axis=0, concat_axis=0, tiled=True)  18 us
    all_to_all x1, blocking collectives, over_chips(): lax.all_to_all(tiles, PX[:2], split_axis=0, concat_axis=0, tiled=True)  15.6 us
    pallas_call x1, Pallas kernels, body(): call(filter_fragments, [shape(FRAG, 9, 8, 128), shape(8, 128)] + [shape(n...  12.4 us
    all_to_all x1, waiting for transfers between devices, over_chips(): lax.all_to_all(tiles, PX[:2], split_axis=0, concat_axis=0, tiled=True)  10.4 us
    all_to_all x1, starting transfers between devices, over_chips(): lax.all_to_all(tiles, PX[:2], split_axis=0, concat_axis=0, tiled=True)  8.78 us
    ppermute x1, starting transfers between devices, body(): other = lax.ppermute(moments, 'px_2', [(0, 1), (1, 0)])  6.85 us
  transfers between devices with their start and end apart: 13, of which 10 were waited for; matrix products, arithmetic and copies ran while one was open for 1% of the time, Pallas kernels for 5%

profile of v4, /device:TPU:10, one launch (start us, length us, event | category | flops | bytes accessed | tf_op | source)
XLA Modules:
  0.0 164.1 jit_solution(15649282925725573465)
XLA Ops:
  0.6 0.0 copy-start.3
  0.6 0.9 copy-done.3
  1.6 0.0 copy-start.6
  1.6 1.0 copy-done.6
  2.6 1.2 shard_map.130
  3.8 0.0 copy-start.1
  3.8 0.0 copy-start.2
  3.8 10.4 %all-to-all-start = ((f32[16,16,512]{2,1,0:T(8,128)}), f32[16,16,512]{2,1,0:T(8,128)S(1)}, u32[]{:S(2)}, u32[]{:S(2)}) async-start(f32[16,16,512]{2,1,0:T(8,128)} %shard_map.130), calls=%async_computation | async-start | bytes 1048576 | tf_op jit(solution)/shard_map/all_to_all | solution.py:616
  14.2 0.1 pad_add_fusion.2
  14.3 0.6 copy-done.9
  14.9 0.1 reshape.34
  15.0 1.9 %collective-permute-start = (s32[8]{0:T(128)S(1)}, s32[8]{0:T(128)S(1)}, u32[]{:S(2)}, u32[]{:S(2)}) collective-permute-start(s32[8]{0:T(128)S(1)} %get-tuple-element.32), channel_id=1, source_target_pairs={{0,16},{1,17},{2,18},{3,19},{4,20},{5,21},{6,22},{7,23},{8,24},{9,... | collective-permute-start | bytes 104 | tf_op jit(solution)/shard_map/ppermute | solution.py:612
  16.9 8.2 %collective-permute-start.1 = (s32[8]{0:T(128)S(1)}, s32[8]{0:T(128)S(1)}, u32[]{:S(2)}, u32[]{:S(2)}) collective-permute-start(s32[8]{0:T(128)S(1)} %get-tuple-element.32), channel_id=1, source_target_pairs={{0,32},{1,33},{2,34},{3,35},{4,36},{5,37},{6,38},{7,39},{8,40},{9,... | collective-permute-start | bytes 104 | tf_op jit(solution)/shard_map/ppermute | solution.py:612
  25.1 0.7 constant_dynamic-slice_fusion.1.ez
  25.9 0.0 collective-permute-done
  25.9 1.4 collective-permute-done.1
  27.3 0.9 all-to-all-done.tiles
  28.2 0.0 copy-done.1
  28.2 0.0 copy-done.2
  28.2 0.0 copy-done.8
  28.2 0.9 shard_map.131
  29.1 6.9 %collective-permute-start.3 = (f32[32,512]{1,0:T(8,128)S(1)}, f32[32,512]{1,0:T(8,128)S(1)}, u32[]{:S(2)}, u32[]{:S(2)}) collective-permute-start(f32[32,512]{1,0:T(8,128)S(1)} %get-tuple-element.20.own), channel_id=1, source_target_pairs={{0,16},{16,0},{1,17},{17,1},{2,18},{18,2},{3,19},{19,3},{4,20},{20... | collective-permute-start | bytes 196616 | tf_op jit(solution)/shard_map/ppermute | solution.py:656
  36.0 0.9 collective-permute-done.3.other
  36.8 0.7 shard_map.132
  37.6 8.8 %all-to-all-start.1 = ((f32[16,8,128]{2,1,0:T(8,128)}), f32[16,8,128]{2,1,0:T(8,128)S(1)}, u32[]{:S(2)}, u32[]{:S(2)}) async-start(f32[16,8,128]{2,1,0:T(8,128)} %bitcast.8), calls=%async_computation.1 | async-start | bytes 131072 | tf_op jit(solution)/shard_map/all_to_all | solution.py:621
  46.4 1.2 constant_dynamic-slice_fusion.ez
  47.6 10.4 %all-to-all-done.1 = f32[16,8,128]{2,1,0:T(8,128)S(1)} async-done(((f32[16,8,128]{2,1,0:T(8,128)}), f32[16,8,128]{2,1,0:T(8,128)S(1)}, u32[]{:S(2)}, u32[]{:S(2)}) %all-to-all-start.1) | async-done | bytes 65568 | tf_op jit(solution)/shard_map/all_to_all | solution.py:621
  58.0 0.8 shard_map.133
  58.8 15.6 %all_to_all.20 = f32[16,8,128]{2,1,0:T(8,128)S(1)} all-to-all(f32[16,8,128]{2,1,0:T(8,128)S(1)} %bitcast.18), channel_id=1, replica_groups=mesh['px_0'=8,'px_1'=2,'px_2'=2,'py'=16] {'px_0','px_1'}, dimensions={0} | all-to-all | bytes 131072 | tf_op jit(solution)/shard_map/all_to_all | solution.py:621
  74.4 1.9 %shard_map.134 = f32[16,16,512]{2,1,0:T(8,128)} custom-call(s32[1]{0:T(128)} %bitcast.7.core, f32[256,512]{1,0:T(8,128)S(1)} %get-tuple-element.19.field, f32[32,512]{1,0:T(8,128)S(1)} %collective-permute-done.3.other, f32[128,128]{1,0:T(8,128)S(1)} %bitcast.16, bf16[512,512]{1,0:T(8,128)(2,1)S(1)} %copy-done.2, bf16[512,512]{1,0:T(8,128)(2,1)S(1)} %copy-done.1, ...), custom_call_target="tpu_custom_call" | custom-call | tf_op jit(solution)/shard_map/pallas_call | solution.py:663
  76.3 7.6 %all-to-all-start.3 = ((f32[16,16,512]{2,1,0:T(8,128)}), f32[16,16,512]{2,1,0:T(8,128)S(1)}, u32[]{:S(2)}, u32[]{:S(2)}) async-start(f32[16,16,512]{2,1,0:T(8,128)} %shard_map.134), calls=%async_computation.3 | async-start | bytes 1048576 | tf_op jit(solution)/shard_map/all_to_all | solution.py:616
  83.9 3.4 %collective-permute-start.2 = (s32[3,8]{1,0:T(4,128)S(1)}, s32[3,8]{1,0:T(4,128)S(1)}, u32[]{:S(2)}, u32[]{:S(2)}) collective-permute-start(s32[3,8]{1,0:T(4,128)S(1)} %pad_add_fusion.1), channel_id=1, source_target_pairs={{0,1},{1,2},{2,3},{3,4},{4,5},{5,6},{6,7},{7,8},{8,9},{9,10},{10,1... | collective-permute-start | bytes 296 | tf_op jit(solution)/shard_map/ppermute | solution.py:612
  87.3 6.7 %collective-permute-done.2 = s32[3,8]{1,0:T(4,128)S(1)} collective-permute-done((s32[3,8]{1,0:T(4,128)S(1)}, s32[3,8]{1,0:T(4,128)S(1)}, u32[]{:S(2)}, u32[]{:S(2)}) %collective-permute-start.2) | collective-permute-done | bytes 128 | tf_op jit(solution)/shard_map/ppermute | solution.py:612
  94.0 0.1 reshape.35.places
  94.0 1.8 %all-to-all-done.3.tiles = f32[16,16,512]{2,1,0:T(8,128)S(1)} async-done(((f32[16,16,512]{2,1,0:T(8,128)}), f32[16,16,512]{2,1,0:T(8,128)S(1)}, u32[]{:S(2)}, u32[]{:S(2)}) %all-to-all-start.3) | async-done | bytes 524320 | tf_op jit(solution)/shard_map/all_to_all | solution.py:616
  95.8 0.0 copy-done
  95.8 0.0 copy-done.4
  95.8 2.2 %shard_map.135 = (f32[16,32,256]{2,1,0:T(8,128)}, f32[20,24,128]{2,1,0:T(8,128)S(1)}) custom-call(s32[36]{0:T(128)S(1)} %reshape.35.places, f32[16,16,512]{2,1,0:T(8,128)S(1)} %all-to-all-done.3.tiles, f32[16,32,256]{2,1,0:T(8,128)S(1)} %copy-done, bf16[2,256,256]{2,1,0:T(8,128)(2,1)S(1)} %copy-done.4), custom_call_target="tpu_custom_call" | custom-call | tf_op jit(solution)/shard_map/pallas_call | solution.py:669
  98.0 3.2 %collective-permute-start.4 = (f32[20,24,128]{2,1,0:T(8,128)S(1)}, f32[20,24,128]{2,1,0:T(8,128)S(1)}, u32[]{:S(2)}, u32[]{:S(2)}) collective-permute-start(f32[20,24,128]{2,1,0:T(8,128)S(1)} %get-tuple-element.23), channel_id=1, source_target_pairs={{1,0},{2,1},{3,2},{4,3},{5,4},{6,5},{7,6},{8,7},{9,8},{10,9},{11,1... | collective-permute-start | bytes 737288 | tf_op jit(solution)/shard_map/ppermute | solution.py:612
  101.3 0.1 slice_reduce_fusion
  101.4 1.0 copy-done.7
  102.4 1.3 shard_map.136
  103.7 2.5 %collective-permute-done.4.refs_1_ = f32[20,24,128]{2,1,0:T(8,128)S(1)} collective-permute-done((f32[20,24,128]{2,1,0:T(8,128)S(1)}, f32[20,24,128]{2,1,0:T(8,128)S(1)}, u32[]{:S(2)}, u32[]{:S(2)}) %collective-permute-start.4) | collective-permute-done | bytes 245792 | tf_op jit(solution)/shard_map/ppermute | solution.py:612
  106.2 3.4 %collective-permute-start.6 = (f32[4,24,128]{2,1,0:T(8,128)S(1)}, f32[4,24,128]{2,1,0:T(8,128)S(1)}, u32[]{:S(2)}, u32[]{:S(2)}) collective-permute-start(f32[4,24,128]{2,1,0:T(8,128)S(1)} %slice_add_fusion.1), channel_id=1, source_target_pairs={{32,0},{33,1},{34,2},{35,3},{36,4},{37,5},{38,6},{39,7},{40,8},{41... | collective-permute-start | bytes 147464 | tf_op jit(solution)/shard_map/ppermute | solution.py:612
  109.7 0.0 copy-start.10
  109.7 0.0 copy-start.11
  109.7 3.7 %collective-permute-start.5 = (f32[8,24,128]{2,1,0:T(8,128)S(1)}, f32[8,24,128]{2,1,0:T(8,128)S(1)}, u32[]{:S(2)}, u32[]{:S(2)}) collective-permute-start(f32[8,24,128]{2,1,0:T(8,128)S(1)} %slice_add_fusion), channel_id=1, source_target_pairs={{16,0},{17,1},{18,2},{19,3},{20,4},{21,5},{22,6},{23,7},{24,8},{25... | collective-permute-start | bytes 294920 | tf_op jit(solution)/shard_map/ppermute | solution.py:612
  113.4 0.0 copy-done.10
  113.5 0.0 copy-done.11
  113.5 0.1 pad_add_fusion.3.meta
  113.5 0.0 copy-done.5
  113.5 2.0 %shard_map.137.refs_4_ = f32[24,9,8,128]{3,2,1,0:T(8,128)S(1)} custom-call(f32[2,192,576]{2,1,0:T(8,128)S(1)} %bitcast.15), custom_call_target="tpu_custom_call" | custom-call | tf_op jit(solution)/shard_map/pallas_call | solution.py:640
  115.6 1.1 collective-permute-done.6.refs_3_
  116.6 0.0 collective-permute-done.5.refs_2_
  116.7 12.4 %shard_map.138 = (f32[24,9,8,128]{3,2,1,0:T(8,128)S(1)}, f32[8,128]{1,0:T(8,128)S(1)}, f32[8,24,128]{2,1,0:T(8,128)S(1)}, f32[8,24,128]{2,1,0:T(8,128)S(1)}, f32[4,24,128]{2,1,0:T(8,128)S(1)}) custom-call(s32[8]{0:T(128)S(1)} %pad_add_fusion.3.meta, f32[8,24,128]{2,1,0:T(8,128)S(1)} %get-tuple-element.22.refs_0_, ...), custom_call_target="tpu_custom_call" | custom-call | tf_op jit(solution)/shard_map/pallas_call | solution.py:678
  129.1 8.7 %collective-permute-start.7 = (f32[8,24,128]{2,1,0:T(8,128)S(1)}, f32[8,24,128]{2,1,0:T(8,128)S(1)}, u32[]{:S(2)}, u32[]{:S(2)}) collective-permute-start(f32[8,24,128]{2,1,0:T(8,128)S(1)} %get-tuple-element.29), channel_id=1, source_target_pairs={{0,16},{1,17},{2,18},{3,19},{4,20},{5,21},{6,22},{7,23},{8,24},{9,... | collective-permute-start | bytes 294920 | tf_op jit(solution)/shard_map/ppermute | solution.py:612
  137.8 3.6 %collective-permute-start.8 = (f32[4,24,128]{2,1,0:T(8,128)S(1)}, f32[4,24,128]{2,1,0:T(8,128)S(1)}, u32[]{:S(2)}, u32[]{:S(2)}) collective-permute-start(f32[4,24,128]{2,1,0:T(8,128)S(1)} %get-tuple-element.30), channel_id=1, source_target_pairs={{0,32},{1,33},{2,34},{3,35},{4,36},{5,37},{6,38},{7,39},{8,40},{9,... | collective-permute-start | bytes 147464 | tf_op jit(solution)/shard_map/ppermute | solution.py:612
  141.4 8.2 %collective-permute-done.8.third = f32[4,24,128]{2,1,0:T(8,128)S(1)} collective-permute-done((f32[4,24,128]{2,1,0:T(8,128)S(1)}, f32[4,24,128]{2,1,0:T(8,128)S(1)}, u32[]{:S(2)}, u32[]{:S(2)}) %collective-permute-start.8) | collective-permute-done | bytes 49184 | tf_op jit(solution)/shard_map/ppermute | solution.py:612
  149.6 0.0 collective-permute-done.7.second
  149.6 1.9 %collective-permute-start.9 = (f32[20,24,128]{2,1,0:T(8,128)S(1)}, f32[20,24,128]{2,1,0:T(8,128)S(1)}, u32[]{:S(2)}, u32[]{:S(2)}) collective-permute-start(f32[20,24,128]{2,1,0:T(8,128)S(1)} %pad_maximum_fusion), channel_id=1, source_target_pairs={{0,1},{1,2},{2,3},{3,4},{4,5},{5,6},{6,7},{7,8},{8,9},{9,10},{10,1... | collective-permute-start | bytes 737288 | tf_op jit(solution)/shard_map/ppermute | solution.py:612
  151.6 2.9 %shard_map.139 = f32[2,192,576]{2,1,0:T(8,128)} custom-call(f32[24,9,8,128]{3,2,1,0:T(8,128)S(1)} %get-tuple-element.26.planes, f32[8,128]{1,0:T(8,128)S(1)} %get-tuple-element.27.scale), custom_call_target="tpu_custom_call" | custom-call | tf_op jit(solution)/shard_map/pallas_call | solution.py:694
  154.5 1.5 shard_map.140.owned
  156.0 5.7 %collective-permute-done.9.beside = f32[20,24,128]{2,1,0:T(8,128)S(1)} collective-permute-done((f32[20,24,128]{2,1,0:T(8,128)S(1)}, f32[20,24,128]{2,1,0:T(8,128)S(1)}, u32[]{:S(2)}, u32[]{:S(2)}) %collective-permute-start.9) | collective-permute-done | bytes 245792 | tf_op jit(solution)/shard_map/ppermute | solution.py:612
  161.8 2.3 %shard_map.141 = f32[16,32,256]{2,1,0:T(8,128)} custom-call(s32[36]{0:T(128)S(1)} %reshape.35.places, f32[16,32,256]{2,1,0:T(8,128)S(1)} %shard_map.140.owned, f32[20,24,128]{2,1,0:T(8,128)S(1)} %collective-permute-done.9.beside), custom_call_target="tpu_custom_call" | custom-call | tf_op jit(solution)/shard_map/pallas_call | solution.py:701
  (14 shorter events, 0.1 us)
Async XLA Ops:
  0.6 1.0 copy-start.3
  1.6 1.0 copy-start.6
  3.8 24.4 %copy-start.1 = (bf16[512,512]{1,0:T(8,128)(2,1)S(1)}, bf16[512,512]{1,0:T(8,128)(2,1)}, u32[]{:S(2)}) copy-start(bf16[512,512]{1,0:T(8,128)(2,1)} %constant.56.clone.table_low) | copy-start | bytes 1572868
  3.8 24.4 %copy-start.2 = (bf16[512,512]{1,0:T(8,128)(2,1)S(1)}, bf16[512,512]{1,0:T(8,128)(2,1)}, u32[]{:S(2)}) copy-start(bf16[512,512]{1,0:T(8,128)(2,1)} %constant.55.clone.table_high) | copy-start | bytes 1572868
  3.8 24.3 %all-to-all-start = ((f32[16,16,512]{2,1,0:T(8,128)}), f32[16,16,512]{2,1,0:T(8,128)S(1)}, u32[]{:S(2)}, u32[]{:S(2)}) async-start(f32[16,16,512]{2,1,0:T(8,128)} %shard_map.130), calls=%async_computation | async-start | bytes 1048576 | tf_op jit(solution)/shard_map/all_to_all | solution.py:616
  14.2 0.7 copy-start.9
  15.0 10.9 %collective-permute-start = (s32[8]{0:T(128)S(1)}, s32[8]{0:T(128)S(1)}, u32[]{:S(2)}, u32[]{:S(2)}) collective-permute-start(s32[8]{0:T(128)S(1)} %get-tuple-element.32), channel_id=1, source_target_pairs={{0,16},{1,17},{2,18},{3,19},{4,20},{5,21},{6,22},{7,23},{8,24},{9,... | collective-permute-start | bytes 104 | tf_op jit(solution)/shard_map/ppermute | solution.py:612
  16.9 10.4 %collective-permute-start.1 = (s32[8]{0:T(128)S(1)}, s32[8]{0:T(128)S(1)}, u32[]{:S(2)}, u32[]{:S(2)}) collective-permute-start(s32[8]{0:T(128)S(1)} %get-tuple-element.32), channel_id=1, source_target_pairs={{0,32},{1,33},{2,34},{3,35},{4,36},{5,37},{6,38},{7,39},{8,40},{9,... | collective-permute-start | bytes 104 | tf_op jit(solution)/shard_map/ppermute | solution.py:612
  27.3 0.9 copy-start.8
  29.1 7.7 %collective-permute-start.3 = (f32[32,512]{1,0:T(8,128)S(1)}, f32[32,512]{1,0:T(8,128)S(1)}, u32[]{:S(2)}, u32[]{:S(2)}) collective-permute-start(f32[32,512]{1,0:T(8,128)S(1)} %get-tuple-element.20.own), channel_id=1, source_target_pairs={{0,16},{16,0},{1,17},{17,1},{2,18},{18,2},{3,19},{19,3},{4,20},{20... | collective-permute-start | bytes 196616 | tf_op jit(solution)/shard_map/ppermute | solution.py:656
  37.6 20.4 %all-to-all-start.1 = ((f32[16,8,128]{2,1,0:T(8,128)}), f32[16,8,128]{2,1,0:T(8,128)S(1)}, u32[]{:S(2)}, u32[]{:S(2)}) async-start(f32[16,8,128]{2,1,0:T(8,128)} %bitcast.8), calls=%async_computation.1 | async-start | bytes 131072 | tf_op jit(solution)/shard_map/all_to_all | solution.py:621
  76.3 19.5 %copy-start = (f32[16,32,256]{2,1,0:T(8,128)S(1)}, f32[16,32,256]{2,1,0:T(8,128)}, u32[]{:S(2)}) copy-start(f32[16,32,256]{2,1,0:T(8,128)} %external.3) | copy-start | bytes 1572868
  76.3 19.5 %copy-start.4 = (bf16[2,256,256]{2,1,0:T(8,128)(2,1)S(1)}, bf16[2,256,256]{2,1,0:T(8,128)(2,1)}, u32[]{:S(2)}) copy-start(bf16[2,256,256]{2,1,0:T(8,128)(2,1)} %constant.57.clone.table) | copy-start | bytes 786436
  76.3 19.5 %all-to-all-start.3 = ((f32[16,16,512]{2,1,0:T(8,128)}), f32[16,16,512]{2,1,0:T(8,128)S(1)}, u32[]{:S(2)}, u32[]{:S(2)}) async-start(f32[16,16,512]{2,1,0:T(8,128)} %shard_map.134), calls=%async_computation.3 | async-start | bytes 1048576 | tf_op jit(solution)/shard_map/all_to_all | solution.py:616
  83.9 10.1 %collective-permute-start.2 = (s32[3,8]{1,0:T(4,128)S(1)}, s32[3,8]{1,0:T(4,128)S(1)}, u32[]{:S(2)}, u32[]{:S(2)}) collective-permute-start(s32[3,8]{1,0:T(4,128)S(1)} %pad_add_fusion.1), channel_id=1, source_target_pairs={{0,1},{1,2},{2,3},{3,4},{4,5},{5,6},{6,7},{7,8},{8,9},{9,10},{10,1... | collective-permute-start | bytes 296 | tf_op jit(solution)/shard_map/ppermute | solution.py:612
  98.0 15.5 %copy-start.5 = (f32[2,8,24,576]{3,2,1,0:T(8,128)S(1)}, f32[2,8,24,576]{3,2,1,0:T(8,128)}, u32[]{:S(2)}) copy-start(f32[2,8,24,576]{3,2,1,0:T(8,128)} %param.13) | copy-start | bytes 2654212
  98.0 8.2 %collective-permute-start.4 = (f32[20,24,128]{2,1,0:T(8,128)S(1)}, f32[20,24,128]{2,1,0:T(8,128)S(1)}, u32[]{:S(2)}, u32[]{:S(2)}) collective-permute-start(f32[20,24,128]{2,1,0:T(8,128)S(1)} %get-tuple-element.23), channel_id=1, source_target_pairs={{1,0},{2,1},{3,2},{4,3},{5,4},{6,5},{7,6},{8,7},{9,8},{10,9},{11,1... | collective-permute-start | bytes 737288 | tf_op jit(solution)/shard_map/ppermute | solution.py:612
  101.4 1.0 copy-start.7
  106.2 10.4 %collective-permute-start.6 = (f32[4,24,128]{2,1,0:T(8,128)S(1)}, f32[4,24,128]{2,1,0:T(8,128)S(1)}, u32[]{:S(2)}, u32[]{:S(2)}) collective-permute-start(f32[4,24,128]{2,1,0:T(8,128)S(1)} %slice_add_fusion.1), channel_id=1, source_target_pairs={{32,0},{33,1},{34,2},{35,3},{36,4},{37,5},{38,6},{39,7},{40,8},{41... | collective-permute-start | bytes 147464 | tf_op jit(solution)/shard_map/ppermute | solution.py:612
  109.7 3.8 %copy-start.10 = (s32[2]{0:T(128)S(1)}, s32[2]{0:T(128)}, u32[]{:S(2)}) copy-start(s32[2]{0:T(128)} %param.15) | copy-start | bytes 28
  109.7 3.8 %copy-start.11 = (s32[2]{0:T(128)S(1)}, s32[2]{0:T(128)}, u32[]{:S(2)}) copy-start(s32[2]{0:T(128)} %param.16) | copy-start | bytes 28
  109.7 6.9 %collective-permute-start.5 = (f32[8,24,128]{2,1,0:T(8,128)S(1)}, f32[8,24,128]{2,1,0:T(8,128)S(1)}, u32[]{:S(2)}, u32[]{:S(2)}) collective-permute-start(f32[8,24,128]{2,1,0:T(8,128)S(1)} %slice_add_fusion), channel_id=1, source_target_pairs={{16,0},{17,1},{18,2},{19,3},{20,4},{21,5},{22,6},{23,7},{24,8},{25... | collective-permute-start | bytes 294920 | tf_op jit(solution)/shard_map/ppermute | solution.py:612
  129.1 20.6 %collective-permute-start.7 = (f32[8,24,128]{2,1,0:T(8,128)S(1)}, f32[8,24,128]{2,1,0:T(8,128)S(1)}, u32[]{:S(2)}, u32[]{:S(2)}) collective-permute-start(f32[8,24,128]{2,1,0:T(8,128)S(1)} %get-tuple-element.29), channel_id=1, source_target_pairs={{0,16},{1,17},{2,18},{3,19},{4,20},{5,21},{6,22},{7,23},{8,24},{9,... | collective-permute-start | bytes 294920 | tf_op jit(solution)/shard_map/ppermute | solution.py:612
  137.8 11.9 %collective-permute-start.8 = (f32[4,24,128]{2,1,0:T(8,128)S(1)}, f32[4,24,128]{2,1,0:T(8,128)S(1)}, u32[]{:S(2)}, u32[]{:S(2)}) collective-permute-start(f32[4,24,128]{2,1,0:T(8,128)S(1)} %get-tuple-element.30), channel_id=1, source_target_pairs={{0,32},{1,33},{2,34},{3,35},{4,36},{5,37},{6,38},{7,39},{8,40},{9,... | collective-permute-start | bytes 147464 | tf_op jit(solution)/shard_map/ppermute | solution.py:612
  149.6 12.1 %collective-permute-start.9 = (f32[20,24,128]{2,1,0:T(8,128)S(1)}, f32[20,24,128]{2,1,0:T(8,128)S(1)}, u32[]{:S(2)}, u32[]{:S(2)}) collective-permute-start(f32[20,24,128]{2,1,0:T(8,128)S(1)} %pad_maximum_fusion), channel_id=1, source_target_pairs={{0,1},{1,2},{2,3},{3,4},{4,5},{5,6},{6,7},{7,8},{8,9},{9,10},{10,1... | collective-permute-start | bytes 737288 | tf_op jit(solution)/shard_map/ppermute | solution.py:612

commit v5 on v4

--- a/solution.py
+++ b/solution.py
@@ -439,11 +439,11 @@
 
         def chunk(number, carry):
             behind, here = list(carry[:9]), list(carry[9:])
-            for k4 in range(8):
-                x = 8 * number + k4
+            for k4 in range(24):
+                x = 24 * number + k4
                 ahead_x = jnp.minimum(x + 1, FRAG - 1)
                 ahead = [source[ahead_x, k] for k in range(9)]
-                if k4 == 7:
+                if k4 == 23:
                     ahead = [jnp.where(x + 1 < FRAG, v, 0.0) for v in ahead]
                 for k in range(9):
                     yi, zi = divmod(k, 3)
@@ -478,7 +478,7 @@
             return tuple(behind + here)
 
         zero = [jnp.zeros((8, 128), F32)] * 9
-        lax.fori_loop(0, 3, chunk, tuple(zero + [source[0, k] for k in range(9)]))
+        lax.fori_loop(0, 1, chunk, tuple(zero + [source[0, k] for k in range(9)]))
 
     apply(start, other, initial=True)
     apply(other, out, earlier=start, even=True)
@@ -634,7 +634,8 @@
     sine_z = jnp.asarray(SINE_Z)
     ey = jnp.asarray(EIGEN_Y)
     ez = lax.dynamic_slice(jnp.asarray(EIGEN_Z), (col_place * KZ, 0), (KZ, 1))
-    ez, above = lax.optimization_barrier((ez, above))
+    chip_ez = lax.dynamic_slice(jnp.asarray(EIGEN_Z), (col_place * KZ + row_place // 2, 0), (1, 1))
+    ez, chip_ez, above = lax.optimization_barrier((ez, chip_ez, above))
     places = jnp.stack([above, moved(above, 0, 1)], 1)[:, :, :6].reshape(36)
 
     planes = call(
@@ -652,11 +653,9 @@
     )(tiles, *sine_y, ey, ez)
 
     core = lax.axis_index("px_2").reshape(1).astype(jnp.int32)
-    chip = row_place // 2
     other = lax.ppermute(moments, "px_2", [(0, 1), (1, 0)])
     chips = call(pair_moments, shape(128, 128), smem=(0,), count=5)(core, moments, other, ey, ez)
     chips = over_chips(chips)
-    chip_ez = lax.dynamic_slice(jnp.asarray(EIGEN_Z), (col_place * KZ + chip, 0), (1, 1))
     chips = call(scan_chips, shape(128, 128), count=3)(chips, ey, chip_ez)
     states = over_chips(chips)
 

time: 165 us -> 162 us (0.982)
  blocking collectives: 15.6 us -> 35.7 us
  waiting for transfers between devices: 39.6 us -> 25.9 us
  starting transfers between devices: 71.8 us -> 63.7 us
    all_to_all x1 -> x2, blocking collectives: 15.6 us -> 35.7 us  [over_chips(): lax.all_to_all(tiles, PX[:2], split_axis=0, concat_axis=0, tiled=True)]
    all_to_all x1 -> x0, waiting for transfers between devices: 10.4 us -> none  [over_chips(): lax.all_to_all(tiles, PX[:2], split_axis=0, concat_axis=0, tiled=True)]
    all_to_all x1 -> x0, starting transfers between devices: 8.78 us -> none  [over_chips(): lax.all_to_all(tiles, PX[:2], split_axis=0, concat_axis=0, tiled=True)]
    ppermute x9, waiting for transfers between devices: 25.7 us -> 22.3 us  [moved(): return lax.ppermute(x, ALL, pairs)]
  transfers between devices with their start and end apart: 13 -> 12, of which waited for: 10 -> 9; matrix products, arithmetic and copies ran while one was open for 1% -> 1% of each run, Pallas kernels for 5% -> 5%
where the time goes in v5:
time: 162 us
  starting transfers between devices  63.7 us (39%)
  blocking collectives  35.7 us (22%)
  Pallas kernels  29.5 us (18%)
  waiting for transfers between devices  25.9 us (16%)
  local copies, waits for them, and re-layouts  5.86 us (4%)
    ppermute x9, starting transfers between devices, moved(): return lax.ppermute(x, ALL, pairs)  38.9 us
    all_to_all x2, blocking collectives, over_chips(): lax.all_to_all(tiles, PX[:2], split_axis=0, concat_axis=0, tiled=True)  35.7 us
    ppermute x9, waiting for transfers between devices, moved(): return lax.ppermute(x, ALL, pairs)  22.3 us
    all_to_all x2, starting transfers between devices, swapped(): return lax.all_to_all(tiles, 'py', split_axis=0, concat_axis=0, tiled=True)  18 us
    pallas_call x1, Pallas kernels, body(): call(filter_fragments, [shape(FRAG, 9, 8, 128), shape(8, 128)] + [shape(n...  12.2 us
    ppermute x1, starting transfers between devices, body(): other = lax.ppermute(moments, 'px_2', [(0, 1), (1, 0)])  6.85 us
    unnamed x24, local copies, waits for them, and re-layouts  3.66 us
  transfers between devices with their start and end apart: 12, of which 9 were waited for; matrix products, arithmetic and copies ran while one was open for 1% of the time, Pallas kernels for 5%

profile of v5, /device:TPU:10, one launch (start us, length us, event | category | flops | bytes accessed | tf_op | source)
XLA Modules:
  0.0 161.7 jit_solution(7152098625505039264)
XLA Ops:
  0.6 0.0 copy-start.3
  0.6 0.9 copy-done.3
  1.6 0.0 copy-start.6
  1.6 1.0 copy-done.6
  2.6 1.2 shard_map.130
  3.8 0.0 copy-start.1
  3.8 0.0 copy-start.2
  3.8 10.4 %all-to-all-start = ((f32[16,16,512]{2,1,0:T(8,128)}), f32[16,16,512]{2,1,0:T(8,128)S(1)}, u32[]{:S(2)}, u32[]{:S(2)}) async-start(f32[16,16,512]{2,1,0:T(8,128)} %shard_map.130), calls=%async_computation | async-start | bytes 1048576 | tf_op jit(solution)/shard_map/all_to_all | solution.py:616
  14.2 0.0 copy-start.9
  14.2 0.1 pad_add_fusion.2
  14.3 0.6 copy-done.9
  14.9 0.1 reshape.34
  15.0 1.9 %collective-permute-start = (s32[8]{0:T(128)S(1)}, s32[8]{0:T(128)S(1)}, u32[]{:S(2)}, u32[]{:S(2)}) collective-permute-start(s32[8]{0:T(128)S(1)} %get-tuple-element.34), channel_id=1, source_target_pairs={{0,16},{1,17},{2,18},{3,19},{4,20},{5,21},{6,22},{7,23},{8,24},{9,... | collective-permute-start | bytes 104 | tf_op jit(solution)/shard_map/ppermute | solution.py:612
  16.9 8.2 %collective-permute-start.1 = (s32[8]{0:T(128)S(1)}, s32[8]{0:T(128)S(1)}, u32[]{:S(2)}, u32[]{:S(2)}) collective-permute-start(s32[8]{0:T(128)S(1)} %get-tuple-element.34), channel_id=1, source_target_pairs={{0,32},{1,33},{2,34},{3,35},{4,36},{5,37},{6,38},{7,39},{8,40},{9,... | collective-permute-start | bytes 104 | tf_op jit(solution)/shard_map/ppermute | solution.py:612
  25.2 1.2 constant_dynamic-slice_fusion.ez
  26.4 0.7 constant_dynamic-slice_fusion.1.ez
  27.1 0.0 collective-permute-done
  27.1 0.2 collective-permute-done.1
  27.3 0.9 all-to-all-done.tiles
  28.2 0.0 copy-done.1
  28.2 0.0 copy-done.2
  28.2 0.0 copy-done.8
  28.2 0.9 shard_map.131
  29.1 6.9 %collective-permute-start.3 = (f32[32,512]{1,0:T(8,128)S(1)}, f32[32,512]{1,0:T(8,128)S(1)}, u32[]{:S(2)}, u32[]{:S(2)}) collective-permute-start(f32[32,512]{1,0:T(8,128)S(1)} %get-tuple-element.21.own), channel_id=1, source_target_pairs={{0,16},{16,0},{1,17},{17,1},{2,18},{18,2},{3,19},{19,3},{4,20},{20... | collective-permute-start | bytes 196616 | tf_op jit(solution)/shard_map/ppermute | solution.py:656
  36.0 0.9 collective-permute-done.3.other
  36.8 0.1 shard_map.132
  37.0 20.2 %all_to_all.20 = f32[16,8,128]{2,1,0:T(8,128)S(1)} all-to-all(f32[16,8,128]{2,1,0:T(8,128)S(1)} %bitcast.17), channel_id=1, replica_groups=mesh['px_0'=8,'px_1'=2,'px_2'=2,'py'=16] {'px_0','px_1'}, dimensions={0} | all-to-all | bytes 131072 | tf_op jit(solution)/shard_map/all_to_all | solution.py:621
  57.1 0.8 shard_map.133
  57.9 15.6 %all_to_all.21 = f32[16,8,128]{2,1,0:T(8,128)S(1)} all-to-all(f32[16,8,128]{2,1,0:T(8,128)S(1)} %bitcast.19), channel_id=1, replica_groups=mesh['px_0'=8,'px_1'=2,'px_2'=2,'py'=16] {'px_0','px_1'}, dimensions={0} | all-to-all | bytes 131072 | tf_op jit(solution)/shard_map/all_to_all | solution.py:621
  73.5 2.0 %shard_map.134 = f32[16,16,512]{2,1,0:T(8,128)} custom-call(s32[1]{0:T(128)} %bitcast.7.core, f32[256,512]{1,0:T(8,128)S(1)} %get-tuple-element.20.field, f32[32,512]{1,0:T(8,128)S(1)} %collective-permute-done.3.other, f32[128,128]{1,0:T(8,128)S(1)} %bitcast.16, bf16[512,512]{1,0:T(8,128)(2,1)S(1)} %copy-done.2, bf16[512,512]{1,0:T(8,128)(2,1)S(1)} %copy-done.1, ...), custom_call_target="tpu_custom_call" | custom-call | tf_op jit(solution)/shard_map/pallas_call | solution.py:662
  75.5 7.6 %all-to-all-start.3 = ((f32[16,16,512]{2,1,0:T(8,128)}), f32[16,16,512]{2,1,0:T(8,128)S(1)}, u32[]{:S(2)}, u32[]{:S(2)}) async-start(f32[16,16,512]{2,1,0:T(8,128)} %shard_map.134), calls=%async_computation.3 | async-start | bytes 1048576 | tf_op jit(solution)/shard_map/all_to_all | solution.py:616
  83.1 3.4 %collective-permute-start.2 = (s32[3,8]{1,0:T(4,128)S(1)}, s32[3,8]{1,0:T(4,128)S(1)}, u32[]{:S(2)}, u32[]{:S(2)}) collective-permute-start(s32[3,8]{1,0:T(4,128)S(1)} %pad_add_fusion.1), channel_id=1, source_target_pairs={{0,1},{1,2},{2,3},{3,4},{4,5},{5,6},{6,7},{7,8},{8,9},{9,10},{10,1... | collective-permute-start | bytes 296 | tf_op jit(solution)/shard_map/ppermute | solution.py:612
  86.4 6.7 %collective-permute-done.2 = s32[3,8]{1,0:T(4,128)S(1)} collective-permute-done((s32[3,8]{1,0:T(4,128)S(1)}, s32[3,8]{1,0:T(4,128)S(1)}, u32[]{:S(2)}, u32[]{:S(2)}) %collective-permute-start.2) | collective-permute-done | bytes 128 | tf_op jit(solution)/shard_map/ppermute | solution.py:612
  93.1 0.1 reshape.35.places
  93.2 1.8 %all-to-all-done.3.tiles = f32[16,16,512]{2,1,0:T(8,128)S(1)} async-done(((f32[16,16,512]{2,1,0:T(8,128)}), f32[16,16,512]{2,1,0:T(8,128)S(1)}, u32[]{:S(2)}, u32[]{:S(2)}) %all-to-all-start.3) | async-done | bytes 524320 | tf_op jit(solution)/shard_map/all_to_all | solution.py:616
  95.0 0.0 copy-done
  95.0 0.0 copy-done.4
  95.0 2.2 %shard_map.135 = (f32[16,32,256]{2,1,0:T(8,128)}, f32[20,24,128]{2,1,0:T(8,128)S(1)}) custom-call(s32[36]{0:T(128)S(1)} %reshape.35.places, f32[16,16,512]{2,1,0:T(8,128)S(1)} %all-to-all-done.3.tiles, f32[16,32,256]{2,1,0:T(8,128)S(1)} %copy-done, bf16[2,256,256]{2,1,0:T(8,128)(2,1)S(1)} %copy-done.4), custom_call_target="tpu_custom_call" | custom-call | tf_op jit(solution)/shard_map/pallas_call | solution.py:668
  97.2 3.2 %collective-permute-start.4 = (f32[20,24,128]{2,1,0:T(8,128)S(1)}, f32[20,24,128]{2,1,0:T(8,128)S(1)}, u32[]{:S(2)}, u32[]{:S(2)}) collective-permute-start(f32[20,24,128]{2,1,0:T(8,128)S(1)} %get-tuple-element.25), channel_id=1, source_target_pairs={{1,0},{2,1},{3,2},{4,3},{5,4},{6,5},{7,6},{8,7},{9,8},{10,9},{11,1... | collective-permute-start | bytes 737288 | tf_op jit(solution)/shard_map/ppermute | solution.py:612
  100.4 0.1 slice_reduce_fusion
  100.5 1.0 copy-done.7
  101.6 1.3 shard_map.136
  102.9 2.5 %collective-permute-done.4.refs_1_ = f32[20,24,128]{2,1,0:T(8,128)S(1)} collective-permute-done((f32[20,24,128]{2,1,0:T(8,128)S(1)}, f32[20,24,128]{2,1,0:T(8,128)S(1)}, u32[]{:S(2)}, u32[]{:S(2)}) %collective-permute-start.4) | collective-permute-done | bytes 245792 | tf_op jit(solution)/shard_map/ppermute | solution.py:612
  105.4 3.5 %collective-permute-start.6 = (f32[4,24,128]{2,1,0:T(8,128)S(1)}, f32[4,24,128]{2,1,0:T(8,128)S(1)}, u32[]{:S(2)}, u32[]{:S(2)}) collective-permute-start(f32[4,24,128]{2,1,0:T(8,128)S(1)} %slice_add_fusion.1), channel_id=1, source_target_pairs={{32,0},{33,1},{34,2},{35,3},{36,4},{37,5},{38,6},{39,7},{40,8},{41... | collective-permute-start | bytes 147464 | tf_op jit(solution)/shard_map/ppermute | solution.py:612
  108.9 0.0 copy-start.10
  108.9 0.0 copy-start.11
  108.9 3.7 %collective-permute-start.5 = (f32[8,24,128]{2,1,0:T(8,128)S(1)}, f32[8,24,128]{2,1,0:T(8,128)S(1)}, u32[]{:S(2)}, u32[]{:S(2)}) collective-permute-start(f32[8,24,128]{2,1,0:T(8,128)S(1)} %slice_add_fusion), channel_id=1, source_target_pairs={{16,0},{17,1},{18,2},{19,3},{20,4},{21,5},{22,6},{23,7},{24,8},{25... | collective-permute-start | bytes 294920 | tf_op jit(solution)/shard_map/ppermute | solution.py:612
  112.6 0.0 copy-done.10
  112.6 0.0 copy-done.11
  112.6 0.1 pad_add_fusion.3.meta
  112.7 0.0 copy-done.5
  112.7 2.0 %shard_map.137.refs_4_ = f32[24,9,8,128]{3,2,1,0:T(8,128)S(1)} custom-call(f32[2,192,576]{2,1,0:T(8,128)S(1)} %bitcast.15), custom_call_target="tpu_custom_call" | custom-call | tf_op jit(solution)/shard_map/pallas_call | solution.py:641
  114.7 1.1 collective-permute-done.6.refs_3_
  115.8 0.0 collective-permute-done.5.refs_2_
  115.8 12.2 %shard_map.138 = (f32[24,9,8,128]{3,2,1,0:T(8,128)S(1)}, f32[8,128]{1,0:T(8,128)S(1)}, f32[8,24,128]{2,1,0:T(8,128)S(1)}, f32[8,24,128]{2,1,0:T(8,128)S(1)}, f32[4,24,128]{2,1,0:T(8,128)S(1)}) custom-call(s32[8]{0:T(128)S(1)} %pad_add_fusion.3.meta, f32[8,24,128]{2,1,0:T(8,128)S(1)} %get-tuple-element.24.refs_0_, ...), custom_call_target="tpu_custom_call" | custom-call | tf_op jit(solution)/shard_map/pallas_call | solution.py:677
  128.1 5.9 %collective-permute-start.7 = (f32[8,24,128]{2,1,0:T(8,128)S(1)}, f32[8,24,128]{2,1,0:T(8,128)S(1)}, u32[]{:S(2)}, u32[]{:S(2)}) collective-permute-start(f32[8,24,128]{2,1,0:T(8,128)S(1)} %get-tuple-element.31), channel_id=1, source_target_pairs={{0,16},{1,17},{2,18},{3,19},{4,20},{5,21},{6,22},{7,23},{8,24},{9,... | collective-permute-start | bytes 294920 | tf_op jit(solution)/shard_map/ppermute | solution.py:612
  133.9 5.1 %collective-permute-start.8 = (f32[4,24,128]{2,1,0:T(8,128)S(1)}, f32[4,24,128]{2,1,0:T(8,128)S(1)}, u32[]{:S(2)}, u32[]{:S(2)}) collective-permute-start(f32[4,24,128]{2,1,0:T(8,128)S(1)} %get-tuple-element.32), channel_id=1, source_target_pairs={{0,32},{1,33},{2,34},{3,35},{4,36},{5,37},{6,38},{7,39},{8,40},{9,... | collective-permute-start | bytes 147464 | tf_op jit(solution)/shard_map/ppermute | solution.py:612
  139.1 6.0 %collective-permute-done.8.third = f32[4,24,128]{2,1,0:T(8,128)S(1)} collective-permute-done((f32[4,24,128]{2,1,0:T(8,128)S(1)}, f32[4,24,128]{2,1,0:T(8,128)S(1)}, u32[]{:S(2)}, u32[]{:S(2)}) %collective-permute-start.8) | collective-permute-done | bytes 49184 | tf_op jit(solution)/shard_map/ppermute | solution.py:612
  145.0 0.0 collective-permute-done.7.second
  145.1 4.0 %collective-permute-start.9 = (f32[20,24,128]{2,1,0:T(8,128)S(1)}, f32[20,24,128]{2,1,0:T(8,128)S(1)}, u32[]{:S(2)}, u32[]{:S(2)}) collective-permute-start(f32[20,24,128]{2,1,0:T(8,128)S(1)} %pad_maximum_fusion), channel_id=1, source_target_pairs={{0,1},{1,2},{2,3},{3,4},{4,5},{5,6},{6,7},{7,8},{8,9},{9,10},{10,1... | collective-permute-start | bytes 737288 | tf_op jit(solution)/shard_map/ppermute | solution.py:612
  149.1 2.9 %shard_map.139 = f32[2,192,576]{2,1,0:T(8,128)} custom-call(f32[24,9,8,128]{3,2,1,0:T(8,128)S(1)} %get-tuple-element.28.planes, f32[8,128]{1,0:T(8,128)S(1)} %get-tuple-element.29.scale), custom_call_target="tpu_custom_call" | custom-call | tf_op jit(solution)/shard_map/pallas_call | solution.py:693
  152.0 1.5 shard_map.140.owned
  153.5 5.9 %collective-permute-done.9.beside = f32[20,24,128]{2,1,0:T(8,128)S(1)} collective-permute-done((f32[20,24,128]{2,1,0:T(8,128)S(1)}, f32[20,24,128]{2,1,0:T(8,128)S(1)}, u32[]{:S(2)}, u32[]{:S(2)}) %collective-permute-start.9) | collective-permute-done | bytes 245792 | tf_op jit(solution)/shard_map/ppermute | solution.py:612
  159.4 2.3 %shard_map.141 = f32[16,32,256]{2,1,0:T(8,128)} custom-call(s32[36]{0:T(128)S(1)} %reshape.35.places, f32[16,32,256]{2,1,0:T(8,128)S(1)} %shard_map.140.owned, f32[20,24,128]{2,1,0:T(8,128)S(1)} %collective-permute-done.9.beside), custom_call_target="tpu_custom_call" | custom-call | tf_op jit(solution)/shard_map/pallas_call | solution.py:700
  (13 shorter events, 0.1 us)
Async XLA Ops:
  0.6 1.0 copy-start.3
  1.6 1.0 copy-start.6
  3.8 24.4 %copy-start.1 = (bf16[512,512]{1,0:T(8,128)(2,1)S(1)}, bf16[512,512]{1,0:T(8,128)(2,1)}, u32[]{:S(2)}) copy-start(bf16[512,512]{1,0:T(8,128)(2,1)} %constant.56.clone.table_low) | copy-start | bytes 1572868
  3.8 24.4 %copy-start.2 = (bf16[512,512]{1,0:T(8,128)(2,1)S(1)}, bf16[512,512]{1,0:T(8,128)(2,1)}, u32[]{:S(2)}) copy-start(bf16[512,512]{1,0:T(8,128)(2,1)} %constant.55.clone.table_high) | copy-start | bytes 1572868
  3.8 24.3 %all-to-all-start = ((f32[16,16,512]{2,1,0:T(8,128)}), f32[16,16,512]{2,1,0:T(8,128)S(1)}, u32[]{:S(2)}, u32[]{:S(2)}) async-start(f32[16,16,512]{2,1,0:T(8,128)} %shard_map.130), calls=%async_computation | async-start | bytes 1048576 | tf_op jit(solution)/shard_map/all_to_all | solution.py:616
  14.2 0.7 copy-start.9
  15.0 12.1 %collective-permute-start = (s32[8]{0:T(128)S(1)}, s32[8]{0:T(128)S(1)}, u32[]{:S(2)}, u32[]{:S(2)}) collective-permute-start(s32[8]{0:T(128)S(1)} %get-tuple-element.34), channel_id=1, source_target_pairs={{0,16},{1,17},{2,18},{3,19},{4,20},{5,21},{6,22},{7,23},{8,24},{9,... | collective-permute-start | bytes 104 | tf_op jit(solution)/shard_map/ppermute | solution.py:612
  16.9 10.4 %collective-permute-start.1 = (s32[8]{0:T(128)S(1)}, s32[8]{0:T(128)S(1)}, u32[]{:S(2)}, u32[]{:S(2)}) collective-permute-start(s32[8]{0:T(128)S(1)} %get-tuple-element.34), channel_id=1, source_target_pairs={{0,32},{1,33},{2,34},{3,35},{4,36},{5,37},{6,38},{7,39},{8,40},{9,... | collective-permute-start | bytes 104 | tf_op jit(solution)/shard_map/ppermute | solution.py:612
  27.3 0.9 copy-start.8
  29.1 7.7 %collective-permute-start.3 = (f32[32,512]{1,0:T(8,128)S(1)}, f32[32,512]{1,0:T(8,128)S(1)}, u32[]{:S(2)}, u32[]{:S(2)}) collective-permute-start(f32[32,512]{1,0:T(8,128)S(1)} %get-tuple-element.21.own), channel_id=1, source_target_pairs={{0,16},{16,0},{1,17},{17,1},{2,18},{18,2},{3,19},{19,3},{4,20},{20... | collective-permute-start | bytes 196616 | tf_op jit(solution)/shard_map/ppermute | solution.py:656
  75.5 19.5 %copy-start = (f32[16,32,256]{2,1,0:T(8,128)S(1)}, f32[16,32,256]{2,1,0:T(8,128)}, u32[]{:S(2)}) copy-start(f32[16,32,256]{2,1,0:T(8,128)} %external.3) | copy-start | bytes 1572868
  75.5 19.5 %copy-start.4 = (bf16[2,256,256]{2,1,0:T(8,128)(2,1)S(1)}, bf16[2,256,256]{2,1,0:T(8,128)(2,1)}, u32[]{:S(2)}) copy-start(bf16[2,256,256]{2,1,0:T(8,128)(2,1)} %constant.57.clone.table) | copy-start | bytes 786436
  75.5 19.5 %all-to-all-start.3 = ((f32[16,16,512]{2,1,0:T(8,128)}), f32[16,16,512]{2,1,0:T(8,128)S(1)}, u32[]{:S(2)}, u32[]{:S(2)}) async-start(f32[16,16,512]{2,1,0:T(8,128)} %shard_map.134), calls=%async_computation.3 | async-start | bytes 1048576 | tf_op jit(solution)/shard_map/all_to_all | solution.py:616
  83.1 10.0 %collective-permute-start.2 = (s32[3,8]{1,0:T(4,128)S(1)}, s32[3,8]{1,0:T(4,128)S(1)}, u32[]{:S(2)}, u32[]{:S(2)}) collective-permute-start(s32[3,8]{1,0:T(4,128)S(1)} %pad_add_fusion.1), channel_id=1, source_target_pairs={{0,1},{1,2},{2,3},{3,4},{4,5},{5,6},{6,7},{7,8},{8,9},{9,10},{10,1... | collective-permute-start | bytes 296 | tf_op jit(solution)/shard_map/ppermute | solution.py:612
  97.2 15.5 %copy-start.5 = (f32[2,8,24,576]{3,2,1,0:T(8,128)S(1)}, f32[2,8,24,576]{3,2,1,0:T(8,128)}, u32[]{:S(2)}) copy-start(f32[2,8,24,576]{3,2,1,0:T(8,128)} %param.13) | copy-start | bytes 2654212
  97.2 8.2 %collective-permute-start.4 = (f32[20,24,128]{2,1,0:T(8,128)S(1)}, f32[20,24,128]{2,1,0:T(8,128)S(1)}, u32[]{:S(2)}, u32[]{:S(2)}) collective-permute-start(f32[20,24,128]{2,1,0:T(8,128)S(1)} %get-tuple-element.25), channel_id=1, source_target_pairs={{1,0},{2,1},{3,2},{4,3},{5,4},{6,5},{7,6},{8,7},{9,8},{10,9},{11,1... | collective-permute-start | bytes 737288 | tf_op jit(solution)/shard_map/ppermute | solution.py:612
  100.5 1.0 copy-start.7
  105.4 10.4 %collective-permute-start.6 = (f32[4,24,128]{2,1,0:T(8,128)S(1)}, f32[4,24,128]{2,1,0:T(8,128)S(1)}, u32[]{:S(2)}, u32[]{:S(2)}) collective-permute-start(f32[4,24,128]{2,1,0:T(8,128)S(1)} %slice_add_fusion.1), channel_id=1, source_target_pairs={{32,0},{33,1},{34,2},{35,3},{36,4},{37,5},{38,6},{39,7},{40,8},{41... | collective-permute-start | bytes 147464 | tf_op jit(solution)/shard_map/ppermute | solution.py:612
  108.9 3.7 %copy-start.10 = (s32[2]{0:T(128)S(1)}, s32[2]{0:T(128)}, u32[]{:S(2)}) copy-start(s32[2]{0:T(128)} %param.15) | copy-start | bytes 28
  108.9 3.7 %copy-start.11 = (s32[2]{0:T(128)S(1)}, s32[2]{0:T(128)}, u32[]{:S(2)}) copy-start(s32[2]{0:T(128)} %param.16) | copy-start | bytes 28
  108.9 6.9 %collective-permute-start.5 = (f32[8,24,128]{2,1,0:T(8,128)S(1)}, f32[8,24,128]{2,1,0:T(8,128)S(1)}, u32[]{:S(2)}, u32[]{:S(2)}) collective-permute-start(f32[8,24,128]{2,1,0:T(8,128)S(1)} %slice_add_fusion), channel_id=1, source_target_pairs={{16,0},{17,1},{18,2},{19,3},{20,4},{21,5},{22,6},{23,7},{24,8},{25... | collective-permute-start | bytes 294920 | tf_op jit(solution)/shard_map/ppermute | solution.py:612
  128.1 17.0 %collective-permute-start.7 = (f32[8,24,128]{2,1,0:T(8,128)S(1)}, f32[8,24,128]{2,1,0:T(8,128)S(1)}, u32[]{:S(2)}, u32[]{:S(2)}) collective-permute-start(f32[8,24,128]{2,1,0:T(8,128)S(1)} %get-tuple-element.31), channel_id=1, source_target_pairs={{0,16},{1,17},{2,18},{3,19},{4,20},{5,21},{6,22},{7,23},{8,24},{9,... | collective-permute-start | bytes 294920 | tf_op jit(solution)/shard_map/ppermute | solution.py:612
  133.9 11.1 %collective-permute-start.8 = (f32[4,24,128]{2,1,0:T(8,128)S(1)}, f32[4,24,128]{2,1,0:T(8,128)S(1)}, u32[]{:S(2)}, u32[]{:S(2)}) collective-permute-start(f32[4,24,128]{2,1,0:T(8,128)S(1)} %get-tuple-element.32), channel_id=1, source_target_pairs={{0,32},{1,33},{2,34},{3,35},{4,36},{5,37},{6,38},{7,39},{8,40},{9,... | collective-permute-start | bytes 147464 | tf_op jit(solution)/shard_map/ppermute | solution.py:612
  145.1 14.3 %collective-permute-start.9 = (f32[20,24,128]{2,1,0:T(8,128)S(1)}, f32[20,24,128]{2,1,0:T(8,128)S(1)}, u32[]{:S(2)}, u32[]{:S(2)}) collective-permute-start(f32[20,24,128]{2,1,0:T(8,128)S(1)} %pad_maximum_fusion), channel_id=1, source_target_pairs={{0,1},{1,2},{2,3},{3,4},{4,5},{5,6},{6,7},{7,8},{8,9},{9,10},{10,1... | collective-permute-start | bytes 737288 | tf_op jit(solution)/shard_map/ppermute | solution.py:612

commit v6 on v5

--- a/solution.py
+++ b/solution.py
@@ -100,18 +100,18 @@
     return rate
 
 
-def put_rows(ref, first, value):
+def put_rows(ref, first, value, width=8):
     for half in range(2):
         for k in range(4):
-            rows = pl.ds(64 * half + first + k, 8, stride=8)
+            rows = pl.ds(8 * width * half + first + k, 8, stride=width)
             ref[rows, :] = value[8 * half : 8 * half + 8, 128 * k : 128 * k + 128]
 
 
-def take_rows(ref, first):
+def take_rows(ref, first, width=8):
     return jnp.concatenate(
         [
             jnp.concatenate(
-                [ref[pl.ds(64 * half + first + k, 8, stride=8), :] for half in range(2)], 0
+                [ref[pl.ds(8 * width * half + first + k, 8, stride=width), :] for half in range(2)], 0
             )
             for k in range(4)
         ],
@@ -124,15 +124,19 @@
     upper = core[0] == 1
     high = jnp.where(upper, own[...], other[...])
     low = jnp.where(upper, other[...], own[...])
-    put_rows(out, 0, high[:KZ] + power * low[:KZ])
-    put_rows(out, 4, low[KZ:] + power * high[KZ:])
+    put_rows(out, 0, high[:KZ] + power * low[:KZ], 16)
+    put_rows(out, 4, low[KZ : 2 * KZ] + power * high[KZ : 2 * KZ], 16)
+    corners = jnp.concatenate([low[2 * KZ : 2 * KZ + 1, :128], high[2 * KZ : 2 * KZ + 1, :128]], 0)
+    corners = jnp.concatenate([corners, jnp.zeros((6, 128), F32)], 0)
+    for chip in range(NPX // 2):
+        out[16 * chip + 8 : 16 * chip + 16, :] = corners
 
 
 def scan_chips(moments, ey, ez, out):
     rate, _ = decay(ey[...], ez[...])
     power = block_power(rate)
     power = power * power
-    right, left = take_rows(moments, 0), take_rows(moments, 4)
+    right, left = take_rows(moments, 0, 16), take_rows(moments, 4, 16)
     count = NPX // 2
     row = lax.broadcasted_iota(jnp.int32, (count, NY), 0)
     before, after = jnp.ones((count, NY), F32), jnp.ones((count, NY), F32)
@@ -154,7 +158,7 @@
     put_rows(out, 4, state - norm * (right_total - across * left_total) * after)
 
 
-def forward_y(tiles, table_high, table_low, ey, ez, field_out, moment_out, merged):
+def forward_y(tiles, table_high, table_low, ey, ez, own_places, field_out, moment_out, merged):
     block = lanes(KZ) // COLS
     for row in range(ROWS):
         for tile in range(4):
@@ -174,7 +178,9 @@
         back = ROWS - 1 - row
         last = field[back * KZ : (back + 1) * KZ] + rate * last
     moment_out[:KZ] = first
-    moment_out[KZ:] = last
+    moment_out[KZ : 2 * KZ] = last
+    moment_out[2 * KZ :] = jnp.zeros((8, NY), F32)
+    moment_out[2 * KZ :, :128] = own_places[...]
 
 
 def back_y(core, field, other, states, table_high, table_low, ey, ez, tiles_out, solved):
@@ -183,7 +189,7 @@
     upper = core[0] == 1
     state, left = take_rows(states, 0), take_rows(states, 4)
     state = jnp.where(upper, other[:KZ] + power * state, state)
-    left = jnp.where(upper, left, other[KZ:] + power * left)
+    left = jnp.where(upper, left, other[KZ : 2 * KZ] + power * left)
     for row in range(ROWS):
         state = field[row * KZ : (row + 1) * KZ] + rate * state
         solved[row * KZ : (row + 1) * KZ] = state
@@ -617,7 +623,7 @@
 
 
 def over_chips(rows):
-    tiles = rows.reshape(NPX // 2, 8, 128)
+    tiles = rows.reshape(NPX // 2, -1, 128)
     return lax.all_to_all(tiles, PX[:2], split_axis=0, concat_axis=0, tiled=True).reshape(rows.shape)
 
 
@@ -627,17 +633,16 @@
     origin = jnp.stack([row_place * ROWS, col_place * COLS, 0])
     local = (anchors - origin[None, :]).astype(jnp.int32)
     own = jnp.pad(local.reshape(6), (0, 2))
-    above = jnp.stack([own, moved(own, 1, 0), moved(own, 2, 0)])
+    own_places = jnp.pad(own.astype(F32)[None, :], ((0, 7), (0, 120)))
     meta = jnp.concatenate([local[:, 0], weights, degrees, weights]).astype(jnp.int32)
 
     sine_y = [jnp.asarray(t) for t in SINE_Y]
     sine_z = jnp.asarray(SINE_Z)
     ey = jnp.asarray(EIGEN_Y)
     ez = lax.dynamic_slice(jnp.asarray(EIGEN_Z), (col_place * KZ, 0), (KZ, 1))
-    chip_ez = lax.dynamic_slice(jnp.asarray(EIGEN_Z), (col_place * KZ + row_place // 2, 0), (1, 1))
-    ez, chip_ez, above = lax.optimization_barrier((ez, chip_ez, above))
-    places = jnp.stack([above, moved(above, 0, 1)], 1)[:, :, :6].reshape(36)
-
+    chip = row_place // 2
+    chip_ez = lax.dynamic_slice(jnp.asarray(EIGEN_Z), (col_place * KZ + chip, 0), (1, 1))
+    ez, chip_ez, own_places = lax.optimization_barrier((ez, chip_ez, own_places))
     planes = call(
         orbitals_in,
         shape(FRAG, 9, 8, 128),
@@ -647,17 +652,22 @@
     tiles = swapped(tiles)
     field, moments = call(
         forward_y,
-        (shape(ROWS * KZ, NY), shape(2 * KZ, NY)),
+        (shape(ROWS * KZ, NY), shape(2 * KZ + 8, NY)),
         [pltpu.VMEM((ROWS * KZ, NY), F32)],
-        count=5,
-    )(tiles, *sine_y, ey, ez)
+        count=6,
+    )(tiles, *sine_y, ey, ez, own_places)
 
     core = lax.axis_index("px_2").reshape(1).astype(jnp.int32)
     other = lax.ppermute(moments, "px_2", [(0, 1), (1, 0)])
-    chips = call(pair_moments, shape(128, 128), smem=(0,), count=5)(core, moments, other, ey, ez)
+    chips = call(pair_moments, shape(256, 128), smem=(0,), count=5)(core, moments, other, ey, ez)
     chips = over_chips(chips)
-    chips = call(scan_chips, shape(128, 128), count=3)(chips, ey, chip_ez)
-    states = over_chips(chips)
+    states = over_chips(call(scan_chips, shape(128, 128), count=3)(chips, ey, chip_ez))
+    before = lax.dynamic_slice(chips, (16 * jnp.maximum(chip - 1, 0) + 8, 0), (2, 8)).astype(jnp.int32)
+    mate = other[2 * KZ, :8].astype(jnp.int32)
+    even = core[0] == 0
+    above = jnp.stack([own, jnp.where(even, before[1], mate), jnp.where(even, before[0], before[1])])
+    above, states = lax.optimization_barrier((above, states))
+    places = jnp.stack([above, moved(above, 0, 1)], 1)[:, :, :6].reshape(36)
 
     tiles = call(
         back_y, shape(NPY, KZ, ROWS * COLS), [pltpu.VMEM((ROWS * KZ, NY), F32)], smem=(0,), count=8

time: 162 us -> 164 us (1.012)
  blocking collectives: 35.7 us -> 0 us
  waiting for transfers between devices: 25.9 us -> 57 us
  Pallas kernels: 29.5 us -> 35 us
    all_to_all x2 -> x0, blocking collectives: 35.7 us -> none  [over_chips(): lax.all_to_all(tiles, PX[:2], split_axis=0, concat_axis=0, tiled=True)]
    all_to_all x0 -> x2, waiting for transfers between devices: none -> 24 us  [over_chips(): lax.all_to_all(tiles, PX[:2], split_axis=0, concat_axis=0, tiled=True)]
    all_to_all x0 -> x2, starting transfers between devices: none -> 18.2 us  [over_chips(): lax.all_to_all(tiles, PX[:2], split_axis=0, concat_axis=0, tiled=True)]
    ppermute x9 -> x7, starting transfers between devices: 38.9 us -> 27.2 us  [moved(): return lax.ppermute(x, ALL, pairs)]
    all_to_all x2, waiting for transfers between devices: 2.63 us -> 13 us  [swapped(): return lax.all_to_all(tiles, 'py', split_axis=0, concat_axis=0, tiled=True)]
    ppermute x1, starting transfers between devices: 6.85 us -> 1.92 us  [body(): other = lax.ppermute(moments, 'px_2', [(0, 1), (1, 0)])]
    pallas_call x1, Pallas kernels: 12.2 us -> 16.5 us  [body(): call(filter_fragments, [shape(FRAG, 9, 8, 128), shape(8, 128)] + [shape(n...]
    ppermute x9 -> x7, waiting for transfers between devices: 22.3 us -> 18.8 us  [moved(): return lax.ppermute(x, ALL, pairs)]
  transfers between devices with their start and end apart: 12 -> 12, of which waited for: 9 -> 10; matrix products, arithmetic and copies ran while one was open for 1% -> 1% of each run, Pallas kernels for 5% -> 5%
where the time goes in v6:
time: 164 us; the launch traced here: 163 us
  starting transfers between devices  63.9 us (39%)
  waiting for transfers between devices  57 us (35%)
  Pallas kernels  35 us (21%)
  local copies, waits for them, and re-layouts  5.87 us (4%)
    ppermute x7, starting transfers between devices, moved(): return lax.ppermute(x, ALL, pairs)  27.2 us
    all_to_all x2, waiting for transfers between devices, over_chips(): lax.all_to_all(tiles, PX[:2], split_axis=0, concat_axis=0, tiled=True)  24 us
    ppermute x7, waiting for transfers between devices, moved(): return lax.ppermute(x, ALL, pairs)  18.8 us
    all_to_all x2, starting transfers between devices, over_chips(): lax.all_to_all(tiles, PX[:2], split_axis=0, concat_axis=0, tiled=True)  18.2 us
    all_to_all x2, starting transfers between devices, swapped(): return lax.all_to_all(tiles, 'py', split_axis=0, concat_axis=0, tiled=True)  16.6 us
    pallas_call x1, Pallas kernels, body(): call(filter_fragments, [shape(FRAG, 9, 8, 128), shape(8, 128)] + [shape(n...  16.5 us
    all_to_all x2, waiting for transfers between devices, swapped(): return lax.all_to_all(tiles, 'py', split_axis=0, concat_axis=0, tiled=True)  13 us
    unnamed x24, local copies, waits for them, and re-layouts  3.66 us
  transfers between devices with their start and end apart: 12, of which 10 were waited for; matrix products, arithmetic and copies ran while one was open for 1% of the time, Pallas kernels for 5%

profile of v6, /device:TPU:10, one launch (start us, length us, event | category | flops | bytes accessed | tf_op | source)
XLA Modules:
  0.0 162.8 jit_solution(12086578030124049999)
XLA Ops:
  0.6 0.0 copy-start.3
  0.6 0.9 copy-done.3
  1.6 0.0 copy-start.6
  1.6 1.0 copy-done.6
  2.6 1.2 shard_map.130
  3.8 0.0 copy-start.1
  3.8 0.0 copy-start.2
  3.8 10.4 %all-to-all-start = ((f32[16,16,512]{2,1,0:T(8,128)}), f32[16,16,512]{2,1,0:T(8,128)S(1)}, u32[]{:S(2)}, u32[]{:S(2)}) async-start(f32[16,16,512]{2,1,0:T(8,128)} %shard_map.130), calls=%async_computation | async-start | bytes 1048576 | tf_op jit(solution)/shard_map/all_to_all | solution.py:622
  14.2 0.0 copy-start.9
  14.2 0.1 pad_add_fusion.2
  14.3 0.6 copy-done.9
  14.9 0.1 reshape.34
  15.0 1.2 constant_dynamic-slice_fusion.ez
  16.2 0.0 copy-start.8
  16.2 0.7 constant_dynamic-slice_fusion.1.ez
  16.9 11.2 %all-to-all-done.tiles = f32[16,16,512]{2,1,0:T(8,128)S(1)} async-done(((f32[16,16,512]{2,1,0:T(8,128)}), f32[16,16,512]{2,1,0:T(8,128)S(1)}, u32[]{:S(2)}, u32[]{:S(2)}) %all-to-all-start) | async-done | bytes 524320 | tf_op jit(solution)/shard_map/all_to_all | solution.py:622
  28.2 0.0 copy-done.1
  28.2 0.0 copy-done.2
  28.2 0.0 copy-done.8
  28.2 0.9 shard_map.131
  29.1 1.9 %collective-permute-start = (f32[40,512]{1,0:T(8,128)S(1)}, f32[40,512]{1,0:T(8,128)S(1)}, u32[]{:S(2)}, u32[]{:S(2)}) collective-permute-start(f32[40,512]{1,0:T(8,128)S(1)} %get-tuple-element.22.own), channel_id=1, source_target_pairs={{0,16},{16,0},{1,17},{17,1},{2,18},{18,2},{3,19},{19,3},{4,20},{20... | collective-permute-start | bytes 245768 | tf_op jit(solution)/shard_map/ppermute | solution.py:661
  31.0 1.2 collective-permute-done.other
  32.3 0.8 shard_map.132
  33.0 13.3 %all-to-all-start.1 = ((f32[16,16,128]{2,1,0:T(8,128)}), f32[16,16,128]{2,1,0:T(8,128)S(1)}, u32[]{:S(2)}, u32[]{:S(2)}) async-start(f32[16,16,128]{2,1,0:T(8,128)} %bitcast.5), calls=%async_computation.1 | async-start | bytes 262144 | tf_op jit(solution)/shard_map/all_to_all | solution.py:627
  46.3 12.4 %all-to-all-done.1 = f32[16,16,128]{2,1,0:T(8,128)S(1)} async-done(((f32[16,16,128]{2,1,0:T(8,128)}), f32[16,16,128]{2,1,0:T(8,128)S(1)}, u32[]{:S(2)}, u32[]{:S(2)}) %all-to-all-start.1) | async-done | bytes 131104 | tf_op jit(solution)/shard_map/all_to_all | solution.py:627
  58.7 1.4 shard_map.133
  60.2 4.8 %all-to-all-start.2 = ((f32[16,8,128]{2,1,0:T(8,128)}), f32[16,8,128]{2,1,0:T(8,128)S(1)}, u32[]{:S(2)}, u32[]{:S(2)}) async-start(f32[16,8,128]{2,1,0:T(8,128)} %bitcast.7), calls=%async_computation.2 | async-start | bytes 131072 | tf_op jit(solution)/shard_map/all_to_all | solution.py:627
  65.0 11.6 %all-to-all-done.2 = f32[16,8,128]{2,1,0:T(8,128)S(1)} async-done(((f32[16,8,128]{2,1,0:T(8,128)}), f32[16,8,128]{2,1,0:T(8,128)S(1)}, u32[]{:S(2)}, u32[]{:S(2)}) %all-to-all-start.2) | async-done | bytes 65568 | tf_op jit(solution)/shard_map/all_to_all | solution.py:627
  76.7 1.9 %shard_map.134 = f32[16,16,512]{2,1,0:T(8,128)} custom-call(s32[1]{0:T(128)} %bitcast.3.core, f32[256,512]{1,0:T(8,128)S(1)} %get-tuple-element.25.field, f32[40,512]{1,0:T(8,128)S(1)} %collective-permute-done.other, f32[128,128]{1,0:T(8,128)S(1)} %bitcast.18, bf16[512,512]{1,0:T(8,128)(2,1)S(1)} %copy-done.2, bf16[512,512]{1,0:T(8,128)(2,1)S(1)} %copy-done.1, ...), custom_call_target="tpu_custom_call" | custom-call | tf_op jit(solution)/shard_map/pallas_call | solution.py:672
  78.6 0.0 copy-start
  78.6 6.2 %all-to-all-start.3 = ((f32[16,16,512]{2,1,0:T(8,128)}), f32[16,16,512]{2,1,0:T(8,128)S(1)}, u32[]{:S(2)}, u32[]{:S(2)}) async-start(f32[16,16,512]{2,1,0:T(8,128)} %shard_map.134), calls=%async_computation.3 | async-start | bytes 1048576 | tf_op jit(solution)/shard_map/all_to_all | solution.py:622
  84.8 3.4 %collective-permute-start.1 = (s32[3,8]{1,0:T(4,128)S(1)}, s32[3,8]{1,0:T(4,128)S(1)}, u32[]{:S(2)}, u32[]{:S(2)}) collective-permute-start(s32[3,8]{1,0:T(4,128)S(1)} %pad_add_fusion.1), channel_id=1, source_target_pairs={{0,1},{1,2},{2,3},{3,4},{4,5},{5,6},{6,7},{7,8},{8,9},{9,10},{10,1... | collective-permute-start | bytes 296 | tf_op jit(solution)/shard_map/ppermute | solution.py:618
  88.2 6.5 %collective-permute-done.1 = s32[3,8]{1,0:T(4,128)S(1)} collective-permute-done((s32[3,8]{1,0:T(4,128)S(1)}, s32[3,8]{1,0:T(4,128)S(1)}, u32[]{:S(2)}, u32[]{:S(2)}) %collective-permute-start.1) | collective-permute-done | bytes 128 | tf_op jit(solution)/shard_map/ppermute | solution.py:618
  94.7 0.1 reshape.40.places
  94.8 1.8 %all-to-all-done.3.tiles = f32[16,16,512]{2,1,0:T(8,128)S(1)} async-done(((f32[16,16,512]{2,1,0:T(8,128)}), f32[16,16,512]{2,1,0:T(8,128)S(1)}, u32[]{:S(2)}, u32[]{:S(2)}) %all-to-all-start.3) | async-done | bytes 524320 | tf_op jit(solution)/shard_map/all_to_all | solution.py:622
  96.6 0.0 copy-done
  96.6 0.0 copy-done.4
  96.6 2.2 %shard_map.135 = (f32[16,32,256]{2,1,0:T(8,128)}, f32[20,24,128]{2,1,0:T(8,128)S(1)}) custom-call(s32[36]{0:T(128)S(1)} %reshape.40.places, f32[16,16,512]{2,1,0:T(8,128)S(1)} %all-to-all-done.3.tiles, f32[16,32,256]{2,1,0:T(8,128)S(1)} %copy-done, bf16[2,256,256]{2,1,0:T(8,128)(2,1)S(1)} %copy-done.4), custom_call_target="tpu_custom_call" | custom-call | tf_op jit(solution)/shard_map/pallas_call | solution.py:678
  98.8 3.3 %collective-permute-start.2 = (f32[20,24,128]{2,1,0:T(8,128)S(1)}, f32[20,24,128]{2,1,0:T(8,128)S(1)}, u32[]{:S(2)}, u32[]{:S(2)}) collective-permute-start(f32[20,24,128]{2,1,0:T(8,128)S(1)} %get-tuple-element.29), channel_id=1, source_target_pairs={{1,0},{2,1},{3,2},{4,3},{5,4},{6,5},{7,6},{8,7},{9,8},{10,9},{11,1... | collective-permute-start | bytes 737288 | tf_op jit(solution)/shard_map/ppermute | solution.py:618
  102.1 0.1 slice_reduce_fusion
  102.2 1.0 copy-done.7
  103.3 1.3 shard_map.136
  104.5 2.4 %collective-permute-done.2.refs_1_ = f32[20,24,128]{2,1,0:T(8,128)S(1)} collective-permute-done((f32[20,24,128]{2,1,0:T(8,128)S(1)}, f32[20,24,128]{2,1,0:T(8,128)S(1)}, u32[]{:S(2)}, u32[]{:S(2)}) %collective-permute-start.2) | collective-permute-done | bytes 245792 | tf_op jit(solution)/shard_map/ppermute | solution.py:618
  107.0 3.4 %collective-permute-start.4 = (f32[4,24,128]{2,1,0:T(8,128)S(1)}, f32[4,24,128]{2,1,0:T(8,128)S(1)}, u32[]{:S(2)}, u32[]{:S(2)}) collective-permute-start(f32[4,24,128]{2,1,0:T(8,128)S(1)} %slice_add_fusion.1), channel_id=1, source_target_pairs={{32,0},{33,1},{34,2},{35,3},{36,4},{37,5},{38,6},{39,7},{40,8},{41... | collective-permute-start | bytes 147464 | tf_op jit(solution)/shard_map/ppermute | solution.py:618
  110.4 0.0 copy-start.10
  110.4 0.0 copy-start.11
  110.5 3.7 %collective-permute-start.3 = (f32[8,24,128]{2,1,0:T(8,128)S(1)}, f32[8,24,128]{2,1,0:T(8,128)S(1)}, u32[]{:S(2)}, u32[]{:S(2)}) collective-permute-start(f32[8,24,128]{2,1,0:T(8,128)S(1)} %slice_add_fusion), channel_id=1, source_target_pairs={{16,0},{17,1},{18,2},{19,3},{20,4},{21,5},{22,6},{23,7},{24,8},{25... | collective-permute-start | bytes 294920 | tf_op jit(solution)/shard_map/ppermute | solution.py:618
  114.2 0.0 copy-done.10
  114.2 0.0 copy-done.11
  114.2 0.1 pad_add_fusion.3.meta
  114.3 0.0 copy-done.5
  114.3 2.0 %shard_map.137.refs_4_ = f32[24,9,8,128]{3,2,1,0:T(8,128)S(1)} custom-call(f32[2,192,576]{2,1,0:T(8,128)S(1)} %bitcast.15), custom_call_target="tpu_custom_call" | custom-call | tf_op jit(solution)/shard_map/pallas_call | solution.py:646
  116.3 1.1 collective-permute-done.4.refs_3_
  117.4 0.0 collective-permute-done.3.refs_2_
  117.4 16.5 %shard_map.138 = (f32[24,9,8,128]{3,2,1,0:T(8,128)S(1)}, f32[8,128]{1,0:T(8,128)S(1)}, f32[8,24,128]{2,1,0:T(8,128)S(1)}, f32[8,24,128]{2,1,0:T(8,128)S(1)}, f32[4,24,128]{2,1,0:T(8,128)S(1)}) custom-call(s32[8]{0:T(128)S(1)} %pad_add_fusion.3.meta, f32[8,24,128]{2,1,0:T(8,128)S(1)} %get-tuple-element.28.refs_0_, ...), custom_call_target="tpu_custom_call" | custom-call | tf_op jit(solution)/shard_map/pallas_call | solution.py:687
  133.9 1.9 %collective-permute-start.5 = (f32[8,24,128]{2,1,0:T(8,128)S(1)}, f32[8,24,128]{2,1,0:T(8,128)S(1)}, u32[]{:S(2)}, u32[]{:S(2)}) collective-permute-start(f32[8,24,128]{2,1,0:T(8,128)S(1)} %get-tuple-element.35), channel_id=1, source_target_pairs={{0,16},{1,17},{2,18},{3,19},{4,20},{5,21},{6,22},{7,23},{8,24},{9,... | collective-permute-start | bytes 294920 | tf_op jit(solution)/shard_map/ppermute | solution.py:618
  135.8 6.6 %collective-permute-start.6 = (f32[4,24,128]{2,1,0:T(8,128)S(1)}, f32[4,24,128]{2,1,0:T(8,128)S(1)}, u32[]{:S(2)}, u32[]{:S(2)}) collective-permute-start(f32[4,24,128]{2,1,0:T(8,128)S(1)} %get-tuple-element.36), channel_id=1, source_target_pairs={{0,32},{1,33},{2,34},{3,35},{4,36},{5,37},{6,38},{7,39},{8,40},{9,... | collective-permute-start | bytes 147464 | tf_op jit(solution)/shard_map/ppermute | solution.py:618
  142.4 4.3 %collective-permute-done.6.third = f32[4,24,128]{2,1,0:T(8,128)S(1)} collective-permute-done((f32[4,24,128]{2,1,0:T(8,128)S(1)}, f32[4,24,128]{2,1,0:T(8,128)S(1)}, u32[]{:S(2)}, u32[]{:S(2)}) %collective-permute-start.6) | collective-permute-done | bytes 49184 | tf_op jit(solution)/shard_map/ppermute | solution.py:618
  146.8 0.0 collective-permute-done.5.second
  146.8 4.9 %collective-permute-start.7 = (f32[20,24,128]{2,1,0:T(8,128)S(1)}, f32[20,24,128]{2,1,0:T(8,128)S(1)}, u32[]{:S(2)}, u32[]{:S(2)}) collective-permute-start(f32[20,24,128]{2,1,0:T(8,128)S(1)} %pad_maximum_fusion), channel_id=1, source_target_pairs={{0,1},{1,2},{2,3},{3,4},{4,5},{5,6},{6,7},{7,8},{8,9},{9,10},{10,1... | collective-permute-start | bytes 737288 | tf_op jit(solution)/shard_map/ppermute | solution.py:618
  151.6 2.9 %shard_map.139 = f32[2,192,576]{2,1,0:T(8,128)} custom-call(f32[24,9,8,128]{3,2,1,0:T(8,128)S(1)} %get-tuple-element.32.planes, f32[8,128]{1,0:T(8,128)S(1)} %get-tuple-element.33.scale), custom_call_target="tpu_custom_call" | custom-call | tf_op jit(solution)/shard_map/pallas_call | solution.py:703
  154.6 1.5 shard_map.140.owned
  156.1 4.4 %collective-permute-done.7.beside = f32[20,24,128]{2,1,0:T(8,128)S(1)} collective-permute-done((f32[20,24,128]{2,1,0:T(8,128)S(1)}, f32[20,24,128]{2,1,0:T(8,128)S(1)}, u32[]{:S(2)}, u32[]{:S(2)}) %collective-permute-start.7) | collective-permute-done | bytes 245792 | tf_op jit(solution)/shard_map/ppermute | solution.py:618
  160.5 2.3 %shard_map.141 = f32[16,32,256]{2,1,0:T(8,128)} custom-call(s32[36]{0:T(128)S(1)} %reshape.40.places, f32[16,32,256]{2,1,0:T(8,128)S(1)} %shard_map.140.owned, f32[20,24,128]{2,1,0:T(8,128)S(1)} %collective-permute-done.7.beside), custom_call_target="tpu_custom_call" | custom-call | tf_op jit(solution)/shard_map/pallas_call | solution.py:710
  (14 shorter events, 0.1 us)
Async XLA Ops:
  0.6 1.0 copy-start.3
  1.6 1.0 copy-start.6
  3.8 24.3 %copy-start.1 = (bf16[512,512]{1,0:T(8,128)(2,1)S(1)}, bf16[512,512]{1,0:T(8,128)(2,1)}, u32[]{:S(2)}) copy-start(bf16[512,512]{1,0:T(8,128)(2,1)} %constant.64.clone.table_low) | copy-start | bytes 1572868
  3.8 24.3 %copy-start.2 = (bf16[512,512]{1,0:T(8,128)(2,1)S(1)}, bf16[512,512]{1,0:T(8,128)(2,1)}, u32[]{:S(2)}) copy-start(bf16[512,512]{1,0:T(8,128)(2,1)} %constant.63.clone.table_high) | copy-start | bytes 1572868
  3.8 24.3 %all-to-all-start = ((f32[16,16,512]{2,1,0:T(8,128)}), f32[16,16,512]{2,1,0:T(8,128)S(1)}, u32[]{:S(2)}, u32[]{:S(2)}) async-start(f32[16,16,512]{2,1,0:T(8,128)} %shard_map.130), calls=%async_computation | async-start | bytes 1048576 | tf_op jit(solution)/shard_map/all_to_all | solution.py:622
  14.2 0.7 copy-start.9
  16.2 11.9 %copy-start.8 = (f32[1,512]{1,0:T(1,128)S(1)}, f32[1,512]{1,0:T(1,128)}, u32[]{:S(2)}) copy-start(f32[1,512]{1,0:T(1,128)} %constant.66.clone.ey) | copy-start | bytes 6148
  29.1 3.2 %collective-permute-start = (f32[40,512]{1,0:T(8,128)S(1)}, f32[40,512]{1,0:T(8,128)S(1)}, u32[]{:S(2)}, u32[]{:S(2)}) collective-permute-start(f32[40,512]{1,0:T(8,128)S(1)} %get-tuple-element.22.own), channel_id=1, source_target_pairs={{0,16},{16,0},{1,17},{17,1},{2,18},{18,2},{3,19},{19,3},{4,20},{20... | collective-permute-start | bytes 245768 | tf_op jit(solution)/shard_map/ppermute | solution.py:661
  33.0 25.7 %all-to-all-start.1 = ((f32[16,16,128]{2,1,0:T(8,128)}), f32[16,16,128]{2,1,0:T(8,128)S(1)}, u32[]{:S(2)}, u32[]{:S(2)}) async-start(f32[16,16,128]{2,1,0:T(8,128)} %bitcast.5), calls=%async_computation.1 | async-start | bytes 262144 | tf_op jit(solution)/shard_map/all_to_all | solution.py:627
  60.2 16.5 %all-to-all-start.2 = ((f32[16,8,128]{2,1,0:T(8,128)}), f32[16,8,128]{2,1,0:T(8,128)S(1)}, u32[]{:S(2)}, u32[]{:S(2)}) async-start(f32[16,8,128]{2,1,0:T(8,128)} %bitcast.7), calls=%async_computation.2 | async-start | bytes 131072 | tf_op jit(solution)/shard_map/all_to_all | solution.py:627
  78.6 17.9 %copy-start = (f32[16,32,256]{2,1,0:T(8,128)S(1)}, f32[16,32,256]{2,1,0:T(8,128)}, u32[]{:S(2)}) copy-start(f32[16,32,256]{2,1,0:T(8,128)} %external.3) | copy-start | bytes 1572868
  78.6 17.9 %copy-start.4 = (bf16[2,256,256]{2,1,0:T(8,128)(2,1)S(1)}, bf16[2,256,256]{2,1,0:T(8,128)(2,1)}, u32[]{:S(2)}) copy-start(bf16[2,256,256]{2,1,0:T(8,128)(2,1)} %constant.65.clone.table) | copy-start | bytes 786436
  78.6 17.9 %all-to-all-start.3 = ((f32[16,16,512]{2,1,0:T(8,128)}), f32[16,16,512]{2,1,0:T(8,128)S(1)}, u32[]{:S(2)}, u32[]{:S(2)}) async-start(f32[16,16,512]{2,1,0:T(8,128)} %shard_map.134), calls=%async_computation.3 | async-start | bytes 1048576 | tf_op jit(solution)/shard_map/all_to_all | solution.py:622
  84.8 9.9 %collective-permute-start.1 = (s32[3,8]{1,0:T(4,128)S(1)}, s32[3,8]{1,0:T(4,128)S(1)}, u32[]{:S(2)}, u32[]{:S(2)}) collective-permute-start(s32[3,8]{1,0:T(4,128)S(1)} %pad_add_fusion.1), channel_id=1, source_target_pairs={{0,1},{1,2},{2,3},{3,4},{4,5},{5,6},{6,7},{7,8},{8,9},{9,10},{10,1... | collective-permute-start | bytes 296 | tf_op jit(solution)/shard_map/ppermute | solution.py:618
  98.8 15.5 %copy-start.5 = (f32[2,8,24,576]{3,2,1,0:T(8,128)S(1)}, f32[2,8,24,576]{3,2,1,0:T(8,128)}, u32[]{:S(2)}) copy-start(f32[2,8,24,576]{3,2,1,0:T(8,128)} %param.13) | copy-start | bytes 2654212
  98.8 8.2 %collective-permute-start.2 = (f32[20,24,128]{2,1,0:T(8,128)S(1)}, f32[20,24,128]{2,1,0:T(8,128)S(1)}, u32[]{:S(2)}, u32[]{:S(2)}) collective-permute-start(f32[20,24,128]{2,1,0:T(8,128)S(1)} %get-tuple-element.29), channel_id=1, source_target_pairs={{1,0},{2,1},{3,2},{4,3},{5,4},{6,5},{7,6},{8,7},{9,8},{10,9},{11,1... | collective-permute-start | bytes 737288 | tf_op jit(solution)/shard_map/ppermute | solution.py:618
  102.2 1.0 copy-start.7
  107.0 10.4 %collective-permute-start.4 = (f32[4,24,128]{2,1,0:T(8,128)S(1)}, f32[4,24,128]{2,1,0:T(8,128)S(1)}, u32[]{:S(2)}, u32[]{:S(2)}) collective-permute-start(f32[4,24,128]{2,1,0:T(8,128)S(1)} %slice_add_fusion.1), channel_id=1, source_target_pairs={{32,0},{33,1},{34,2},{35,3},{36,4},{37,5},{38,6},{39,7},{40,8},{41... | collective-permute-start | bytes 147464 | tf_op jit(solution)/shard_map/ppermute | solution.py:618
  110.4 3.8 %copy-start.10 = (s32[2]{0:T(128)S(1)}, s32[2]{0:T(128)}, u32[]{:S(2)}) copy-start(s32[2]{0:T(128)} %param.15) | copy-start | bytes 28
  110.4 3.8 %copy-start.11 = (s32[2]{0:T(128)S(1)}, s32[2]{0:T(128)}, u32[]{:S(2)}) copy-start(s32[2]{0:T(128)} %param.16) | copy-start | bytes 28
  110.5 7.0 %collective-permute-start.3 = (f32[8,24,128]{2,1,0:T(8,128)S(1)}, f32[8,24,128]{2,1,0:T(8,128)S(1)}, u32[]{:S(2)}, u32[]{:S(2)}) collective-permute-start(f32[8,24,128]{2,1,0:T(8,128)S(1)} %slice_add_fusion), channel_id=1, source_target_pairs={{16,0},{17,1},{18,2},{19,3},{20,4},{21,5},{22,6},{23,7},{24,8},{25... | collective-permute-start | bytes 294920 | tf_op jit(solution)/shard_map/ppermute | solution.py:618
  133.9 12.9 %collective-permute-start.5 = (f32[8,24,128]{2,1,0:T(8,128)S(1)}, f32[8,24,128]{2,1,0:T(8,128)S(1)}, u32[]{:S(2)}, u32[]{:S(2)}) collective-permute-start(f32[8,24,128]{2,1,0:T(8,128)S(1)} %get-tuple-element.35), channel_id=1, source_target_pairs={{0,16},{1,17},{2,18},{3,19},{4,20},{5,21},{6,22},{7,23},{8,24},{9,... | collective-permute-start | bytes 294920 | tf_op jit(solution)/shard_map/ppermute | solution.py:618
  135.8 10.9 %collective-permute-start.6 = (f32[4,24,128]{2,1,0:T(8,128)S(1)}, f32[4,24,128]{2,1,0:T(8,128)S(1)}, u32[]{:S(2)}, u32[]{:S(2)}) collective-permute-start(f32[4,24,128]{2,1,0:T(8,128)S(1)} %get-tuple-element.36), channel_id=1, source_target_pairs={{0,32},{1,33},{2,34},{3,35},{4,36},{5,37},{6,38},{7,39},{8,40},{9,... | collective-permute-start | bytes 147464 | tf_op jit(solution)/shard_map/ppermute | solution.py:618
  146.8 13.7 %collective-permute-start.7 = (f32[20,24,128]{2,1,0:T(8,128)S(1)}, f32[20,24,128]{2,1,0:T(8,128)S(1)}, u32[]{:S(2)}, u32[]{:S(2)}) collective-permute-start(f32[20,24,128]{2,1,0:T(8,128)S(1)} %pad_maximum_fusion), channel_id=1, source_target_pairs={{0,1},{1,2},{2,3},{3,4},{4,5},{5,6},{6,7},{7,8},{8,9},{9,10},{10,1... | collective-permute-start | bytes 737288 | tf_op jit(solution)/shard_map/ppermute | solution.py:618

commit v7 on v3

--- a/solution.py
+++ b/solution.py
@@ -399,11 +399,11 @@
 
         def chunk(number, carry):
             behind, here = list(carry[:9]), list(carry[9:])
-            for k4 in range(8):
-                x = 8 * number + k4
+            for k4 in range(24):
+                x = 24 * number + k4
                 ahead_x = jnp.minimum(x + 1, FRAG - 1)
                 ahead = [source[ahead_x, k] for k in range(9)]
-                if k4 == 7:
+                if k4 == 23:
                     ahead = [jnp.where(x + 1 < FRAG, v, 0.0) for v in ahead]
                 for k in range(9):
                     yi, zi = divmod(k, 3)
@@ -438,7 +438,7 @@
             return tuple(behind + here)
 
         zero = [jnp.zeros((8, 128), F32)] * 9
-        lax.fori_loop(0, 3, chunk, tuple(zero + [source[0, k] for k in range(9)]))
+        lax.fori_loop(0, 1, chunk, tuple(zero + [source[0, k] for k in range(9)]))
 
     apply(start, other, initial=True)
     apply(other, out, earlier=start, even=True)

time: 161 us -> 160 us (level)
  the two profiles are of different devices: /device:TPU:38 before, /device:TPU:34 now
where the time goes in v7:
time: 160 us; the launch traced here: 159 us
  starting transfers between devices  62.3 us (39%)
  waiting for transfers between devices  58.1 us (36%)
  Pallas kernels  31.9 us (20%)
  local copies, waits for them, and re-layouts  5.3 us (3%)
    ppermute x9, waiting for transfers between devices, moved(): return lax.ppermute(x, ALL, pairs)  30.6 us
    ppermute x9, starting transfers between devices, moved(): return lax.ppermute(x, ALL, pairs)  29.8 us
    ppermute x5, waiting for transfers between devices, body(): got = lax.ppermute(totals, ALL, pairs)  25.7 us
    all_to_all x2, starting transfers between devices, body(): tiles = lax.all_to_all(tiles, 'py', split_axis=0, concat_axis=0, tiled=True)  17.1 us
    pallas_call x1, Pallas kernels, body(): call(filter_fragments, [shape(FRAG, 9, 8, 128), shape(8, 128)] + [shape(n...  15.5 us
    ppermute x5, starting transfers between devices, body(): got = lax.ppermute(totals, ALL, pairs)  15.3 us
    unnamed x24, local copies, waits for them, and re-layouts  4.29 us
  transfers between devices with their start and end apart: 16, of which 13 were waited for; matrix products, arithmetic and copies ran while one was open for 1% of the time, Pallas kernels for 5%

profile of v7, /device:TPU:34, one launch (start us, length us, event | category | flops | bytes accessed | tf_op | source)
XLA Modules:
  0.0 159.1 jit_solution(5869900704151676450)
XLA Ops:
  0.6 0.0 copy-start.3
  0.6 0.9 copy-done.3
  1.6 1.0 copy-done.6
  2.6 1.2 shard_map.130
  3.8 10.4 %all-to-all-start = ((f32[16,16,512]{2,1,0:T(8,128)}), f32[16,16,512]{2,1,0:T(8,128)S(1)}, u32[]{:S(2)}, u32[]{:S(2)}) async-start(f32[16,16,512]{2,1,0:T(8,128)} %shard_map.130), calls=%async_computation | async-start | bytes 1048576 | tf_op jit(solution)/shard_map/all_to_all | solution.py:604
  14.2 0.1 pad_add_fusion.2
  14.3 0.6 copy-done.9
  14.9 0.1 reshape.22
  15.0 1.9 %collective-permute-start = (s32[8]{0:T(128)S(1)}, s32[8]{0:T(128)S(1)}, u32[]{:S(2)}, u32[]{:S(2)}) collective-permute-start(s32[8]{0:T(128)S(1)} %get-tuple-element.58), channel_id=1, source_target_pairs={{0,16},{1,17},{2,18},{3,19},{4,20},{5,21},{6,22},{7,23},{8,24},{9,... | collective-permute-start | bytes 104 | tf_op jit(solution)/shard_map/ppermute | solution.py:572
  16.9 8.2 %collective-permute-start.1 = (s32[8]{0:T(128)S(1)}, s32[8]{0:T(128)S(1)}, u32[]{:S(2)}, u32[]{:S(2)}) collective-permute-start(s32[8]{0:T(128)S(1)} %get-tuple-element.58), channel_id=1, source_target_pairs={{0,32},{1,33},{2,34},{3,35},{4,36},{5,37},{6,38},{7,39},{8,40},{9,... | collective-permute-start | bytes 104 | tf_op jit(solution)/shard_map/ppermute | solution.py:572
  25.2 0.7 constant_dynamic-slice_fusion.ez
  25.9 0.1 collective-permute-done
  25.9 2.5 %collective-permute-done.1 = s32[8]{0:T(128)S(1)} collective-permute-done((s32[8]{0:T(128)S(1)}, s32[8]{0:T(128)S(1)}, u32[]{:S(2)}, u32[]{:S(2)}) %collective-permute-start.1) | collective-permute-done | bytes 64 | tf_op jit(solution)/shard_map/ppermute | solution.py:572
  28.4 0.0 all-to-all-done.tiles
  28.4 0.0 copy-done.1
  28.4 0.0 copy-done.2
  28.5 0.6 copy-done.8
  29.1 0.9 shard_map.131
  30.0 7.2 %collective-permute-start.3 = (f32[32,512]{1,0:T(8,128)S(1)}, f32[32,512]{1,0:T(8,128)S(1)}, u32[]{:S(2)}, u32[]{:S(2)}) collective-permute-start(f32[32,512]{1,0:T(8,128)S(1)} %get-tuple-element.23), channel_id=1, source_target_pairs={{0,16},{1,17},{2,18},{3,19},{4,20},{5,21},{6,22},{7,23},{8,24},{9,... | collective-permute-start | bytes 196616 | tf_op jit(solution)/shard_map/ppermute | solution.py:615
  37.2 0.1 shard_map.132
  37.3 0.7 collective-permute-done.3
  38.1 2.4 %collective-permute-start.4 = (f32[32,512]{1,0:T(8,128)S(1)}, f32[32,512]{1,0:T(8,128)S(1)}, u32[]{:S(2)}, u32[]{:S(2)}) collective-permute-start(f32[32,512]{1,0:T(8,128)S(1)} %pad_maximum_fusion.1), channel_id=1, source_target_pairs={{0,32},{1,33},{2,34},{3,35},{4,36},{5,37},{6,38},{7,39},{8,40},{9,... | collective-permute-start | bytes 196616 | tf_op jit(solution)/shard_map/ppermute | solution.py:615
  40.5 9.1 %collective-permute-done.4 = f32[32,512]{1,0:T(8,128)S(1)} collective-permute-done((f32[32,512]{1,0:T(8,128)S(1)}, f32[32,512]{1,0:T(8,128)S(1)}, u32[]{:S(2)}, u32[]{:S(2)}) %collective-permute-start.4) | collective-permute-done | bytes 65568 | tf_op jit(solution)/shard_map/ppermute | solution.py:615
  49.7 1.9 %collective-permute-start.5 = (f32[32,512]{1,0:T(8,128)S(1)}, f32[32,512]{1,0:T(8,128)S(1)}, u32[]{:S(2)}, u32[]{:S(2)}) collective-permute-start(f32[32,512]{1,0:T(8,128)S(1)} %pad_maximum_fusion.2), channel_id=1, source_target_pairs={{0,64},{1,65},{2,66},{3,67},{4,68},{5,69},{6,70},{7,71},{8,72},{9,... | collective-permute-start | bytes 196616 | tf_op jit(solution)/shard_map/ppermute | solution.py:615
  51.7 4.2 %collective-permute-done.5 = f32[32,512]{1,0:T(8,128)S(1)} collective-permute-done((f32[32,512]{1,0:T(8,128)S(1)}, f32[32,512]{1,0:T(8,128)S(1)}, u32[]{:S(2)}, u32[]{:S(2)}) %collective-permute-start.5) | collective-permute-done | bytes 65568 | tf_op jit(solution)/shard_map/ppermute | solution.py:615
  55.9 1.9 %collective-permute-start.6 = (f32[32,512]{1,0:T(8,128)S(1)}, f32[32,512]{1,0:T(8,128)S(1)}, u32[]{:S(2)}, u32[]{:S(2)}) collective-permute-start(f32[32,512]{1,0:T(8,128)S(1)} %pad_maximum_fusion.3), channel_id=1, source_target_pairs={{0,128},{1,129},{2,130},{3,131},{4,132},{5,133},{6,134},{7,135},{8... | collective-permute-start | bytes 196616 | tf_op jit(solution)/shard_map/ppermute | solution.py:615
  57.9 5.3 %collective-permute-done.6 = f32[32,512]{1,0:T(8,128)S(1)} collective-permute-done((f32[32,512]{1,0:T(8,128)S(1)}, f32[32,512]{1,0:T(8,128)S(1)}, u32[]{:S(2)}, u32[]{:S(2)}) %collective-permute-start.6) | collective-permute-done | bytes 65568 | tf_op jit(solution)/shard_map/ppermute | solution.py:615
  63.2 1.9 %collective-permute-start.7 = (f32[32,512]{1,0:T(8,128)S(1)}, f32[32,512]{1,0:T(8,128)S(1)}, u32[]{:S(2)}, u32[]{:S(2)}) collective-permute-start(f32[32,512]{1,0:T(8,128)S(1)} %pad_maximum_fusion.4), channel_id=1, source_target_pairs={{0,384},{1,385},{2,386},{3,387},{4,388},{5,389},{6,390},{7,391},{8... | collective-permute-start | bytes 196616 | tf_op jit(solution)/shard_map/ppermute | solution.py:615
  65.2 6.3 %collective-permute-done.7 = f32[32,512]{1,0:T(8,128)S(1)} collective-permute-done((f32[32,512]{1,0:T(8,128)S(1)}, f32[32,512]{1,0:T(8,128)S(1)}, u32[]{:S(2)}, u32[]{:S(2)}) %collective-permute-start.7) | collective-permute-done | bytes 65568 | tf_op jit(solution)/shard_map/ppermute | solution.py:615
  71.6 2.0 %shard_map.133 = f32[16,16,512]{2,1,0:T(8,128)} custom-call(f32[256,512]{1,0:T(8,128)S(1)} %get-tuple-element.22.field, f32[32,512]{1,0:T(8,128)S(1)} %pad_maximum_fusion.5.totals, f32[16,512]{1,0:T(8,128)S(1)} %fusion.10.right, f32[16,512]{1,0:T(8,128)S(1)} %fusion.1.left, f32[2,16,512]{2,1,0:T(8,128)S(1)} %get-tuple-element.26.ends, ...), custom_call_target="tpu_custom_call" | custom-call | tf_op jit(solution)/shard_map/pallas_call | solution.py:622
  73.6 6.7 %all-to-all-start.1 = ((f32[16,16,512]{2,1,0:T(8,128)}), f32[16,16,512]{2,1,0:T(8,128)S(1)}, u32[]{:S(2)}, u32[]{:S(2)}) async-start(f32[16,16,512]{2,1,0:T(8,128)} %shard_map.133), calls=%async_computation.1 | async-start | bytes 1048576 | tf_op jit(solution)/shard_map/all_to_all | solution.py:625
  80.4 3.4 %collective-permute-start.2 = (s32[3,8]{1,0:T(4,128)S(1)}, s32[3,8]{1,0:T(4,128)S(1)}, u32[]{:S(2)}, u32[]{:S(2)}) collective-permute-start(s32[3,8]{1,0:T(4,128)S(1)} %pad_add_fusion.1), channel_id=1, source_target_pairs={{0,1},{1,2},{2,3},{3,4},{4,5},{5,6},{6,7},{7,8},{8,9},{9,10},{10,1... | collective-permute-start | bytes 296 | tf_op jit(solution)/shard_map/ppermute | solution.py:572
  83.7 6.0 %collective-permute-done.2 = s32[3,8]{1,0:T(4,128)S(1)} collective-permute-done((s32[3,8]{1,0:T(4,128)S(1)}, s32[3,8]{1,0:T(4,128)S(1)}, u32[]{:S(2)}, u32[]{:S(2)}) %collective-permute-start.2) | collective-permute-done | bytes 128 | tf_op jit(solution)/shard_map/ppermute | solution.py:572
  89.7 0.1 reshape.23.places
  89.8 1.8 %all-to-all-done.1.tiles = f32[16,16,512]{2,1,0:T(8,128)S(1)} async-done(((f32[16,16,512]{2,1,0:T(8,128)}), f32[16,16,512]{2,1,0:T(8,128)S(1)}, u32[]{:S(2)}, u32[]{:S(2)}) %all-to-all-start.1) | async-done | bytes 524320 | tf_op jit(solution)/shard_map/all_to_all | solution.py:625
  91.6 0.0 copy-done
  91.6 0.0 copy-done.4
  91.6 2.2 %shard_map.134 = (f32[16,32,256]{2,1,0:T(8,128)}, f32[20,24,128]{2,1,0:T(8,128)S(1)}) custom-call(s32[36]{0:T(128)S(1)} %reshape.23.places, f32[16,16,512]{2,1,0:T(8,128)S(1)} %all-to-all-done.1.tiles, f32[16,32,256]{2,1,0:T(8,128)S(1)} %copy-done, bf16[2,256,256]{2,1,0:T(8,128)(2,1)S(1)} %copy-done.4), custom_call_target="tpu_custom_call" | custom-call | tf_op jit(solution)/shard_map/pallas_call | solution.py:628
  93.8 3.2 %collective-permute-start.8 = (f32[20,24,128]{2,1,0:T(8,128)S(1)}, f32[20,24,128]{2,1,0:T(8,128)S(1)}, u32[]{:S(2)}, u32[]{:S(2)}) collective-permute-start(f32[20,24,128]{2,1,0:T(8,128)S(1)} %get-tuple-element.29), channel_id=1, source_target_pairs={{1,0},{2,1},{3,2},{4,3},{5,4},{6,5},{7,6},{8,7},{9,8},{10,9},{11,1... | collective-permute-start | bytes 737288 | tf_op jit(solution)/shard_map/ppermute | solution.py:572
  97.0 0.1 slice_reduce_fusion
  97.1 1.0 copy-done.7
  98.2 1.3 shard_map.135
  99.4 2.5 %collective-permute-done.8.refs_1_ = f32[20,24,128]{2,1,0:T(8,128)S(1)} collective-permute-done((f32[20,24,128]{2,1,0:T(8,128)S(1)}, f32[20,24,128]{2,1,0:T(8,128)S(1)}, u32[]{:S(2)}, u32[]{:S(2)}) %collective-permute-start.8) | collective-permute-done | bytes 245792 | tf_op jit(solution)/shard_map/ppermute | solution.py:572
  102.0 1.9 %collective-permute-start.10 = (f32[4,24,128]{2,1,0:T(8,128)S(1)}, f32[4,24,128]{2,1,0:T(8,128)S(1)}, u32[]{:S(2)}, u32[]{:S(2)}) collective-permute-start(f32[4,24,128]{2,1,0:T(8,128)S(1)} %slice_add_fusion.1), channel_id=1, source_target_pairs={{32,0},{33,1},{34,2},{35,3},{36,4},{37,5},{38,6},{39,7},{40,8},{41... | collective-permute-start | bytes 147464 | tf_op jit(solution)/shard_map/ppermute | solution.py:572
  103.9 0.0 copy-start.10
  103.9 0.0 copy-start.11
  104.0 1.9 %collective-permute-start.9 = (f32[8,24,128]{2,1,0:T(8,128)S(1)}, f32[8,24,128]{2,1,0:T(8,128)S(1)}, u32[]{:S(2)}, u32[]{:S(2)}) collective-permute-start(f32[8,24,128]{2,1,0:T(8,128)S(1)} %slice_add_fusion), channel_id=1, source_target_pairs={{16,0},{17,1},{18,2},{19,3},{20,4},{21,5},{22,6},{23,7},{24,8},{25... | collective-permute-start | bytes 294920 | tf_op jit(solution)/shard_map/ppermute | solution.py:572
  105.9 0.0 copy-done.10
  105.9 0.0 copy-done.11
  105.9 0.1 pad_add_fusion.3.meta
  106.0 0.0 copy-done.5
  106.0 2.0 %shard_map.136.refs_4_ = f32[24,9,8,128]{3,2,1,0:T(8,128)S(1)} custom-call(f32[2,192,576]{2,1,0:T(8,128)S(1)} %bitcast.41), custom_call_target="tpu_custom_call" | custom-call | tf_op jit(solution)/shard_map/pallas_call | solution.py:591
  108.1 3.8 %collective-permute-done.10.refs_3_ = f32[4,24,128]{2,1,0:T(8,128)S(1)} collective-permute-done((f32[4,24,128]{2,1,0:T(8,128)S(1)}, f32[4,24,128]{2,1,0:T(8,128)S(1)}, u32[]{:S(2)}, u32[]{:S(2)}) %collective-permute-start.10) | collective-permute-done | bytes 49184 | tf_op jit(solution)/shard_map/ppermute | solution.py:572
  111.9 0.0 collective-permute-done.9.refs_2_
  111.9 15.5 %shard_map.137 = (f32[24,9,8,128]{3,2,1,0:T(8,128)S(1)}, f32[8,128]{1,0:T(8,128)S(1)}, f32[8,24,128]{2,1,0:T(8,128)S(1)}, f32[8,24,128]{2,1,0:T(8,128)S(1)}, f32[4,24,128]{2,1,0:T(8,128)S(1)}) custom-call(s32[8]{0:T(128)S(1)} %pad_add_fusion.3.meta, f32[8,24,128]{2,1,0:T(8,128)S(1)} %get-tuple-element.28.refs_0_, ...), custom_call_target="tpu_custom_call" | custom-call | tf_op jit(solution)/shard_map/pallas_call | solution.py:637
  127.4 4.7 %collective-permute-start.11 = (f32[8,24,128]{2,1,0:T(8,128)S(1)}, f32[8,24,128]{2,1,0:T(8,128)S(1)}, u32[]{:S(2)}, u32[]{:S(2)}) collective-permute-start(f32[8,24,128]{2,1,0:T(8,128)S(1)} %get-tuple-element.35), channel_id=1, source_target_pairs={{0,16},{1,17},{2,18},{3,19},{4,20},{5,21},{6,22},{7,23},{8,24},{9,... | collective-permute-start | bytes 294920 | tf_op jit(solution)/shard_map/ppermute | solution.py:572
  132.0 2.6 %collective-permute-start.12 = (f32[4,24,128]{2,1,0:T(8,128)S(1)}, f32[4,24,128]{2,1,0:T(8,128)S(1)}, u32[]{:S(2)}, u32[]{:S(2)}) collective-permute-start(f32[4,24,128]{2,1,0:T(8,128)S(1)} %get-tuple-element.36), channel_id=1, source_target_pairs={{0,32},{1,33},{2,34},{3,35},{4,36},{5,37},{6,38},{7,39},{8,40},{9,... | collective-permute-start | bytes 147464 | tf_op jit(solution)/shard_map/ppermute | solution.py:572
  134.7 9.3 %collective-permute-done.12.third = f32[4,24,128]{2,1,0:T(8,128)S(1)} collective-permute-done((f32[4,24,128]{2,1,0:T(8,128)S(1)}, f32[4,24,128]{2,1,0:T(8,128)S(1)}, u32[]{:S(2)}, u32[]{:S(2)}) %collective-permute-start.12) | collective-permute-done | bytes 49184 | tf_op jit(solution)/shard_map/ppermute | solution.py:572
  144.0 0.0 collective-permute-done.11.second
  144.1 1.9 %collective-permute-start.13 = (f32[20,24,128]{2,1,0:T(8,128)S(1)}, f32[20,24,128]{2,1,0:T(8,128)S(1)}, u32[]{:S(2)}, u32[]{:S(2)}) collective-permute-start(f32[20,24,128]{2,1,0:T(8,128)S(1)} %pad_maximum_fusion), channel_id=1, source_target_pairs={{0,1},{1,2},{2,3},{3,4},{4,5},{5,6},{6,7},{7,8},{8,9},{9,10},{10,1... | collective-permute-start | bytes 737288 | tf_op jit(solution)/shard_map/ppermute | solution.py:572
  146.0 2.9 %shard_map.138 = f32[2,192,576]{2,1,0:T(8,128)} custom-call(f32[24,9,8,128]{3,2,1,0:T(8,128)S(1)} %get-tuple-element.32.planes, f32[8,128]{1,0:T(8,128)S(1)} %get-tuple-element.33.scale), custom_call_target="tpu_custom_call" | custom-call | tf_op jit(solution)/shard_map/pallas_call | solution.py:653
  148.9 1.5 shard_map.139.owned
  150.4 6.3 %collective-permute-done.13.beside = f32[20,24,128]{2,1,0:T(8,128)S(1)} collective-permute-done((f32[20,24,128]{2,1,0:T(8,128)S(1)}, f32[20,24,128]{2,1,0:T(8,128)S(1)}, u32[]{:S(2)}, u32[]{:S(2)}) %collective-permute-start.13) | collective-permute-done | bytes 245792 | tf_op jit(solution)/shard_map/ppermute | solution.py:572
  156.8 2.3 %shard_map.140 = f32[16,32,256]{2,1,0:T(8,128)} custom-call(s32[36]{0:T(128)S(1)} %reshape.23.places, f32[16,32,256]{2,1,0:T(8,128)S(1)} %shard_map.139.owned, f32[20,24,128]{2,1,0:T(8,128)S(1)} %collective-permute-done.13.beside), custom_call_target="tpu_custom_call" | custom-call | tf_op jit(solution)/shard_map/pallas_call | solution.py:660
  (34 shorter events, 0.3 us)
Async XLA Ops:
  0.6 1.0 copy-start.3
  1.6 1.0 copy-start.6
  3.8 24.6 %copy-start.1 = (bf16[512,512]{1,0:T(8,128)(2,1)S(1)}, bf16[512,512]{1,0:T(8,128)(2,1)}, u32[]{:S(2)}) copy-start(bf16[512,512]{1,0:T(8,128)(2,1)} %constant.75.clone.table_low) | copy-start | bytes 1572868
  3.8 24.6 %copy-start.2 = (bf16[512,512]{1,0:T(8,128)(2,1)S(1)}, bf16[512,512]{1,0:T(8,128)(2,1)}, u32[]{:S(2)}) copy-start(bf16[512,512]{1,0:T(8,128)(2,1)} %constant.74.clone.table_high) | copy-start | bytes 1572868
  3.8 24.6 %all-to-all-start = ((f32[16,16,512]{2,1,0:T(8,128)}), f32[16,16,512]{2,1,0:T(8,128)S(1)}, u32[]{:S(2)}, u32[]{:S(2)}) async-start(f32[16,16,512]{2,1,0:T(8,128)} %shard_map.130), calls=%async_computation | async-start | bytes 1048576 | tf_op jit(solution)/shard_map/all_to_all | solution.py:604
  14.2 0.7 copy-start.9
  15.0 10.9 %collective-permute-start = (s32[8]{0:T(128)S(1)}, s32[8]{0:T(128)S(1)}, u32[]{:S(2)}, u32[]{:S(2)}) collective-permute-start(s32[8]{0:T(128)S(1)} %get-tuple-element.58), channel_id=1, source_target_pairs={{0,16},{1,17},{2,18},{3,19},{4,20},{5,21},{6,22},{7,23},{8,24},{9,... | collective-permute-start | bytes 104 | tf_op jit(solution)/shard_map/ppermute | solution.py:572
  16.9 11.5 %collective-permute-start.1 = (s32[8]{0:T(128)S(1)}, s32[8]{0:T(128)S(1)}, u32[]{:S(2)}, u32[]{:S(2)}) collective-permute-start(s32[8]{0:T(128)S(1)} %get-tuple-element.58), channel_id=1, source_target_pairs={{0,32},{1,33},{2,34},{3,35},{4,36},{5,37},{6,38},{7,39},{8,40},{9,... | collective-permute-start | bytes 104 | tf_op jit(solution)/shard_map/ppermute | solution.py:572
  28.4 0.7 copy-start.8
  30.0 8.1 %collective-permute-start.3 = (f32[32,512]{1,0:T(8,128)S(1)}, f32[32,512]{1,0:T(8,128)S(1)}, u32[]{:S(2)}, u32[]{:S(2)}) collective-permute-start(f32[32,512]{1,0:T(8,128)S(1)} %get-tuple-element.23), channel_id=1, source_target_pairs={{0,16},{1,17},{2,18},{3,19},{4,20},{5,21},{6,22},{7,23},{8,24},{9,... | collective-permute-start | bytes 196616 | tf_op jit(solution)/shard_map/ppermute | solution.py:615
  38.1 11.5 %collective-permute-start.4 = (f32[32,512]{1,0:T(8,128)S(1)}, f32[32,512]{1,0:T(8,128)S(1)}, u32[]{:S(2)}, u32[]{:S(2)}) collective-permute-start(f32[32,512]{1,0:T(8,128)S(1)} %pad_maximum_fusion.1), channel_id=1, source_target_pairs={{0,32},{1,33},{2,34},{3,35},{4,36},{5,37},{6,38},{7,39},{8,40},{9,... | collective-permute-start | bytes 196616 | tf_op jit(solution)/shard_map/ppermute | solution.py:615
  49.7 6.2 %collective-permute-start.5 = (f32[32,512]{1,0:T(8,128)S(1)}, f32[32,512]{1,0:T(8,128)S(1)}, u32[]{:S(2)}, u32[]{:S(2)}) collective-permute-start(f32[32,512]{1,0:T(8,128)S(1)} %pad_maximum_fusion.2), channel_id=1, source_target_pairs={{0,64},{1,65},{2,66},{3,67},{4,68},{5,69},{6,70},{7,71},{8,72},{9,... | collective-permute-start | bytes 196616 | tf_op jit(solution)/shard_map/ppermute | solution.py:615
  55.9 7.3 %collective-permute-start.6 = (f32[32,512]{1,0:T(8,128)S(1)}, f32[32,512]{1,0:T(8,128)S(1)}, u32[]{:S(2)}, u32[]{:S(2)}) collective-permute-start(f32[32,512]{1,0:T(8,128)S(1)} %pad_maximum_fusion.3), channel_id=1, source_target_pairs={{0,128},{1,129},{2,130},{3,131},{4,132},{5,133},{6,134},{7,135},{8... | collective-permute-start | bytes 196616 | tf_op jit(solution)/shard_map/ppermute | solution.py:615
  63.2 8.3 %collective-permute-start.7 = (f32[32,512]{1,0:T(8,128)S(1)}, f32[32,512]{1,0:T(8,128)S(1)}, u32[]{:S(2)}, u32[]{:S(2)}) collective-permute-start(f32[32,512]{1,0:T(8,128)S(1)} %pad_maximum_fusion.4), channel_id=1, source_target_pairs={{0,384},{1,385},{2,386},{3,387},{4,388},{5,389},{6,390},{7,391},{8... | collective-permute-start | bytes 196616 | tf_op jit(solution)/shard_map/ppermute | solution.py:615
  73.6 18.0 %copy-start = (f32[16,32,256]{2,1,0:T(8,128)S(1)}, f32[16,32,256]{2,1,0:T(8,128)}, u32[]{:S(2)}) copy-start(f32[16,32,256]{2,1,0:T(8,128)} %external.3) | copy-start | bytes 1572868
  73.6 18.0 %copy-start.4 = (bf16[2,256,256]{2,1,0:T(8,128)(2,1)S(1)}, bf16[2,256,256]{2,1,0:T(8,128)(2,1)}, u32[]{:S(2)}) copy-start(bf16[2,256,256]{2,1,0:T(8,128)(2,1)} %constant.76.clone.table) | copy-start | bytes 786436
  73.6 18.0 %all-to-all-start.1 = ((f32[16,16,512]{2,1,0:T(8,128)}), f32[16,16,512]{2,1,0:T(8,128)S(1)}, u32[]{:S(2)}, u32[]{:S(2)}) async-start(f32[16,16,512]{2,1,0:T(8,128)} %shard_map.133), calls=%async_computation.1 | async-start | bytes 1048576 | tf_op jit(solution)/shard_map/all_to_all | solution.py:625
  80.4 9.4 %collective-permute-start.2 = (s32[3,8]{1,0:T(4,128)S(1)}, s32[3,8]{1,0:T(4,128)S(1)}, u32[]{:S(2)}, u32[]{:S(2)}) collective-permute-start(s32[3,8]{1,0:T(4,128)S(1)} %pad_add_fusion.1), channel_id=1, source_target_pairs={{0,1},{1,2},{2,3},{3,4},{4,5},{5,6},{6,7},{7,8},{8,9},{9,10},{10,1... | collective-permute-start | bytes 296 | tf_op jit(solution)/shard_map/ppermute | solution.py:572
  93.8 12.2 %copy-start.5 = (f32[2,8,24,576]{3,2,1,0:T(8,128)S(1)}, f32[2,8,24,576]{3,2,1,0:T(8,128)}, u32[]{:S(2)}) copy-start(f32[2,8,24,576]{3,2,1,0:T(8,128)} %param.13) | copy-start | bytes 2654212
  93.8 8.2 %collective-permute-start.8 = (f32[20,24,128]{2,1,0:T(8,128)S(1)}, f32[20,24,128]{2,1,0:T(8,128)S(1)}, u32[]{:S(2)}, u32[]{:S(2)}) collective-permute-start(f32[20,24,128]{2,1,0:T(8,128)S(1)} %get-tuple-element.29), channel_id=1, source_target_pairs={{1,0},{2,1},{3,2},{4,3},{5,4},{6,5},{7,6},{8,7},{9,8},{10,9},{11,1... | collective-permute-start | bytes 737288 | tf_op jit(solution)/shard_map/ppermute | solution.py:572
  97.1 1.0 copy-start.7
  102.0 9.9 %collective-permute-start.10 = (f32[4,24,128]{2,1,0:T(8,128)S(1)}, f32[4,24,128]{2,1,0:T(8,128)S(1)}, u32[]{:S(2)}, u32[]{:S(2)}) collective-permute-start(f32[4,24,128]{2,1,0:T(8,128)S(1)} %slice_add_fusion.1), channel_id=1, source_target_pairs={{32,0},{33,1},{34,2},{35,3},{36,4},{37,5},{38,6},{39,7},{40,8},{41... | collective-permute-start | bytes 147464 | tf_op jit(solution)/shard_map/ppermute | solution.py:572
  103.9 2.0 %copy-start.10 = (s32[2]{0:T(128)S(1)}, s32[2]{0:T(128)}, u32[]{:S(2)}) copy-start(s32[2]{0:T(128)} %param.15) | copy-start | bytes 28
  103.9 2.0 %copy-start.11 = (s32[2]{0:T(128)S(1)}, s32[2]{0:T(128)}, u32[]{:S(2)}) copy-start(s32[2]{0:T(128)} %param.16) | copy-start | bytes 28
  104.0 7.9 %collective-permute-start.9 = (f32[8,24,128]{2,1,0:T(8,128)S(1)}, f32[8,24,128]{2,1,0:T(8,128)S(1)}, u32[]{:S(2)}, u32[]{:S(2)}) collective-permute-start(f32[8,24,128]{2,1,0:T(8,128)S(1)} %slice_add_fusion), channel_id=1, source_target_pairs={{16,0},{17,1},{18,2},{19,3},{20,4},{21,5},{22,6},{23,7},{24,8},{25... | collective-permute-start | bytes 294920 | tf_op jit(solution)/shard_map/ppermute | solution.py:572
  127.4 16.7 %collective-permute-start.11 = (f32[8,24,128]{2,1,0:T(8,128)S(1)}, f32[8,24,128]{2,1,0:T(8,128)S(1)}, u32[]{:S(2)}, u32[]{:S(2)}) collective-permute-start(f32[8,24,128]{2,1,0:T(8,128)S(1)} %get-tuple-element.35), channel_id=1, source_target_pairs={{0,16},{1,17},{2,18},{3,19},{4,20},{5,21},{6,22},{7,23},{8,24},{9,... | collective-permute-start | bytes 294920 | tf_op jit(solution)/shard_map/ppermute | solution.py:572
  132.0 12.0 %collective-permute-start.12 = (f32[4,24,128]{2,1,0:T(8,128)S(1)}, f32[4,24,128]{2,1,0:T(8,128)S(1)}, u32[]{:S(2)}, u32[]{:S(2)}) collective-permute-start(f32[4,24,128]{2,1,0:T(8,128)S(1)} %get-tuple-element.36), channel_id=1, source_target_pairs={{0,32},{1,33},{2,34},{3,35},{4,36},{5,37},{6,38},{7,39},{8,40},{9,... | collective-permute-start | bytes 147464 | tf_op jit(solution)/shard_map/ppermute | solution.py:572
  144.1 12.7 %collective-permute-start.13 = (f32[20,24,128]{2,1,0:T(8,128)S(1)}, f32[20,24,128]{2,1,0:T(8,128)S(1)}, u32[]{:S(2)}, u32[]{:S(2)}) collective-permute-start(f32[20,24,128]{2,1,0:T(8,128)S(1)} %pad_maximum_fusion), channel_id=1, source_target_pairs={{0,1},{1,2},{2,3},{3,4},{4,5},{5,6},{6,7},{7,8},{8,9},{9,10},{10,1... | collective-permute-start | bytes 737288 | tf_op jit(solution)/shard_map/ppermute | solution.py:572
